TPU v7x, 32 devices: a whole 2x2x4 slice. The times are simulated.
32 devices in a mesh: dx: 4 (over z), dy: 4 (over y, x), dz: 2 (over core).
Axes of the slice: x: 2, y: 2, z: 4, core: 2. Of those that a mesh axis runs over, the one named last changes fastest.
Arguments:
- node_state: bfloat16 [8, 8, 4, 32, 128], P('dx', 'dy', 'dz'), may hold values from -6 to 6
- mesh_base: int32 [3, 8, 8, 4, 32], P(None, 'dx', 'dy', 'dz'), may hold values from 0 to 127, as said below
- mesh_frac: float32 [3, 8, 8, 4, 32], P(None, 'dx', 'dy', 'dz'), may hold values from 0 to 1
- charge: float32 [8, 8, 4, 32], P('dx', 'dy', 'dz'), may hold values from -0.5 to 0.5
- nbr_code: int32 [8, 8, 4, 32, 128], P('dx', 'dy', 'dz'), may hold values from 0 to 863, as said below
- nbr_count: int32 [8, 8, 4, 32], P('dx', 'dy', 'dz'), may hold values from 32 to 128, as said below
- radial_weight: float32 [8, 128], replicated, may hold values from -2 to 2
- mix_weight: bfloat16 [3, 128, 128], replicated, may hold values from -0.5 to 0.5
- force_weight: float32 [128], replicated, may hold values from -0.5 to 0.5
Outputs:
- node_next: bfloat16 [8, 8, 4, 32, 128], P('dx', 'dy', 'dz')
- forces: float32 [3, 8, 8, 4, 32], P(None, 'dx', 'dy', 'dz')
Inputs may be any that keep to these rules, and one draw needn't show every extreme that they name: `mesh_base`: entry d of an atom in octant (X, Y, Z) lies in the atom's octant: from 32 / 2 times its octant index along d up to 16 more, exclusive. In every octant the first atom sits at the lower end and the second at the upper end in every dimension. `nbr_code`: The first atom of every octant has the largest code in its first slot and 0 in its second. `nbr_count`: slots from the count on are padding. The first atom of every octant has 128 live slots, the second 128 // 4.
All inputs are finite; a program needn't handle non-finite values.
Results may differ from a plain program's by a relative error of at most 0.00095.
The roundings to bfloat16 on the way count: a program that leaves them out, or rounds other values in their place, can miss the bound.
Values may be sent and summed in bfloat16 or wider, within the bound.
No kernel may reach another device: no remote copies, remote signals or barrier semaphores. Data moves between devices by JAX's collectives and lax.ppermute only.
A program may use at most 64 MiB of HBM per device.

v0:
```python
import math

import jax
import jax.numpy as jnp
from jax import lax
from jax.sharding import PartitionSpec as P

NB = 8
NBR = 128
MB = 32
KZW = 8


cell_size = 1.13
ewald_beta = 0.625
coulomb = 332.0637
sigma_low = 8.0
sigma_rate = 1.5
highest = lax.Precision.HIGHEST


def with_halo(cells, sides, width):
    for axis, dim in sides:
        count = lax.axis_size(axis)
        head = lax.slice_in_dim(cells, 0, width, axis=dim)
        tail = lax.slice_in_dim(cells, cells.shape[dim] - width, cells.shape[dim], axis=dim)
        cells = jnp.concatenate(
            [
                lax.ppermute(tail, axis, [(i, (i + 1) % count) for i in range(count)]),
                cells,
                lax.ppermute(head, axis, [((i + 1) % count, i) for i in range(count)]),
            ],
            axis=dim,
        )
    return cells


def spline_terms(fraction):
    remainder = 1.0 - fraction
    frac_square = fraction * fraction
    frac_cube = frac_square * fraction
    weights = jnp.stack(
        [
            remainder * remainder * remainder / 6.0,
            (3.0 * frac_cube - 6.0 * frac_square + 4.0) / 6.0,
            (-3.0 * frac_cube + 3.0 * frac_square + 3.0 * fraction + 1.0) / 6.0,
            frac_cube / 6.0,
        ]
    )
    slopes = jnp.stack(
        [
            -0.5 * remainder * remainder,
            1.5 * frac_square - 2.0 * fraction,
            -1.5 * frac_square + fraction + 0.5,
            0.5 * frac_square,
        ]
    )
    return (weights, slopes)


def harmonics(direction):
    unit_x, unit_y, unit_z = (direction[0], direction[1], direction[2])
    root_three = math.sqrt(3.0)
    root_fifteen = math.sqrt(15.0)
    root_five = math.sqrt(5.0)
    return jnp.stack(
        [
            jnp.ones_like(unit_x),
            root_three * unit_x,
            root_three * unit_y,
            root_three * unit_z,
            root_fifteen * unit_x * unit_y,
            root_fifteen * unit_y * unit_z,
            0.5 * root_five * (3.0 * unit_z * unit_z - 1.0),
            root_fifteen * unit_x * unit_z,
            0.5 * root_fifteen * (unit_x * unit_x - unit_y * unit_y),
        ]
    )


def edge_terms(displace, active):
    square = jnp.sum(displace * displace, axis=0)
    direction = displace / jnp.sqrt(square + 1.0)
    angular = harmonics(direction)
    distance = cell_size * jnp.sqrt(square)
    widths = sigma_low * jnp.power(sigma_rate, jnp.arange(NB).astype(jnp.float32))
    radial = jnp.exp(-jnp.square(distance[None] / widths[:, None, None]))
    products = radial[:, None] * angular[None] * active.astype(jnp.float32)[None, None]
    atom_rows = displace.shape[1]
    return jnp.transpose(products, (2, 0, 1, 3)).reshape(atom_rows, NB * 9, -1).astype(jnp.bfloat16)


def node_update(edge_values, neighbour_state, own_state, radial_weight, mix_weight, force_weight):
    summed = jnp.einsum(
        "bkn,bnc->bkc", edge_values, neighbour_state, preferred_element_type=jnp.float32
    )
    atom_rows = summed.shape[0]
    summed = summed.reshape(atom_rows, NB, 9, -1)
    message = (jnp.sum(summed * radial_weight[None, :, None, :], axis=1) / math.sqrt(NBR)).astype(
        jnp.bfloat16
    )
    scalar = jnp.dot(message[:, 0], mix_weight[0], preferred_element_type=jnp.float32)
    vector = jnp.einsum(
        "bmc,cd->bmd", message[:, 1:4], mix_weight[1], preferred_element_type=jnp.float32
    )
    tensor = jnp.einsum(
        "bmc,cd->bmd", message[:, 4:9], mix_weight[2], preferred_element_type=jnp.float32
    )
    invariant = scalar + jnp.sum(tensor * tensor, axis=1)
    gating = jax.nn.sigmoid(invariant)
    updated = (own_state.astype(jnp.float32) + jax.nn.silu(invariant)).astype(jnp.bfloat16)
    short_push = jnp.sum(vector * (gating * force_weight)[:, None, :], axis=2)
    return (updated, jnp.transpose(short_push))


def phases(wavenumber, cell_index, extent):
    return 2.0 * math.pi / extent * jnp.mod(wavenumber * cell_index, extent).astype(jnp.float32)


def wave_sums(coeff, start_cells, wavenumber, extent, orient):
    wave_re = jnp.zeros((start_cells.shape[0], wavenumber.shape[0]), jnp.float32)
    wave_im = jnp.zeros((start_cells.shape[0], wavenumber.shape[0]), jnp.float32)
    for stencil in range(4):
        angles = phases(wavenumber[None, :], (start_cells + stencil)[:, None], extent)
        wave_re = wave_re + coeff[stencil][:, None] * jnp.cos(angles)
        wave_im = wave_im + coeff[stencil][:, None] * jnp.sin(angles)
    return (wave_re, orient * wave_im)


def cell_table(coeff, local_cells, cell_index):
    table = jnp.zeros((local_cells.shape[0], cell_index.shape[0]), jnp.float32)
    for stencil in range(4):
        match = (cell_index[None, :] == (local_cells + stencil)[:, None]).astype(jnp.float32)
        table = table + coeff[stencil][:, None] * match
    return table


def influence(modes_x, modes_y, modes_z, length_x, length_y, length_z):

    def folded(wavenumber, extent):
        return jnp.where(2 * wavenumber >= extent, wavenumber - extent, wavenumber).astype(
            jnp.float32
        ) / (cell_size * extent)

    wave_square = (
        jnp.square(folded(modes_x, length_x))
        + jnp.square(folded(modes_y, length_y))
        + jnp.square(folded(modes_z, length_z))
    )
    volume = cell_size**3 * length_x * length_y * length_z
    return (
        coulomb
        / (math.pi * volume)
        * jnp.exp(-math.pi**2 * wave_square / ewald_beta**2)
        / wave_square
    )


def projected(value_re, value_im, wave_y_re, wave_y_im, wave_z_re, wave_z_im):
    inner_re = jnp.sum(value_re * wave_y_re[:, :, None] - value_im * wave_y_im[:, :, None], axis=1)
    inner_im = jnp.sum(value_re * wave_y_im[:, :, None] + value_im * wave_y_re[:, :, None], axis=1)
    return 2.0 * jnp.sum(inner_re * wave_z_re - inner_im * wave_z_im, axis=1)


def shards(
    node_state,
    mesh_base,
    mesh_frac,
    charge,
    nbr_code,
    nbr_count,
    radial_weight,
    mix_weight,
    force_weight,
):
    count_x = lax.axis_size("dx")
    count_y = lax.axis_size("dy")
    count_z = lax.axis_size("dz")
    index_x = lax.axis_index("dx")
    index_y = lax.axis_index("dy")
    index_z = lax.axis_index("dz")
    octants = node_state.shape[3]
    channels = node_state.shape[4]
    atom_total = 8 * octants
    half_block = MB // 2
    block_cells = MB + 3
    length_x = MB * count_x
    length_y = MB * count_y
    length_z = MB * count_z
    places = mesh_base.astype(jnp.float32) + mesh_frac
    halo_state = with_halo(node_state, (("dx", 0), ("dy", 1), ("dz", 2)), 1)
    halo_places = with_halo(places, (("dx", 1), ("dy", 2), ("dz", 3)), 1)
    flat_state = halo_state.reshape(64 * octants, channels)
    flat_places = halo_places.reshape(3, 64 * octants)
    piece_rows = octants // 2
    slot_index = jnp.arange(NBR, dtype=jnp.int32)

    def one_block(inputs):
        block_id, code_rows, count_rows, own_places, state_rows = inputs
        octant = block_id // 2
        corner_x = octant // 4
        corner_y = octant // 2 % 2
        corner_z = octant % 2
        side_code = code_rows // octants
        slot_code = code_rows % octants
        step_x = side_code // 9 - 1
        step_y = side_code // 3 % 3 - 1
        step_z = side_code % 3 - 1
        neighbour = (
            ((corner_x + 1 + step_x) * 4 + corner_y + 1 + step_y) * 4 + corner_z + 1 + step_z
        ) * octants + slot_code
        reach_x = 2 * index_x + corner_x + step_x
        reach_y = 2 * index_y + corner_y + step_y
        reach_z = 2 * index_z + corner_z + step_z
        wrap_shift = jnp.stack(
            [
                (reach_x - jnp.mod(reach_x, 2 * count_x)) * half_block,
                (reach_y - jnp.mod(reach_y, 2 * count_y)) * half_block,
                (reach_z - jnp.mod(reach_z, 2 * count_z)) * half_block,
            ]
        ).astype(jnp.float32)
        displace = flat_places[:, neighbour] + wrap_shift - own_places[:, :, None]
        active = slot_index[None, :] < count_rows[:, None]
        edge_values = edge_terms(displace, active)
        return node_update(
            edge_values, flat_state[neighbour], state_rows, radial_weight, mix_weight, force_weight
        )

    updated, short_push = lax.map(
        one_block,
        (
            jnp.arange(16, dtype=jnp.int32),
            nbr_code.reshape(16, piece_rows, NBR),
            nbr_count.reshape(16, piece_rows),
            jnp.transpose(places.reshape(3, 16, piece_rows), (1, 0, 2)),
            node_state.reshape(16, piece_rows, channels),
        ),
    )
    node_next = updated.reshape(node_state.shape)
    short_force = jnp.transpose(short_push, (1, 0, 2)).reshape(3, atom_total)
    base_rows = mesh_base.reshape(3, atom_total)
    frac_rows = mesh_frac.reshape(3, atom_total)
    charge_rows = charge.reshape(atom_total)
    anchor_x = index_x * MB
    cell_index = jnp.arange(block_cells, dtype=jnp.int32)
    planes = 1 + jnp.arange(KZW, dtype=jnp.int32)
    rows_dev = MB * KZW // count_z
    row_start = (index_y * count_z + index_z) * rows_dev
    own_modes = row_start // KZW + jnp.arange(rows_dev // KZW, dtype=jnp.int32)
    modes_x = jnp.arange(length_x, dtype=jnp.int32)
    packed = jnp.concatenate([charge_rows[None], base_rows.astype(jnp.float32), frac_rows], axis=0)[
        None
    ]
    gathered = lax.all_gather(packed, ("dy", "dz"), axis=0, tiled=True)
    group_count = gathered.shape[0]
    group_size = math.gcd(group_count, 4)

    def bundle_modes(bundle):
        flat_rows = jnp.transpose(bundle, (1, 0, 2)).reshape(7, -1)
        charges_now = flat_rows[0]
        base_now = flat_rows[1:4].astype(jnp.int32)
        weights_now, slopes_now = spline_terms(flat_rows[4:7])
        table_now = cell_table(weights_now[:, 0], base_now[0] - anchor_x, cell_index)
        wave_y_re, wave_y_im = wave_sums(weights_now[:, 1], base_now[1], own_modes, length_y, -1.0)
        wave_z_re, wave_z_im = wave_sums(weights_now[:, 2], base_now[2], planes, length_z, -1.0)
        mixed_re = (
            wave_y_re[:, :, None] * wave_z_re[:, None, :]
            - wave_y_im[:, :, None] * wave_z_im[:, None, :]
        ).reshape(-1, rows_dev)
        mixed_im = (
            wave_y_re[:, :, None] * wave_z_im[:, None, :]
            + wave_y_im[:, :, None] * wave_z_re[:, None, :]
        ).reshape(-1, rows_dev)
        left_side = jnp.transpose(table_now * charges_now[:, None])
        return jnp.stack(
            [
                jnp.dot(left_side, mixed_re, precision=highest),
                jnp.dot(left_side, mixed_im, precision=highest),
            ],
            axis=1,
        )

    modes_sum = jnp.sum(
        lax.map(
            bundle_modes, gathered.reshape(group_count // group_size, group_size, 7, atom_total)
        ),
        axis=0,
    )
    slab_rows = jnp.transpose(modes_sum, (2, 1, 0))
    received = lax.all_gather(slab_rows[None], "dx", axis=0, tiled=True)
    shard_count = received.shape[0]
    cells_now = (jnp.arange(shard_count, dtype=jnp.int32) * MB)[:, None] + cell_index[None, :]
    angle_x = phases(cells_now.reshape(-1)[:, None], modes_x[None, :], length_x)
    cos_x = jnp.cos(angle_x)
    sin_x = jnp.sin(angle_x)
    lined_up = jnp.transpose(received, (1, 2, 0, 3)).reshape(received.shape[1], 2, -1)
    spec_re = jnp.dot(lined_up[:, 0], cos_x, precision=highest) + jnp.dot(
        lined_up[:, 1], sin_x, precision=highest
    )
    spec_im = jnp.dot(lined_up[:, 1], cos_x, precision=highest) - jnp.dot(
        lined_up[:, 0], sin_x, precision=highest
    )
    spectrum = jnp.stack([spec_re, spec_im], axis=1)
    global_rows = row_start + jnp.arange(rows_dev, dtype=jnp.int32)
    green_table = influence(
        modes_x[None, :],
        (global_rows // KZW)[:, None],
        (global_rows % KZW + 1)[:, None],
        length_x,
        length_y,
        length_z,
    )
    scaled = spectrum * green_table[:, None, :]
    angle_back = phases(modes_x[:, None], (anchor_x + cell_index)[None, :], length_x)
    cos_back = jnp.cos(angle_back)
    sin_back = jnp.sin(angle_back)
    back_re = jnp.dot(scaled[:, 0], cos_back, precision=highest) - jnp.dot(
        scaled[:, 1], sin_back, precision=highest
    )
    back_im = jnp.dot(scaled[:, 0], sin_back, precision=highest) + jnp.dot(
        scaled[:, 1], cos_back, precision=highest
    )
    back_re_cols = jnp.transpose(back_re)
    back_im_cols = jnp.transpose(back_im)
    wave_count = rows_dev // KZW
    bundle_size = math.gcd(lax.axis_size(("dy", "dz")) * 1, 4)

    def bundle_push(bundle):
        flat_rows = jnp.transpose(bundle, (1, 0, 2)).reshape(7, -1)
        charges_now = flat_rows[0]
        base_now = flat_rows[1:4].astype(jnp.int32)
        weights_now, slopes_now = spline_terms(flat_rows[4:7])
        table_now = cell_table(weights_now[:, 0], base_now[0] - anchor_x, cell_index)
        tilt_now = cell_table(slopes_now[:, 0], base_now[0] - anchor_x, cell_index)
        value_re = jnp.dot(table_now, back_re_cols, precision=highest).reshape(-1, wave_count, KZW)
        value_im = jnp.dot(table_now, back_im_cols, precision=highest).reshape(-1, wave_count, KZW)
        tilt_re = jnp.dot(tilt_now, back_re_cols, precision=highest).reshape(-1, wave_count, KZW)
        tilt_im = jnp.dot(tilt_now, back_im_cols, precision=highest).reshape(-1, wave_count, KZW)
        wave_y = wave_sums(weights_now[:, 1], base_now[1], own_modes, length_y, 1.0)
        slope_y = wave_sums(slopes_now[:, 1], base_now[1], own_modes, length_y, 1.0)
        wave_z = wave_sums(weights_now[:, 2], base_now[2], planes, length_z, 1.0)
        slope_z = wave_sums(slopes_now[:, 2], base_now[2], planes, length_z, 1.0)
        grad_x = projected(tilt_re, tilt_im, wave_y[0], wave_y[1], wave_z[0], wave_z[1])
        grad_y = projected(value_re, value_im, slope_y[0], slope_y[1], wave_z[0], wave_z[1])
        grad_z = projected(value_re, value_im, wave_y[0], wave_y[1], slope_z[0], slope_z[1])
        pushed = -(charges_now / cell_size) * jnp.stack([grad_x, grad_y, grad_z])
        return jnp.transpose(pushed.reshape(3, bundle_size, atom_total), (1, 0, 2))

    long_force = lax.psum_scatter(
        lax.map(
            bundle_push,
            gathered.reshape(
                lax.axis_size(("dy", "dz")) * 1 // bundle_size, bundle_size, 7, atom_total
            ),
        ).reshape(lax.axis_size(("dy", "dz")) * 1, 3, atom_total),
        ("dy", "dz"),
        scatter_dimension=0,
        tiled=True,
    )[0]
    forces = (short_force + long_force).reshape(3, 2, 2, 2, octants)
    return (node_next, forces)


def solution(mesh):
    placed = (
        P("dx", "dy", "dz", None, None),
        P(None, "dx", "dy", "dz", None),
        P(None, "dx", "dy", "dz", None),
        P("dx", "dy", "dz", None),
        P("dx", "dy", "dz", None, None),
        P("dx", "dy", "dz", None),
        P(),
        P(),
        P(),
    )
    return jax.shard_map(
        shards,
        mesh=mesh,
        in_specs=placed,
        out_specs=(P("dx", "dy", "dz", None, None), P(None, "dx", "dy", "dz", None)),
        check_vma=False,
    )
```

profile of v0, /device:TPU:0, one launch (start us, length us, event | category | flops | bytes accessed | tf_op | source)
XLA Modules:
  0.0 413.6 jit_solution(6346871818479647586)
XLA Ops:
  12.8 9.4 %all-gather.2 = f32[8,7,256]{2,1,0:T(8,128)S(1)} all-gather(f32[1,7,256]{2,1,0:T(8,128)S(1)} %maximum_bitcast_fusion.1), channel_id=2, replica_groups=mesh['dx'=4,'dy'=4,'dz'=2] {'dy','dz'}, dimensions={0}, use_global_device_ids=true | all-gather | bytes 64512 | tf_op jit(solution)/shard_map/all_gather | solution.py:254
  22.3 13.1 %while.47 = (s32[]{:T(128)}, f32[2,35,2,128]{3,1,2,0:T(8,128)S(1)}, f32[2,4,7,256]{3,2,1,0:T(8,128)S(1)}, s32[]{:T(128)}, s32[]{:T(128)}, /*index=5*/s32[]{:T(128)}) while((s32[]{:T(128)}, f32[2,35,2,128]{3,1,2,0:T(8,128)S(1)}, f32[2,4,7,256]{3,2,1,0:T(8,128)S(1)}, s32[]{:T(128)}, s32[]{:T(128)}, ...), condition=%wide.region_7.8_spmd.clone.clone, body=%wide.region_6.7_spmd.clone.clone.sunk | while | flops 113572632 | bytes 1195285 | solution.py:284
  35.4 13.8 %all-gather.1 = f32[512,2,35]{0,2,1:T(8,128)S(1)} all-gather(f32[128,2,35]{0,2,1:T(8,128)S(1)} %bitcast.429), channel_id=3, replica_groups=mesh['dx'=4,'dy'=4,'dz'=2] {'dx'}, dimensions={0}, use_global_device_ids=true | all-gather | bytes 179200 | tf_op jit(solution)/shard_map/all_gather | solution.py:290
  54.5 27.1 %while.48 = (s32[]{:T(128)}, f32[2,4,3,256]{3,2,1,0:T(4,128)S(1)}, f32[2,4,7,256]{3,1,2,0:T(4,128)S(1)}, s32[]{:T(128)}, f32[35,128]{1,0:T(8,128)S(1)}, /*index=5*/f32[35,128]{1,0:T(8,128)S(1)}, s32[]{:T(128)}, s32[]{:T(128)}) while((s32[]{:T(128)}, f32[2,4,3,256]{3,2,1,0:T(4,128)S(1)}, ...), condition=%wide.region_19.20_spmd.clone.clone, body=%wide.region_9.19_spmd.clone.clone.sunk | while | flops 227147808 | bytes 4978981 | solution.py:350
  84.7 22.3 %all-reduce = f32[8,3,256]{2,1,0:T(4,128)S(1)} all-reduce(f32[8,3,256]{2,1,0:T(4,128)S(1)} %bitcast.467), channel_id=4, replica_groups=mesh['dx'=4,'dy'=4,'dz'=2] {'dy','dz'}, use_global_device_ids=true, to_apply=%region_20.21.clone | all-reduce | flops 6144 | bytes 49152
  118.7 294.2 %while.46 = (s32[]{:T(128)}, bf16[16,16,128]{2,1,0:T(8,128)(2,1)S(1)}, f32[16,3,16]{2,1,0:T(4,128)S(1)}, bf16[16,16,128]{2,1,0:T(8,128)(2,1)S(1)}, s32[16]{0:T(1...) while((s32[]{:T(128)}, ...), condition=%wide.region_5.6_spmd.clone, body=%wide.region_0.5_spmd.clone.sunk | while | flops 43745308 | bytes 6859662 | solution.py:229
  129.8 6.2 %gather_fusion = bf16[2048,128]{1,0:T(8,128)(2,1)S(1)} fusion(bf16[2048,128]{1,0:T(8,128)(2,1)S(1)} %get-tuple-element.1437, s32[2048]{0:T(1024)S(1)} %bitcast_clamp_fusion.2), kind=kCustom, calls=%fused_computation.1.clone.clone.1 | custom fusion | bytes 1056768 | tf_op jit(solution)/shard_map/while/body/eval_jaxpr/gather | solution.py:226
  141.1 5.5 %gather_fusion.1 = f32[2048,3]{1,0:T(8,128)S(1)} fusion(f32[3,2048]{0,1:T(8,128)S(1)} %get-tuple-element.1431, s32[2048]{0:T(1024)S(1)} %bitcast_clamp_fusion.2), kind=kCustom, calls=%fused_computation.clone.clone.1 | custom fusion | bytes 57344 | tf_op jit(solution)/shard_map/while/body/eval_jaxpr/gather | solution.py:222
  148.2 6.2 %gather_fusion = bf16[2048,128]{1,0:T(8,128)(2,1)S(1)} fusion(bf16[2048,128]{1,0:T(8,128)(2,1)S(1)} %get-tuple-element.1437, s32[2048]{0:T(1024)S(1)} %bitcast_clamp_fusion.2), kind=kCustom, calls=%fused_computation.1.clone.clone.1 | custom fusion | bytes 1056768 | tf_op jit(solution)/shard_map/while/body/eval_jaxpr/gather | solution.py:226
  159.4 5.5 %gather_fusion.1 = f32[2048,3]{1,0:T(8,128)S(1)} fusion(f32[3,2048]{0,1:T(8,128)S(1)} %get-tuple-element.1431, s32[2048]{0:T(1024)S(1)} %bitcast_clamp_fusion.2), kind=kCustom, calls=%fused_computation.clone.clone.1 | custom fusion | bytes 57344 | tf_op jit(solution)/shard_map/while/body/eval_jaxpr/gather | solution.py:222
  166.6 6.2 %gather_fusion = bf16[2048,128]{1,0:T(8,128)(2,1)S(1)} fusion(bf16[2048,128]{1,0:T(8,128)(2,1)S(1)} %get-tuple-element.1437, s32[2048]{0:T(1024)S(1)} %bitcast_clamp_fusion.2), kind=kCustom, calls=%fused_computation.1.clone.clone.1 | custom fusion | bytes 1056768 | tf_op jit(solution)/shard_map/while/body/eval_jaxpr/gather | solution.py:226
  185.0 6.2 %gather_fusion = bf16[2048,128]{1,0:T(8,128)(2,1)S(1)} fusion(bf16[2048,128]{1,0:T(8,128)(2,1)S(1)} %get-tuple-element.1437, s32[2048]{0:T(1024)S(1)} %bitcast_clamp_fusion.2), kind=kCustom, calls=%fused_computation.1.clone.clone.1 | custom fusion | bytes 1056768 | tf_op jit(solution)/shard_map/while/body/eval_jaxpr/gather | solution.py:226
  203.4 6.2 %gather_fusion = bf16[2048,128]{1,0:T(8,128)(2,1)S(1)} fusion(bf16[2048,128]{1,0:T(8,128)(2,1)S(1)} %get-tuple-element.1437, s32[2048]{0:T(1024)S(1)} %bitcast_clamp_fusion.2), kind=kCustom, calls=%fused_computation.1.clone.clone.1 | custom fusion | bytes 1056768 | tf_op jit(solution)/shard_map/while/body/eval_jaxpr/gather | solution.py:226
  214.6 5.5 %gather_fusion.1 = f32[2048,3]{1,0:T(8,128)S(1)} fusion(f32[3,2048]{0,1:T(8,128)S(1)} %get-tuple-element.1431, s32[2048]{0:T(1024)S(1)} %bitcast_clamp_fusion.2), kind=kCustom, calls=%fused_computation.clone.clone.1 | custom fusion | bytes 57344 | tf_op jit(solution)/shard_map/while/body/eval_jaxpr/gather | solution.py:222
  221.8 6.2 %gather_fusion = bf16[2048,128]{1,0:T(8,128)(2,1)S(1)} fusion(bf16[2048,128]{1,0:T(8,128)(2,1)S(1)} %get-tuple-element.1437, s32[2048]{0:T(1024)S(1)} %bitcast_clamp_fusion.2), kind=kCustom, calls=%fused_computation.1.clone.clone.1 | custom fusion | bytes 1056768 | tf_op jit(solution)/shard_map/while/body/eval_jaxpr/gather | solution.py:226
  233.0 5.5 %gather_fusion.1 = f32[2048,3]{1,0:T(8,128)S(1)} fusion(f32[3,2048]{0,1:T(8,128)S(1)} %get-tuple-element.1431, s32[2048]{0:T(1024)S(1)} %bitcast_clamp_fusion.2), kind=kCustom, calls=%fused_computation.clone.clone.1 | custom fusion | bytes 57344 | tf_op jit(solution)/shard_map/while/body/eval_jaxpr/gather | solution.py:222
  240.2 6.2 %gather_fusion = bf16[2048,128]{1,0:T(8,128)(2,1)S(1)} fusion(bf16[2048,128]{1,0:T(8,128)(2,1)S(1)} %get-tuple-element.1437, s32[2048]{0:T(1024)S(1)} %bitcast_clamp_fusion.2), kind=kCustom, calls=%fused_computation.1.clone.clone.1 | custom fusion | bytes 1056768 | tf_op jit(solution)/shard_map/while/body/eval_jaxpr/gather | solution.py:226
  258.5 6.2 %gather_fusion = bf16[2048,128]{1,0:T(8,128)(2,1)S(1)} fusion(bf16[2048,128]{1,0:T(8,128)(2,1)S(1)} %get-tuple-element.1437, s32[2048]{0:T(1024)S(1)} %bitcast_clamp_fusion.2), kind=kCustom, calls=%fused_computation.1.clone.clone.1 | custom fusion | bytes 1056768 | tf_op jit(solution)/shard_map/while/body/eval_jaxpr/gather | solution.py:226
  269.8 5.5 %gather_fusion.1 = f32[2048,3]{1,0:T(8,128)S(1)} fusion(f32[3,2048]{0,1:T(8,128)S(1)} %get-tuple-element.1431, s32[2048]{0:T(1024)S(1)} %bitcast_clamp_fusion.2), kind=kCustom, calls=%fused_computation.clone.clone.1 | custom fusion | bytes 57344 | tf_op jit(solution)/shard_map/while/body/eval_jaxpr/gather | solution.py:222
  276.9 6.2 %gather_fusion = bf16[2048,128]{1,0:T(8,128)(2,1)S(1)} fusion(bf16[2048,128]{1,0:T(8,128)(2,1)S(1)} %get-tuple-element.1437, s32[2048]{0:T(1024)S(1)} %bitcast_clamp_fusion.2), kind=kCustom, calls=%fused_computation.1.clone.clone.1 | custom fusion | bytes 1056768 | tf_op jit(solution)/shard_map/while/body/eval_jaxpr/gather | solution.py:226
  288.2 5.5 %gather_fusion.1 = f32[2048,3]{1,0:T(8,128)S(1)} fusion(f32[3,2048]{0,1:T(8,128)S(1)} %get-tuple-element.1431, s32[2048]{0:T(1024)S(1)} %bitcast_clamp_fusion.2), kind=kCustom, calls=%fused_computation.clone.clone.1 | custom fusion | bytes 57344 | tf_op jit(solution)/shard_map/while/body/eval_jaxpr/gather | solution.py:222
  295.3 6.2 %gather_fusion = bf16[2048,128]{1,0:T(8,128)(2,1)S(1)} fusion(bf16[2048,128]{1,0:T(8,128)(2,1)S(1)} %get-tuple-element.1437, s32[2048]{0:T(1024)S(1)} %bitcast_clamp_fusion.2), kind=kCustom, calls=%fused_computation.1.clone.clone.1 | custom fusion | bytes 1056768 | tf_op jit(solution)/shard_map/while/body/eval_jaxpr/gather | solution.py:226
  306.5 5.5 %gather_fusion.1 = f32[2048,3]{1,0:T(8,128)S(1)} fusion(f32[3,2048]{0,1:T(8,128)S(1)} %get-tuple-element.1431, s32[2048]{0:T(1024)S(1)} %bitcast_clamp_fusion.2), kind=kCustom, calls=%fused_computation.clone.clone.1 | custom fusion | bytes 57344 | tf_op jit(solution)/shard_map/while/body/eval_jaxpr/gather | solution.py:222
  313.7 6.2 %gather_fusion = bf16[2048,128]{1,0:T(8,128)(2,1)S(1)} fusion(bf16[2048,128]{1,0:T(8,128)(2,1)S(1)} %get-tuple-element.1437, s32[2048]{0:T(1024)S(1)} %bitcast_clamp_fusion.2), kind=kCustom, calls=%fused_computation.1.clone.clone.1 | custom fusion | bytes 1056768 | tf_op jit(solution)/shard_map/while/body/eval_jaxpr/gather | solution.py:226
  332.1 6.2 %gather_fusion = bf16[2048,128]{1,0:T(8,128)(2,1)S(1)} fusion(bf16[2048,128]{1,0:T(8,128)(2,1)S(1)} %get-tuple-element.1437, s32[2048]{0:T(1024)S(1)} %bitcast_clamp_fusion.2), kind=kCustom, calls=%fused_computation.1.clone.clone.1 | custom fusion | bytes 1056768 | tf_op jit(solution)/shard_map/while/body/eval_jaxpr/gather | solution.py:226
  343.3 5.5 %gather_fusion.1 = f32[2048,3]{1,0:T(8,128)S(1)} fusion(f32[3,2048]{0,1:T(8,128)S(1)} %get-tuple-element.1431, s32[2048]{0:T(1024)S(1)} %bitcast_clamp_fusion.2), kind=kCustom, calls=%fused_computation.clone.clone.1 | custom fusion | bytes 57344 | tf_op jit(solution)/shard_map/while/body/eval_jaxpr/gather | solution.py:222
  350.5 6.2 %gather_fusion = bf16[2048,128]{1,0:T(8,128)(2,1)S(1)} fusion(bf16[2048,128]{1,0:T(8,128)(2,1)S(1)} %get-tuple-element.1437, s32[2048]{0:T(1024)S(1)} %bitcast_clamp_fusion.2), kind=kCustom, calls=%fused_computation.1.clone.clone.1 | custom fusion | bytes 1056768 | tf_op jit(solution)/shard_map/while/body/eval_jaxpr/gather | solution.py:226
  361.7 5.5 %gather_fusion.1 = f32[2048,3]{1,0:T(8,128)S(1)} fusion(f32[3,2048]{0,1:T(8,128)S(1)} %get-tuple-element.1431, s32[2048]{0:T(1024)S(1)} %bitcast_clamp_fusion.2), kind=kCustom, calls=%fused_computation.clone.clone.1 | custom fusion | bytes 57344 | tf_op jit(solution)/shard_map/while/body/eval_jaxpr/gather | solution.py:222
  368.9 6.2 %gather_fusion = bf16[2048,128]{1,0:T(8,128)(2,1)S(1)} fusion(bf16[2048,128]{1,0:T(8,128)(2,1)S(1)} %get-tuple-element.1437, s32[2048]{0:T(1024)S(1)} %bitcast_clamp_fusion.2), kind=kCustom, calls=%fused_computation.1.clone.clone.1 | custom fusion | bytes 1056768 | tf_op jit(solution)/shard_map/while/body/eval_jaxpr/gather | solution.py:226
  380.1 5.5 %gather_fusion.1 = f32[2048,3]{1,0:T(8,128)S(1)} fusion(f32[3,2048]{0,1:T(8,128)S(1)} %get-tuple-element.1431, s32[2048]{0:T(1024)S(1)} %bitcast_clamp_fusion.2), kind=kCustom, calls=%fused_computation.clone.clone.1 | custom fusion | bytes 57344 | tf_op jit(solution)/shard_map/while/body/eval_jaxpr/gather | solution.py:222
  387.3 6.2 %gather_fusion = bf16[2048,128]{1,0:T(8,128)(2,1)S(1)} fusion(bf16[2048,128]{1,0:T(8,128)(2,1)S(1)} %get-tuple-element.1437, s32[2048]{0:T(1024)S(1)} %bitcast_clamp_fusion.2), kind=kCustom, calls=%fused_computation.1.clone.clone.1 | custom fusion | bytes 1056768 | tf_op jit(solution)/shard_map/while/body/eval_jaxpr/gather | solution.py:226
  405.6 6.2 %gather_fusion = bf16[2048,128]{1,0:T(8,128)(2,1)S(1)} fusion(bf16[2048,128]{1,0:T(8,128)(2,1)S(1)} %get-tuple-element.1437, s32[2048]{0:T(1024)S(1)} %bitcast_clamp_fusion.2), kind=kCustom, calls=%fused_computation.1.clone.clone.1 | custom fusion | bytes 1056768 | tf_op jit(solution)/shard_map/while/body/eval_jaxpr/gather | solution.py:226
  (723 shorter events, 168.1 us)
Async XLA Ops:
  1.4 80.3 %collective-permute-start = (f32[3,1,2,2,32]{4,3,2,1,0:T(2,128)S(1)}, f32[3,1,2,2,32]{4,3,2,1,0:T(2,128)S(1)}, u32[]{:S(2)}, u32[]{:S(2)}) collective-permute-start(f32[3,1,2,2,32]{4,3,2,1,0:T(2,128)S(1)} %get-tuple-element.1008), channel_id=1, source_target_pairs={{0,8},{8,16},{16,24},{24,0},{1,9},{9,17},{17,25},{25,1},{2,10},{10... | collective-permute-start | bytes 4616 | tf_op jit(solution)/shard_map/ppermute | solution.py:29
  4.5 77.2 %collective-permute-start.1 = (f32[3,1,2,2,32]{4,3,2,1,0:T(2,128)S(1)}, f32[3,1,2,2,32]{4,3,2,1,0:T(2,128)S(1)}, u32[]{:S(2)}, u32[]{:S(2)}) collective-permute-start(f32[3,1,2,2,32]{4,3,2,1,0:T(2,128)S(1)} %get-tuple-element.1009), channel_id=1, source_target_pairs={{8,0},{16,8},{24,16},{0,24},{9,1},{17,9},{25,17},{1,25},{10,2},{18... | collective-permute-start | bytes 4616 | tf_op jit(solution)/shard_map/ppermute | solution.py:31
  7.3 3.9 copy-start.3
  7.3 100.9 %collective-permute-start.6 = (bf16[1,2,2,32,128]{4,3,2,1,0:T(8,128)(2,1)S(1)}, bf16[1,2,2,32,128]{4,3,2,1,0:T(8,128)(2,1)S(1)}, u32[]{:S(2)}, u32[]{:S(2)}) collective-permute-start(bf16[1,2,2,32,128]{4,3,2,1,0:T(8,128)(2,1)S(1)} %get-tuple-element.1003), channel_id=1, source_target_pairs={{0,8},{8,16},{16,24},{24,0},{1,9},{9,17},{17,25},{25,1},{2,10},{10... | collective-permute-start | bytes 98312 | tf_op jit(solution)/shard_map/ppermute | solution.py:29
  7.4 101.7 %collective-permute-start.7 = (bf16[1,2,2,32,128]{4,3,2,1,0:T(8,128)(2,1)S(1)}, bf16[1,2,2,32,128]{4,3,2,1,0:T(8,128)(2,1)S(1)}, u32[]{:S(2)}, u32[]{:S(2)}) collective-permute-start(bf16[1,2,2,32,128]{4,3,2,1,0:T(8,128)(2,1)S(1)} %get-tuple-element.1002), channel_id=1, source_target_pairs={{8,0},{16,8},{24,16},{0,24},{9,1},{17,9},{25,17},{1,25},{10,2},{18... | collective-permute-start | bytes 98312 | tf_op jit(solution)/shard_map/ppermute | solution.py:31
  11.2 0.7 copy-start.4
  12.1 0.7 copy-start.7
  81.7 26.6 %collective-permute-start.2 = (f32[3,4,1,2,32]{4,3,2,1,0:T(2,128)S(1)}, f32[3,4,1,2,32]{4,3,2,1,0:T(2,128)S(1)}, u32[]{:S(2)}, u32[]{:S(2)}) collective-permute-start(f32[3,4,1,2,32]{4,3,2,1,0:T(2,128)S(1)} %get-tuple-element.1006), channel_id=1, source_target_pairs={{0,2},{2,4},{4,6},{6,0},{1,3},{3,5},{5,7},{7,1},{8,10},{10,12},{12... | collective-permute-start | bytes 9224 | tf_op jit(solution)/shard_map/ppermute | solution.py:29
  83.2 25.0 %collective-permute-start.3 = (f32[3,4,1,2,32]{4,3,2,1,0:T(2,128)S(1)}, f32[3,4,1,2,32]{4,3,2,1,0:T(2,128)S(1)}, u32[]{:S(2)}, u32[]{:S(2)}) collective-permute-start(f32[3,4,1,2,32]{4,3,2,1,0:T(2,128)S(1)} %get-tuple-element.1007), channel_id=1, source_target_pairs={{2,0},{4,2},{6,4},{0,6},{3,1},{5,3},{7,5},{1,7},{10,8},{12,10},{14... | collective-permute-start | bytes 9224 | tf_op jit(solution)/shard_map/ppermute | solution.py:31
  107.0 0.7 copy-start.9
  108.2 0.8 copy-start.1
  109.1 5.2 %collective-permute-start.8 = (bf16[4,1,2,32,128]{4,3,2,1,0:T(8,128)(2,1)S(1)}, bf16[4,1,2,32,128]{4,3,2,1,0:T(8,128)(2,1)S(1)}, u32[]{:S(2)}, u32[]{:S(2)}) collective-permute-start(bf16[4,1,2,32,128]{4,3,2,1,0:T(8,128)(2,1)S(1)} %get-tuple-element.1000), channel_id=1, source_target_pairs={{0,2},{2,4},{4,6},{6,0},{1,3},{3,5},{5,7},{7,1},{8,10},{10,12},{12... | collective-permute-start | bytes 196616 | tf_op jit(solution)/shard_map/ppermute | solution.py:29
  109.2 5.9 %collective-permute-start.9 = (bf16[4,1,2,32,128]{4,3,2,1,0:T(8,128)(2,1)S(1)}, bf16[4,1,2,32,128]{4,3,2,1,0:T(8,128)(2,1)S(1)}, u32[]{:S(2)}, u32[]{:S(2)}) collective-permute-start(bf16[4,1,2,32,128]{4,3,2,1,0:T(8,128)(2,1)S(1)} %get-tuple-element.1001), channel_id=1, source_target_pairs={{2,0},{4,2},{6,4},{0,6},{3,1},{5,3},{7,5},{1,7},{10,8},{12,10},{14... | collective-permute-start | bytes 196616 | tf_op jit(solution)/shard_map/ppermute | solution.py:31
  112.2 5.1 %collective-permute-start.4 = (f32[3,4,4,1,32]{4,3,2,1,0:T(1,128)S(1)}, f32[3,4,4,1,32]{4,3,2,1,0:T(1,128)S(1)}, u32[]{:S(2)}, u32[]{:S(2)}) collective-permute-start(f32[3,4,4,1,32]{4,3,2,1,0:T(1,128)S(1)} %get-tuple-element.1004), channel_id=1, source_target_pairs={{0,1},{1,0},{2,3},{3,2},{4,5},{5,4},{6,7},{7,6},{8,9},{9,8},{10,11... | collective-permute-start | bytes 18440 | tf_op jit(solution)/shard_map/ppermute | solution.py:29
  112.2 5.0 %collective-permute-start.5 = (f32[3,4,4,1,32]{4,3,2,1,0:T(1,128)S(1)}, f32[3,4,4,1,32]{4,3,2,1,0:T(1,128)S(1)}, u32[]{:S(2)}, u32[]{:S(2)}) collective-permute-start(f32[3,4,4,1,32]{4,3,2,1,0:T(1,128)S(1)} %get-tuple-element.1005), channel_id=1, source_target_pairs={{1,0},{0,1},{3,2},{2,3},{5,4},{4,5},{7,6},{6,7},{9,8},{8,9},{11,10... | collective-permute-start | bytes 18440 | tf_op jit(solution)/shard_map/ppermute | solution.py:31
  115.2 2.7 collective-permute-start.10
  115.2 2.6 collective-permute-start.11
  116.5 0.7 copy-start.6
  117.8 0.9 copy-start
  117.9 0.8 copy-start.2
  117.9 0.8 copy-start.5
  412.9 0.7 copy-start.8
where the time goes:
time: 417 us; the launch traced here: 414 us
  local copies, waits for them, and re-layouts  212 us (51%)
  matrix products  49.1 us (12%)
  blocking collectives  45.6 us (11%)
  loops' own time  45.2 us (11%)
  other arithmetic  42.1 us (10%)
  starting transfers between devices  16.1 us (4%)
    gather x16, local copies, waits for them, and re-layouts, one_block(): flat_state[neighbour]  98.9 us
    gather x32, local copies, waits for them, and re-layouts, one_block(): displace = flat_places[:, neighbour] + wrap_shift - own_places[:, :, None]  92.7 us
    another operation x1, loops' own time, shards(): lax.map(one_block, (jnp.arange(16, dtype=jnp.int32), nbr_code.reshape(16,...  44.6 us
    unnamed x1, blocking collectives  22.3 us
    all_gather x1, blocking collectives, shards(): received = lax.all_gather(slab_rows[None], 'dx', axis=0, tiled=True)  13.8 us
    mul x16, other arithmetic, one_block(): (reach_x - jnp.mod(reach_x, 2 * count_x)) * half_block  12.1 us
    gather x16, other arithmetic, one_block(): displace = flat_places[:, neighbour] + wrap_shift - own_places[:, :, None]  11.9 us
    ppermute x6, starting transfers between devices, with_halo(): lax.ppermute(head, axis, [((i + 1) % count, i) for i in range(count)])  11.3 us
  transfers between devices with their start and end apart: 12, of which 2 were waited for; matrix products, arithmetic and copies ran while one was open for 12% of the time, Pallas kernels for 0%

commit v1 on v0

--- a/solution.py
+++ b/solution.py
@@ -1,8 +1,11 @@
+import functools
 import math
 
 import jax
 import jax.numpy as jnp
 from jax import lax
+from jax.experimental import pallas as pl
+from jax.experimental.pallas import tpu as pltpu
 from jax.sharding import PartitionSpec as P
 
 NB = 8
@@ -17,22 +20,6 @@
 sigma_low = 8.0
 sigma_rate = 1.5
 highest = lax.Precision.HIGHEST
-
-
-def with_halo(cells, sides, width):
-    for axis, dim in sides:
-        count = lax.axis_size(axis)
-        head = lax.slice_in_dim(cells, 0, width, axis=dim)
-        tail = lax.slice_in_dim(cells, cells.shape[dim] - width, cells.shape[dim], axis=dim)
-        cells = jnp.concatenate(
-            [
-                lax.ppermute(tail, axis, [(i, (i + 1) % count) for i in range(count)]),
-                cells,
-                lax.ppermute(head, axis, [((i + 1) % count, i) for i in range(count)]),
-            ],
-            axis=dim,
-        )
-    return cells
 
 
 def spline_terms(fraction):
@@ -58,59 +45,271 @@
     return (weights, slopes)
 
 
-def harmonics(direction):
-    unit_x, unit_y, unit_z = (direction[0], direction[1], direction[2])
+def spread_halo(block, width):
+    for axis, dim in (("dx", 0), ("dy", 1), ("dz", 2)):
+        count = lax.axis_size(axis)
+        head = lax.slice_in_dim(block, 0, width, axis=dim)
+        tail = lax.slice_in_dim(block, block.shape[dim] - width, block.shape[dim], axis=dim)
+        block = jnp.concatenate(
+            [
+                lax.ppermute(tail, axis, [(i, (i + 1) % count) for i in range(count)]),
+                block,
+                lax.ppermute(head, axis, [((i + 1) % count, i) for i in range(count)]),
+            ],
+            axis=dim,
+        )
+    return block
+
+
+def exact_pieces(values):
+    pieces = []
+    for _ in range(3):
+        piece = lax.reduce_precision(values, 8, 7)
+        pieces.append(piece.astype(jnp.bfloat16))
+        values = values - piece
+    return pieces
+
+
+def pack_atoms(node_state, places):
+    slots = node_state.shape[3]
+    channels = node_state.shape[4]
+    cells = jnp.concatenate(exact_pieces(places), axis=4)
+    cells = jnp.transpose(cells, (1, 2, 3, 0, 4))
+    cells = jnp.pad(cells, ((0, 0),) * 3 + ((0, 13), (0, channels - 3 * slots)))
+    return jnp.concatenate([node_state, cells], axis=3)
+
+
+def neighbour_kernel(
+    sizes,
+    packed_ref,
+    code_ref,
+    own_ref,
+    radial_ref,
+    mix_ref,
+    force_ref,
+    next_ref,
+    push_ref,
+    place_ref,
+    state_ref,
+    table_ref,
+    count_ref,
+    hot_ref,
+    message_ref,
+    *edge_refs,
+):
+    count_x, count_y, count_z, slots, basis = sizes
+    octant = pl.program_id(0)
+    columns = state_ref.shape[0]
+    tiles = columns // 128
+    per_tile = 128 // slots
+    corner = ((octant // 4) * 4 + octant // 2 % 2) * 4 + octant % 2
+    sides = [(side // 9 * 4 + side // 3 % 3) * 4 + side % 3 for side in range(27)]
+    row_of = lax.broadcasted_iota(jnp.int32, (8, 128), 0)
+    lane_of = lax.broadcasted_iota(jnp.int32, (8, 128), 1)
+
+    @pl.when(octant == 0)
+    def _():
+        half = MB // 2
+        state_ref[27 * slots :, :] = jnp.zeros((slots, 128), jnp.bfloat16)
+        starts = [2 * lax.axis_index(axis) - 1 for axis in ("dx", "dy", "dz")]
+
+        def unwrapped(place, start, count):
+            reach = start + place
+            below = jnp.where(reach < 0, -2 * count * half, 0)
+            return jnp.where(reach >= 2 * count, 2 * count * half, below).astype(jnp.float32)
+
+        @pl.loop(0, 64)
+        def _(cell):
+            rows = packed_ref[cell, slots : slots + 16, :].astype(jnp.float32)[:8]
+            total = (rows + pltpu.roll(rows, 128 - slots, 1)) + pltpu.roll(rows, 128 - 2 * slots, 1)
+            shift_x = unwrapped(cell // 16, starts[0], count_x)
+            shift_y = unwrapped(cell // 4 % 4, starts[1], count_y)
+            shift_z = unwrapped(cell % 4, starts[2], count_z)
+            shift = jnp.where(row_of == 0, shift_x, jnp.where(row_of == 1, shift_y, shift_z))
+            place_ref[cell] = total + shift
+
+    for side in range(27):
+        state_ref[side * slots : (side + 1) * slots, :] = packed_ref[corner + sides[side], :slots, :]
+    for tile in range(tiles):
+        joined = jnp.zeros((8, 128), jnp.float32)
+        for part in range(per_tile):
+            side = tile * per_tile + part
+            if side < 27:
+                moved = place_ref[corner + sides[side]]
+                if part:
+                    moved = pltpu.roll(moved, part * slots, 1)
+                joined = jnp.where(lane_of // slots == part, moved, joined)
+        table_ref[tile] = joined
+
+    cell_iota = lax.broadcasted_iota(jnp.int32, (128, 128), 0).astype(jnp.float32).astype(jnp.bfloat16)
+    one = jnp.ones((128, 128), jnp.bfloat16)
+    zero = jnp.zeros((128, 128), jnp.bfloat16)
+    for block in range(slots // 8):
+        rows = slice(8 * block, 8 * block + 8)
+        codes = code_ref[rows, :]
+        live = lane_of.astype(jnp.float32) < own_ref[rows, 3:4]
+        high = jnp.where(live, codes // 128, 64)
+        low = (codes % 128).astype(jnp.float32)
+        for atom in range(8):
+            low_row = jnp.broadcast_to(low[atom : atom + 1], (16, 128)).astype(jnp.bfloat16)
+            low_hot = jnp.where(cell_iota == jnp.concatenate([low_row] * 8, axis=0), one, zero)
+            high_hot = (row_of == high[atom : atom + 1]).astype(jnp.float32).astype(jnp.bfloat16)
+            count_ref[:, 8 * block + atom, :] = lax.dot_general(
+                high_hot, low_hot, (((1,), (1,)), ((), ())), preferred_element_type=jnp.float32
+            )
+    lane_float = lane_of.astype(jnp.float32)
+    for block in range(slots // 8):
+        rows = slice(8 * block, 8 * block + 8)
+        best = jnp.full((8, 128), -1.0, jnp.float32)
+        for tile in range(tiles):
+            times = count_ref[tile, rows, :]
+            split = (times == 3.0) | ((times > 4.0) & (times < 8.0))
+            best = jnp.where(split, lane_float + 128.0 * tile, best)
+        chosen = jnp.max(best, axis=1, keepdims=True)
+        rest = jnp.zeros((8, 128), jnp.float32)
+        for tile in range(tiles):
+            times = count_ref[tile, rows, :]
+            hot = lane_float + 128.0 * tile == chosen
+            part = jnp.where(times > 4.0, times - 4.0, times - 2.0)
+            rest = rest + jnp.where(hot, part, 0.0)
+            count_ref[tile, rows, :] = jnp.where(hot, times - part, times)
+            hot_ref[rows, tile * 128 : tile * 128 + 128] = jnp.where(hot, 1.0, 0.0)
+        total = jnp.sum(rest, axis=1, keepdims=True)
+        spare = lane_of - (128 - slots) == row_of + 8 * block
+        last = count_ref[tiles - 1, rows, :]
+        count_ref[tiles - 1, rows, :] = jnp.where(spare, total, last)
+    hots = hot_ref[...]
+    state_ref[27 * slots :, :] = jnp.dot(
+        hots.astype(jnp.bfloat16), state_ref[...], preferred_element_type=jnp.float32
+    ).astype(jnp.bfloat16)
+    spots = jnp.concatenate([table_ref[tile] for tile in range(tiles)], axis=1)
+    found = lax.dot_general(
+        spots, hots, (((1,), (1,)), ((), ())), precision=highest, preferred_element_type=jnp.float32
+    )
+    table_ref[tiles - 1] = jnp.where(
+        lane_of < 128 - slots, table_ref[tiles - 1], jnp.concatenate([found] * per_tile, axis=1)
+    )
+
     root_three = math.sqrt(3.0)
     root_fifteen = math.sqrt(15.0)
     root_five = math.sqrt(5.0)
-    return jnp.stack(
-        [
-            jnp.ones_like(unit_x),
-            root_three * unit_x,
-            root_three * unit_y,
-            root_three * unit_z,
-            root_fifteen * unit_x * unit_y,
-            root_fifteen * unit_y * unit_z,
-            0.5 * root_five * (3.0 * unit_z * unit_z - 1.0),
-            root_fifteen * unit_x * unit_z,
-            0.5 * root_fifteen * (unit_x * unit_x - unit_y * unit_y),
-        ]
-    )
-
-
-def edge_terms(displace, active):
-    square = jnp.sum(displace * displace, axis=0)
-    direction = displace / jnp.sqrt(square + 1.0)
-    angular = harmonics(direction)
-    distance = cell_size * jnp.sqrt(square)
-    widths = sigma_low * jnp.power(sigma_rate, jnp.arange(NB).astype(jnp.float32))
-    radial = jnp.exp(-jnp.square(distance[None] / widths[:, None, None]))
-    products = radial[:, None] * angular[None] * active.astype(jnp.float32)[None, None]
-    atom_rows = displace.shape[1]
-    return jnp.transpose(products, (2, 0, 1, 3)).reshape(atom_rows, NB * 9, -1).astype(jnp.bfloat16)
-
-
-def node_update(edge_values, neighbour_state, own_state, radial_weight, mix_weight, force_weight):
-    summed = jnp.einsum(
-        "bkn,bnc->bkc", edge_values, neighbour_state, preferred_element_type=jnp.float32
-    )
-    atom_rows = summed.shape[0]
-    summed = summed.reshape(atom_rows, NB, 9, -1)
-    message = (jnp.sum(summed * radial_weight[None, :, None, :], axis=1) / math.sqrt(NBR)).astype(
-        jnp.bfloat16
-    )
-    scalar = jnp.dot(message[:, 0], mix_weight[0], preferred_element_type=jnp.float32)
-    vector = jnp.einsum(
-        "bmc,cd->bmd", message[:, 1:4], mix_weight[1], preferred_element_type=jnp.float32
-    )
-    tensor = jnp.einsum(
-        "bmc,cd->bmd", message[:, 4:9], mix_weight[2], preferred_element_type=jnp.float32
-    )
-    invariant = scalar + jnp.sum(tensor * tensor, axis=1)
-    gating = jax.nn.sigmoid(invariant)
-    updated = (own_state.astype(jnp.float32) + jax.nn.silu(invariant)).astype(jnp.bfloat16)
-    short_push = jnp.sum(vector * (gating * force_weight)[:, None, :], axis=2)
-    return (updated, jnp.transpose(short_push))
+    rates = [
+        -(cell_size**2) / (sigma_low * sigma_rate**b) ** 2 * math.log2(math.e) for b in range(basis)
+    ]
+    for block in range(slots // 8):
+        rows = slice(8 * block, 8 * block + 8)
+        edge_ref = edge_refs[block % len(edge_refs)]
+        own = own_ref[rows, :]
+        for tile in range(tiles):
+            times = count_ref[tile, rows, :]
+            spots = table_ref[tile]
+            dx = spots[0:1] - own[:, 0:1]
+            dy = spots[1:2] - own[:, 1:2]
+            dz = spots[2:3] - own[:, 2:3]
+            square = dx * dx + dy * dy + dz * dz
+            scale = lax.rsqrt(square + 1.0)
+            ux = dx * scale
+            uy = dy * scale
+            uz = dz * scale
+            tx = root_fifteen * ux
+            angular = [
+                None,
+                root_three * ux,
+                root_three * uy,
+                root_three * uz,
+                tx * uy,
+                root_fifteen * uy * uz,
+                0.5 * root_five * (3.0 * uz * uz - 1.0),
+                tx * uz,
+                0.5 * root_fifteen * (ux * ux - uy * uy),
+            ]
+            for pair in range(basis // 2):
+                first = times * jnp.exp2(square * rates[2 * pair])
+                second = times * jnp.exp2(square * rates[2 * pair + 1])
+                for degree in range(9):
+                    if degree:
+                        parts = [first * angular[degree], second * angular[degree]]
+                    else:
+                        parts = [first, second]
+                    at = (degree * basis + 2 * pair) * 8
+                    edge_ref[at : at + 16, tile * 128 : tile * 128 + 128] = jnp.concatenate(
+                        parts, axis=0
+                    ).astype(jnp.bfloat16)
+        summed = jnp.dot(edge_ref[...], state_ref[...], preferred_element_type=jnp.float32)
+        for degree in range(9):
+            total = summed[degree * basis * 8 : degree * basis * 8 + 8] * radial_ref[0:1, :]
+            for b in range(1, basis):
+                at = (degree * basis + b) * 8
+                total = total + summed[at : at + 8] * radial_ref[b : b + 1, :]
+            message_ref[degree, rows, :] = total / math.sqrt(NBR)
+    message = message_ref[...].astype(jnp.bfloat16).reshape(9 * slots, 128)
+    scalar = jnp.dot(message[:slots], mix_ref[0], preferred_element_type=jnp.float32)
+    vector = jnp.dot(message[slots : 4 * slots], mix_ref[1], preferred_element_type=jnp.float32)
+    tensor = jnp.dot(message[4 * slots :], mix_ref[2], preferred_element_type=jnp.float32)
+    invariant = scalar
+    squares = tensor * tensor
+    for m in range(5):
+        invariant = invariant + squares[m * slots : (m + 1) * slots]
+    gating = 1.0 / (1.0 + jnp.exp(-invariant))
+    own_state = packed_ref[corner + 21, :slots, :].astype(jnp.float32)
+    next_ref[...] = (own_state + invariant * gating).astype(jnp.bfloat16)
+    weighted = gating * force_ref[...]
+    pushes = vector * jnp.concatenate([weighted] * 3, axis=0)
+    push_ref[0] = lax.dot_general(
+        jnp.ones((8, 128), jnp.float32),
+        pushes,
+        (((1,), (1,)), ((), ())),
+        precision=highest,
+        preferred_element_type=jnp.float32,
+    )
+
+
+def neighbour_sums(packed, nbr_code, own_rows, radial_weight, mix_weight, force_weight):
+    slots = nbr_code.shape[3]
+    channels = packed.shape[-1]
+    basis = radial_weight.shape[0]
+    columns = 28 * slots
+    sizes = (lax.axis_size("dx"), lax.axis_size("dy"), lax.axis_size("dz"), slots, basis)
+    edges = pltpu.VMEM((9 * basis * 8, columns), jnp.bfloat16)
+    whole = lambda *shape: pl.BlockSpec(shape, lambda o: (0,) * len(shape))
+    return pl.pallas_call(
+        functools.partial(neighbour_kernel, sizes),
+        grid=(8,),
+        in_specs=[
+            whole(64, slots + 16, channels),
+            pl.BlockSpec((slots, NBR), lambda o: (o, 0)),
+            pl.BlockSpec((slots, 4), lambda o: (o, 0)),
+            whole(basis, channels),
+            whole(3, channels, channels),
+            whole(1, channels),
+        ],
+        out_specs=[
+            pl.BlockSpec((slots, channels), lambda o: (o, 0)),
+            pl.BlockSpec((1, 8, 3 * slots), lambda o: (o, 0, 0)),
+        ],
+        out_shape=[
+            jax.ShapeDtypeStruct((8 * slots, channels), jnp.bfloat16),
+            jax.ShapeDtypeStruct((8, 8, 3 * slots), jnp.float32),
+        ],
+        scratch_shapes=[
+            pltpu.VMEM((64, 8, 128), jnp.float32),
+            pltpu.VMEM((columns, channels), jnp.bfloat16),
+            pltpu.VMEM((columns // 128, 8, 128), jnp.float32),
+            pltpu.VMEM((8, slots, 128), jnp.float32),
+            pltpu.VMEM((slots, columns), jnp.float32),
+            pltpu.VMEM((9, slots, channels), jnp.float32),
+            edges,
+            edges,
+        ],
+        cost_estimate=pl.CostEstimate(flops=4_200_000_000, bytes_accessed=2_000_000, transcendentals=2_000_000),
+    )(
+        packed.reshape(64, slots + 16, channels),
+        nbr_code.reshape(8 * slots, NBR),
+        own_rows,
+        radial_weight,
+        mix_weight,
+        force_weight[None],
+    )
 
 
 def phases(wavenumber, cell_index, extent):
@@ -188,56 +387,15 @@
     length_y = MB * count_y
     length_z = MB * count_z
     places = mesh_base.astype(jnp.float32) + mesh_frac
-    halo_state = with_halo(node_state, (("dx", 0), ("dy", 1), ("dz", 2)), 1)
-    halo_places = with_halo(places, (("dx", 1), ("dy", 2), ("dz", 3)), 1)
-    flat_state = halo_state.reshape(64 * octants, channels)
-    flat_places = halo_places.reshape(3, 64 * octants)
-    piece_rows = octants // 2
-    slot_index = jnp.arange(NBR, dtype=jnp.int32)
-
-    def one_block(inputs):
-        block_id, code_rows, count_rows, own_places, state_rows = inputs
-        octant = block_id // 2
-        corner_x = octant // 4
-        corner_y = octant // 2 % 2
-        corner_z = octant % 2
-        side_code = code_rows // octants
-        slot_code = code_rows % octants
-        step_x = side_code // 9 - 1
-        step_y = side_code // 3 % 3 - 1
-        step_z = side_code % 3 - 1
-        neighbour = (
-            ((corner_x + 1 + step_x) * 4 + corner_y + 1 + step_y) * 4 + corner_z + 1 + step_z
-        ) * octants + slot_code
-        reach_x = 2 * index_x + corner_x + step_x
-        reach_y = 2 * index_y + corner_y + step_y
-        reach_z = 2 * index_z + corner_z + step_z
-        wrap_shift = jnp.stack(
-            [
-                (reach_x - jnp.mod(reach_x, 2 * count_x)) * half_block,
-                (reach_y - jnp.mod(reach_y, 2 * count_y)) * half_block,
-                (reach_z - jnp.mod(reach_z, 2 * count_z)) * half_block,
-            ]
-        ).astype(jnp.float32)
-        displace = flat_places[:, neighbour] + wrap_shift - own_places[:, :, None]
-        active = slot_index[None, :] < count_rows[:, None]
-        edge_values = edge_terms(displace, active)
-        return node_update(
-            edge_values, flat_state[neighbour], state_rows, radial_weight, mix_weight, force_weight
-        )
-
-    updated, short_push = lax.map(
-        one_block,
-        (
-            jnp.arange(16, dtype=jnp.int32),
-            nbr_code.reshape(16, piece_rows, NBR),
-            nbr_count.reshape(16, piece_rows),
-            jnp.transpose(places.reshape(3, 16, piece_rows), (1, 0, 2)),
-            node_state.reshape(16, piece_rows, channels),
-        ),
+    packed_halo = spread_halo(pack_atoms(node_state, places), 1)
+    own_rows = jnp.transpose(
+        jnp.concatenate([places, nbr_count.astype(jnp.float32)[None]], axis=0).reshape(4, atom_total)
+    )
+    updated, pushes = neighbour_sums(
+        packed_halo, nbr_code, own_rows, radial_weight, mix_weight, force_weight
     )
     node_next = updated.reshape(node_state.shape)
-    short_force = jnp.transpose(short_push, (1, 0, 2)).reshape(3, atom_total)
+    short_force = jnp.transpose(pushes[:, 0].reshape(8, 3, octants), (1, 0, 2)).reshape(3, atom_total)
     base_rows = mesh_base.reshape(3, atom_total)
     frac_rows = mesh_frac.reshape(3, atom_total)
     charge_rows = charge.reshape(atom_total)

time: 417 us -> 144 us (0.35)
  local copies, waits for them, and re-layouts: 212 us -> 5.56 us
  loops' own time: 45.2 us -> 0.54 us
  Pallas kernels: 0 us -> 34.2 us
  other arithmetic: 42.1 us -> 11.7 us
  matrix products: 49.1 us -> 36.4 us
  starting transfers between devices: 16.1 us -> 8.73 us
    gather x48 -> x0, local copies, waits for them, and re-layouts: 192 us -> none  [the longest x16 98.9 us: one_block(): flat_state[neighbour]]
    another operation x1 -> x0, loops' own time: 44.6 us -> none  [shards(): lax.map(one_block, (jnp.arange(16, dtype=jnp.int32), nbr_code.reshape(16,...]
    pallas_call x0 -> x1, Pallas kernels: none -> 34.2 us  [neighbour_sums(): pl.pallas_call(functools.partial(neighbour_kernel, sizes), grid=(8,), in_...]
    mul x80 -> x0, other arithmetic: 13.3 us -> none  [the longest x16 12.1 us: one_block(): (reach_x - jnp.mod(reach_x, 2 * count_x)) * half_block]
    dot_general x64 -> x0, matrix products: 12.7 us -> none  [the longest x16 4.8 us: node_update(): jnp.einsum('bkn,bnc->bkc', edge_values, neighbour_state, preferred_elemen...]
    gather x16 -> x0, other arithmetic: 11.9 us -> none  [one_block(): displace = flat_places[:, neighbour] + wrap_shift - own_places[:, :, None]]
    dynamic_slice x48 -> x0, local copies, waits for them, and re-layouts: 10.2 us -> none  [shards(): lax.map(one_block, (jnp.arange(16, dtype=jnp.int32), nbr_code.reshape(16,...]
    ppermute x12 -> x6, starting transfers between devices: 16.1 us -> 8.73 us  [the longest x3 4.71 us: spread_halo(): lax.ppermute(tail, axis, [(i, (i + 1) % count) for i in range(count)])]
  transfers between devices with their start and end apart: 12 -> 6, of which waited for: 2 -> 0; matrix products, arithmetic and copies ran while one was open for 12% -> 35% of each run, Pallas kernels for 0% -> 0%
where the time goes in v1:
time: 144 us
  blocking collectives  45.3 us (31%)
  matrix products  36.4 us (25%)
  Pallas kernels  34.2 us (24%)
  other arithmetic  11.7 us (8%)
  starting transfers between devices  8.73 us (6%)
  local copies, waits for them, and re-layouts  5.56 us (4%)
    pallas_call x1, Pallas kernels, neighbour_sums(): pl.pallas_call(functools.partial(neighbour_kernel, sizes), grid=(8,), in_...  34.2 us
    unnamed x1, blocking collectives  22.3 us
    all_gather x1, blocking collectives, shards(): received = lax.all_gather(slab_rows[None], 'dx', axis=0, tiled=True)  13.6 us
    all_gather x1, blocking collectives, shards(): gathered = lax.all_gather(packed, ('dy', 'dz'), axis=0, tiled=True)  9.41 us
    dot_general x2, matrix products, bundle_push(): jnp.dot(table_now, back_im_cols, precision=highest)  5.98 us
    dot_general x2, matrix products, bundle_push(): jnp.dot(table_now, back_re_cols, precision=highest)  5.58 us
    dot_general x2, matrix products, bundle_push(): jnp.dot(tilt_now, back_re_cols, precision=highest)  5.58 us
    dot_general x2, matrix products, bundle_push(): jnp.dot(tilt_now, back_im_cols, precision=highest)  5.54 us
  transfers between devices with their start and end apart: 6, of which 0 were waited for; matrix products, arithmetic and copies ran while one was open for 35% of the time, Pallas kernels for 0%

profile of v1, /device:TPU:0, one launch (start us, length us, event | category | flops | bytes accessed | tf_op | source)
XLA Modules:
  0.0 143.5 jit_solution(16902204620556518412)
XLA Ops:
  1.5 0.8 fusion.215
  2.3 3.1 %collective-permute-start = (bf16[1,2,2,48,128]{4,3,2,1,0:T(8,128)(2,1)S(1)}, bf16[1,2,2,48,128]{4,3,2,1,0:T(8,128)(2,1)S(1)}, u32[]{:S(2)}, u32[]{:S(2)}) collective-permute-start(bf16[1,2,2,48,128]{4,3,2,1,0:T(8,128)(2,1)S(1)} %get-tuple-element.580), channel_id=1, source_target_pairs={{0,8},{8,16},{16,24},{24,0},{1,9},{9,17},{17,25},{25,1},{2,10},{10... | collective-permute-start | bytes 147464 | tf_op jit(solution)/shard_map/ppermute | solution.py:55
  5.4 2.1 %collective-permute-start.1 = (bf16[1,2,2,48,128]{4,3,2,1,0:T(8,128)(2,1)S(1)}, bf16[1,2,2,48,128]{4,3,2,1,0:T(8,128)(2,1)S(1)}, u32[]{:S(2)}, u32[]{:S(2)}) collective-permute-start(bf16[1,2,2,48,128]{4,3,2,1,0:T(8,128)(2,1)S(1)} %get-tuple-element.581), channel_id=1, source_target_pairs={{8,0},{16,8},{24,16},{0,24},{9,1},{17,9},{25,17},{1,25},{10,2},{18... | collective-permute-start | bytes 147464 | tf_op jit(solution)/shard_map/ppermute | solution.py:57
  8.2 0.8 reshape.2567
  9.1 0.8 broadcast_in_dim_reshape.4
  9.9 9.4 %all-gather.2 = f32[8,7,256]{2,1,0:T(8,128)S(1)} all-gather(f32[1,7,256]{2,1,0:T(8,128)S(1)} %maximum_bitcast_fusion.1), channel_id=2, replica_groups=mesh['dx'=4,'dy'=4,'dz'=2] {'dy','dz'}, dimensions={0}, use_global_device_ids=true | all-gather | bytes 64512 | tf_op jit(solution)/shard_map/all_gather | solution.py:412
  19.3 13.1 %while.30 = (s32[]{:T(128)}, f32[2,35,2,128]{3,1,2,0:T(8,128)S(1)}, f32[2,4,7,256]{3,2,1,0:T(8,128)S(1)}, s32[]{:T(128)}, s32[]{:T(128)}, /*index=5*/s32[]{:T(128)}) while((s32[]{:T(128)}, f32[2,35,2,128]{3,1,2,0:T(8,128)S(1)}, f32[2,4,7,256]{3,2,1,0:T(8,128)S(1)}, s32[]{:T(128)}, s32[]{:T(128)}, ...), condition=%wide.region_1.2_spmd.clone.clone, body=%wide.region_0.1_spmd.clone.clone.sunk | while | flops 113572632 | bytes 1195285 | solution.py:442
  19.5 1.1 multiply_add_fusion.12
  21.3 2.3 %convolution_bitcast_fusion.12 = f32[35,1,128]{2,0,1:T(8,128)S(1)} fusion(f32[1024,8]{0,1:T(8,128)S(1)} %get-tuple-element.760, f32[1024,16]{0,1:T(8,128)S(1)} %get-tuple-element.769, f32[1024,8]{0,1:T(8,128)S(1)} %get-tuple-element.770, f32[1024,16]{0,1:T(8,128)S(1)} %get-tuple-element.771, f32[1024]{0:T(1024)S(1)} %bitcast.340, ...), kind=kOutput, calls=%fused_computation.11.clone.1 | convolution fusion | flops 55873536 | bytes 251392 | tf_op jit(solution)/shard_map/while/body/eval_jaxpr/dot_general | solution.py:435
  23.6 2.3 %convolution_bitcast_fusion.11 = f32[35,1,128]{2,0,1:T(8,128)S(1)} fusion(f32[1024,8]{0,1:T(8,128)S(1)} %get-tuple-element.760, f32[1024,16]{0,1:T(8,128)S(1)} %get-tuple-element.769, f32[1024,8]{0,1:T(8,128)S(1)} %get-tuple-element.770, f32[1024,16]{0,1:T(8,128)S(1)} %get-tuple-element.771, f32[1024]{0:T(1024)S(1)} %bitcast.341, ...), kind=kOutput, calls=%fused_computation.10.clone.1 | convolution fusion | flops 55873536 | bytes 251392 | tf_op jit(solution)/shard_map/while/body/eval_jaxpr/dot_general | solution.py:436
  26.1 1.1 multiply_add_fusion.12
  27.9 2.3 %convolution_bitcast_fusion.12 = f32[35,1,128]{2,0,1:T(8,128)S(1)} fusion(f32[1024,8]{0,1:T(8,128)S(1)} %get-tuple-element.760, f32[1024,16]{0,1:T(8,128)S(1)} %get-tuple-element.769, f32[1024,8]{0,1:T(8,128)S(1)} %get-tuple-element.770, f32[1024,16]{0,1:T(8,128)S(1)} %get-tuple-element.771, f32[1024]{0:T(1024)S(1)} %bitcast.340, ...), kind=kOutput, calls=%fused_computation.11.clone.1 | convolution fusion | flops 55873536 | bytes 251392 | tf_op jit(solution)/shard_map/while/body/eval_jaxpr/dot_general | solution.py:435
  30.1 2.3 %convolution_bitcast_fusion.11 = f32[35,1,128]{2,0,1:T(8,128)S(1)} fusion(f32[1024,8]{0,1:T(8,128)S(1)} %get-tuple-element.760, f32[1024,16]{0,1:T(8,128)S(1)} %get-tuple-element.769, f32[1024,8]{0,1:T(8,128)S(1)} %get-tuple-element.770, f32[1024,16]{0,1:T(8,128)S(1)} %get-tuple-element.771, f32[1024]{0:T(1024)S(1)} %bitcast.341, ...), kind=kOutput, calls=%fused_computation.10.clone.1 | convolution fusion | flops 55873536 | bytes 251392 | tf_op jit(solution)/shard_map/while/body/eval_jaxpr/dot_general | solution.py:436
  32.5 13.6 %all-gather.1 = f32[512,2,35]{0,2,1:T(8,128)S(1)} all-gather(f32[128,2,35]{0,2,1:T(8,128)S(1)} %bitcast.306), channel_id=3, replica_groups=mesh['dx'=4,'dy'=4,'dz'=2] {'dx'}, dimensions={0}, use_global_device_ids=true | all-gather | bytes 179200 | tf_op jit(solution)/shard_map/all_gather | solution.py:448
  51.4 1.5 %collective-permute-start.2 = (bf16[4,1,2,48,128]{4,3,2,1,0:T(8,128)(2,1)S(1)}, bf16[4,1,2,48,128]{4,3,2,1,0:T(8,128)(2,1)S(1)}, u32[]{:S(2)}, u32[]{:S(2)}) collective-permute-start(bf16[4,1,2,48,128]{4,3,2,1,0:T(8,128)(2,1)S(1)} %get-tuple-element.576), channel_id=1, source_target_pairs={{0,2},{2,4},{4,6},{6,0},{1,3},{3,5},{5,7},{7,1},{8,10},{10,12},{12... | collective-permute-start | bytes 294920 | tf_op jit(solution)/shard_map/ppermute | solution.py:55
  52.9 1.4 collective-permute-start.3
  54.4 27.1 %while.31 = (s32[]{:T(128)}, f32[2,4,3,256]{3,2,1,0:T(4,128)S(1)}, f32[2,4,7,256]{3,1,2,0:T(4,128)S(1)}, s32[]{:T(128)}, f32[35,128]{1,0:T(8,128)S(1)}, /*index=5*/f32[35,128]{1,0:T(8,128)S(1)}, s32[]{:T(128)}, s32[]{:T(128)}) while((s32[]{:T(128)}, f32[2,4,3,256]{3,2,1,0:T(4,128)S(1)}, ...), condition=%wide.region_13.14_spmd.clone.clone, body=%wide.region_3.13_spmd.clone.clone.sunk | while | flops 227147808 | bytes 4978981 | solution.py:508
  54.5 2.8 %convolution_bitcast_fusion.15 = f32[1024,16,8]{0,2,1:T(8,128)S(1)} fusion(f32[35,128]{1,0:T(8,128)S(1)} %get-tuple-element.884, f32[1024]{0:T(1024)S(1)} %bitcast.332, s32[1024]{0:T(1024)S(1)} %get-tuple-element.798, f32[1024]{0:T(1024)S(1)} %bitcast.330, s32[1024]{0:T(1024)S(1)} %get-tuple-element.799, f32[1024]{0:T(1024)S(1)} %bitcast.338, ...), kind=kOutput, calls=%fused_computation.155.clone.1 | convolution fusion | flops 55444480 | bytes 574976 | tf_op jit(solution)/shard_map/while/body/eval_jaxpr/dot_general | solution.py:495
  57.3 2.8 %convolution_bitcast_fusion.14 = f32[1024,16,8]{0,2,1:T(8,128)S(1)} fusion(f32[35,128]{1,0:T(8,128)S(1)} %get-tuple-element.885, f32[1024]{0:T(1024)S(1)} %bitcast.333, s32[1024]{0:T(1024)S(1)} %get-tuple-element.798, f32[1024]{0:T(1024)S(1)} %bitcast.331, s32[1024]{0:T(1024)S(1)} %get-tuple-element.799, f32[1024]{0:T(1024)S(1)} %bitcast.339, ...), kind=kOutput, calls=%fused_computation.154.clone.1 | convolution fusion | flops 55444480 | bytes 574976 | tf_op jit(solution)/shard_map/while/body/eval_jaxpr/dot_general | solution.py:496
  60.2 1.2 multiply_add_fusion.13
  61.3 2.8 %convolution_bitcast_fusion.13 = f32[1024,16,8]{0,2,1:T(8,128)S(1)} fusion(f32[35,128]{1,0:T(8,128)S(1)} %get-tuple-element.884, f32[1024]{0:T(1024)S(1)} %bitcast.324, f32[1024]{0:T(1024)S(1)} %bitcast.322, f32[1024]{0:T(1024)S(1)} %bitcast.318, f32[1024]{0:T(1024)S(1)} %bitcast.316, s32[1024]{0:T(1024)S(1)} %get-tuple-element.798, ...), kind=kOutput, calls=%fused_computation.153.clone.1 | convolution fusion | flops 55444480 | bytes 574976 | tf_op jit(solution)/shard_map/while/body/eval_jaxpr/dot_general | solution.py:493
  64.1 3.0 %subtract_reduce_fusion.8 = (f32[1024,8]{0,1:T(8,128)S(1)}, f32[1024,8]{0,1:T(8,128)S(1)}, f32[1024,8]{0,1:T(8,128)S(1)}, f32[1024,8]{0,1:T(8,128)S(1)}, f32[1024,8]{0,1:T(8,128)S(1)}, /*index=5*/f32[1024,8]{0,1:T(8,128)S(1)}) fusion(f32[1024,16,8]{0,2,1:T(8,128)S(1)} %convolution_bitcast_fusion.13, f32[1024,16]{0,1:T(8,128)S(1)} %get-tuple-element.817, ...), kind=kOutput, calls=%fused_computation.173.clone.1 | convolution fusion | flops 58541056 | bytes 2082304 | tf_op jit(solution)/shard_map/while/body/eval_jaxpr/dot_general | solution.py:494
  68.1 2.8 %convolution_bitcast_fusion.15 = f32[1024,16,8]{0,2,1:T(8,128)S(1)} fusion(f32[35,128]{1,0:T(8,128)S(1)} %get-tuple-element.884, f32[1024]{0:T(1024)S(1)} %bitcast.332, s32[1024]{0:T(1024)S(1)} %get-tuple-element.798, f32[1024]{0:T(1024)S(1)} %bitcast.330, s32[1024]{0:T(1024)S(1)} %get-tuple-element.799, f32[1024]{0:T(1024)S(1)} %bitcast.338, ...), kind=kOutput, calls=%fused_computation.155.clone.1 | convolution fusion | flops 55444480 | bytes 574976 | tf_op jit(solution)/shard_map/while/body/eval_jaxpr/dot_general | solution.py:495
  70.9 2.8 %convolution_bitcast_fusion.14 = f32[1024,16,8]{0,2,1:T(8,128)S(1)} fusion(f32[35,128]{1,0:T(8,128)S(1)} %get-tuple-element.885, f32[1024]{0:T(1024)S(1)} %bitcast.333, s32[1024]{0:T(1024)S(1)} %get-tuple-element.798, f32[1024]{0:T(1024)S(1)} %bitcast.331, s32[1024]{0:T(1024)S(1)} %get-tuple-element.799, f32[1024]{0:T(1024)S(1)} %bitcast.339, ...), kind=kOutput, calls=%fused_computation.154.clone.1 | convolution fusion | flops 55444480 | bytes 574976 | tf_op jit(solution)/shard_map/while/body/eval_jaxpr/dot_general | solution.py:496
  73.7 1.2 multiply_add_fusion.13
  74.9 2.8 %convolution_bitcast_fusion.13 = f32[1024,16,8]{0,2,1:T(8,128)S(1)} fusion(f32[35,128]{1,0:T(8,128)S(1)} %get-tuple-element.884, f32[1024]{0:T(1024)S(1)} %bitcast.324, f32[1024]{0:T(1024)S(1)} %bitcast.322, f32[1024]{0:T(1024)S(1)} %bitcast.318, f32[1024]{0:T(1024)S(1)} %bitcast.316, s32[1024]{0:T(1024)S(1)} %get-tuple-element.798, ...), kind=kOutput, calls=%fused_computation.153.clone.1 | convolution fusion | flops 55444480 | bytes 574976 | tf_op jit(solution)/shard_map/while/body/eval_jaxpr/dot_general | solution.py:493
  77.7 3.0 %subtract_reduce_fusion.8 = (f32[1024,8]{0,1:T(8,128)S(1)}, f32[1024,8]{0,1:T(8,128)S(1)}, f32[1024,8]{0,1:T(8,128)S(1)}, f32[1024,8]{0,1:T(8,128)S(1)}, f32[1024,8]{0,1:T(8,128)S(1)}, /*index=5*/f32[1024,8]{0,1:T(8,128)S(1)}) fusion(f32[1024,16,8]{0,2,1:T(8,128)S(1)} %convolution_bitcast_fusion.13, f32[1024,16]{0,1:T(8,128)S(1)} %get-tuple-element.817, ...), kind=kOutput, calls=%fused_computation.173.clone.1 | convolution fusion | flops 58541056 | bytes 2082304 | tf_op jit(solution)/shard_map/while/body/eval_jaxpr/dot_general | solution.py:494
  82.2 22.3 %all-reduce.1 = f32[8,3,256]{2,1,0:T(4,128)S(1)} all-reduce(f32[8,3,256]{2,1,0:T(4,128)S(1)} %bitcast.343), channel_id=4, replica_groups=mesh['dx'=4,'dy'=4,'dz'=2] {'dy','dz'}, use_global_device_ids=true, to_apply=%region_14.15.clone | all-reduce | flops 6144 | bytes 49152
  106.0 0.8 copy.29
  106.8 1.0 pad_maximum_fusion
  107.8 34.2 %shard_map.104 = (bf16[256,128]{1,0:T(8,128)(2,1)}, f32[8,8,96]{2,1,0:T(8,128)}) custom-call(bf16[64,48,128]{2,1,0:T(8,128)(2,1)} %bitcast.272, s32[256,128]{1,0:T(8,128)} %bitcast.344, f32[256,4]{1,0:T(8,128)} %bitcast.307, f32[8,128]{1,0:T(8,128)} %radial_ref.1, bf16[3,128,128]{2,1,0:T(8,128)(2,1)} %mix_ref.1, f32[1,128]{1,0:T(1,128)} %bitcast.345), custom_call_target="tpu_custom_call" | custom-call | flops 4200000000 | bytes 2000000 | tf_op jit(solution)/shard_map/pallas_call | solution.py:275
  142.0 0.8 slice_reduce_fusion
  (132 shorter events, 12.9 us)
Async XLA Ops:
  2.3 49.0 %collective-permute-start = (bf16[1,2,2,48,128]{4,3,2,1,0:T(8,128)(2,1)S(1)}, bf16[1,2,2,48,128]{4,3,2,1,0:T(8,128)(2,1)S(1)}, u32[]{:S(2)}, u32[]{:S(2)}) collective-permute-start(bf16[1,2,2,48,128]{4,3,2,1,0:T(8,128)(2,1)S(1)} %get-tuple-element.580), channel_id=1, source_target_pairs={{0,8},{8,16},{16,24},{24,0},{1,9},{9,17},{17,25},{25,1},{2,10},{10... | collective-permute-start | bytes 147464 | tf_op jit(solution)/shard_map/ppermute | solution.py:55
  5.4 45.9 %collective-permute-start.1 = (bf16[1,2,2,48,128]{4,3,2,1,0:T(8,128)(2,1)S(1)}, bf16[1,2,2,48,128]{4,3,2,1,0:T(8,128)(2,1)S(1)}, u32[]{:S(2)}, u32[]{:S(2)}) collective-permute-start(bf16[1,2,2,48,128]{4,3,2,1,0:T(8,128)(2,1)S(1)} %get-tuple-element.581), channel_id=1, source_target_pairs={{8,0},{16,8},{24,16},{0,24},{9,1},{17,9},{25,17},{1,25},{10,2},{18... | collective-permute-start | bytes 147464 | tf_op jit(solution)/shard_map/ppermute | solution.py:57
  49.2 2.2 %copy-start = (bf16[2,2,2,32,128]{4,3,2,1,0:T(8,128)(2,1)S(1)}, bf16[2,2,2,32,128]{4,3,2,1,0:T(8,128)(2,1)}, u32[]{:S(2)}) copy-start(bf16[2,2,2,32,128]{4,3,2,1,0:T(8,128)(2,1)} %param.13) | copy-start | bytes 196612
  51.4 53.1 %collective-permute-start.2 = (bf16[4,1,2,48,128]{4,3,2,1,0:T(8,128)(2,1)S(1)}, bf16[4,1,2,48,128]{4,3,2,1,0:T(8,128)(2,1)S(1)}, u32[]{:S(2)}, u32[]{:S(2)}) collective-permute-start(bf16[4,1,2,48,128]{4,3,2,1,0:T(8,128)(2,1)S(1)} %get-tuple-element.576), channel_id=1, source_target_pairs={{0,2},{2,4},{4,6},{6,0},{1,3},{3,5},{5,7},{7,1},{8,10},{10,12},{12... | collective-permute-start | bytes 294920 | tf_op jit(solution)/shard_map/ppermute | solution.py:55
  52.9 51.6 %collective-permute-start.3 = (bf16[4,1,2,48,128]{4,3,2,1,0:T(8,128)(2,1)S(1)}, bf16[4,1,2,48,128]{4,3,2,1,0:T(8,128)(2,1)S(1)}, u32[]{:S(2)}, u32[]{:S(2)}) collective-permute-start(bf16[4,1,2,48,128]{4,3,2,1,0:T(8,128)(2,1)S(1)} %get-tuple-element.577), channel_id=1, source_target_pairs={{2,0},{4,2},{6,4},{0,6},{3,1},{5,3},{7,5},{1,7},{10,8},{12,10},{14... | collective-permute-start | bytes 294920 | tf_op jit(solution)/shard_map/ppermute | solution.py:57
  54.4 27.2 %copy-start.2 = (u32[32]{0:T(128)S(1)}, u32[32]{0:T(128)}, u32[]{:S(2)}) copy-start(u32[32]{0:T(128)} %constant.556) | copy-start | bytes 388
  104.5 1.4 copy-start.1
  104.6 2.2 %collective-permute-start.4 = (bf16[4,4,1,48,128]{4,3,2,1,0:T(8,128)(2,1)S(1)}, bf16[4,4,1,48,128]{4,3,2,1,0:T(8,128)(2,1)S(1)}, u32[]{:S(2)}, u32[]{:S(2)}) collective-permute-start(bf16[4,4,1,48,128]{4,3,2,1,0:T(8,128)(2,1)S(1)} %get-tuple-element.574), channel_id=1, source_target_pairs={{0,1},{1,0},{2,3},{3,2},{4,5},{5,4},{6,7},{7,6},{8,9},{9,8},{10,11... | collective-permute-start | bytes 589832 | tf_op jit(solution)/shard_map/ppermute | solution.py:55
  104.7 2.2 %collective-permute-start.5 = (bf16[4,4,1,48,128]{4,3,2,1,0:T(8,128)(2,1)S(1)}, bf16[4,4,1,48,128]{4,3,2,1,0:T(8,128)(2,1)S(1)}, u32[]{:S(2)}, u32[]{:S(2)}) collective-permute-start(bf16[4,4,1,48,128]{4,3,2,1,0:T(8,128)(2,1)S(1)} %get-tuple-element.575), channel_id=1, source_target_pairs={{1,0},{0,1},{3,2},{2,3},{5,4},{4,5},{7,6},{6,7},{9,8},{8,9},{11,10... | collective-permute-start | bytes 589832 | tf_op jit(solution)/shard_map/ppermute | solution.py:57

commit v2 on v1

--- a/solution.py
+++ b/solution.py
@@ -3,6 +3,7 @@
 
 import jax
 import jax.numpy as jnp
+import numpy as np
 from jax import lax
 from jax.experimental import pallas as pl
 from jax.experimental.pallas import tpu as pltpu
@@ -20,29 +21,6 @@
 sigma_low = 8.0
 sigma_rate = 1.5
 highest = lax.Precision.HIGHEST
-
-
-def spline_terms(fraction):
-    remainder = 1.0 - fraction
-    frac_square = fraction * fraction
-    frac_cube = frac_square * fraction
-    weights = jnp.stack(
-        [
-            remainder * remainder * remainder / 6.0,
-            (3.0 * frac_cube - 6.0 * frac_square + 4.0) / 6.0,
-            (-3.0 * frac_cube + 3.0 * frac_square + 3.0 * fraction + 1.0) / 6.0,
-            frac_cube / 6.0,
-        ]
-    )
-    slopes = jnp.stack(
-        [
-            -0.5 * remainder * remainder,
-            1.5 * frac_square - 2.0 * fraction,
-            -1.5 * frac_square + fraction + 0.5,
-            0.5 * frac_square,
-        ]
-    )
-    return (weights, slopes)
 
 
 def spread_halo(block, width):
@@ -312,53 +290,268 @@
     )
 
 
-def phases(wavenumber, cell_index, extent):
-    return 2.0 * math.pi / extent * jnp.mod(wavenumber * cell_index, extent).astype(jnp.float32)
-
-
-def wave_sums(coeff, start_cells, wavenumber, extent, orient):
-    wave_re = jnp.zeros((start_cells.shape[0], wavenumber.shape[0]), jnp.float32)
-    wave_im = jnp.zeros((start_cells.shape[0], wavenumber.shape[0]), jnp.float32)
-    for stencil in range(4):
-        angles = phases(wavenumber[None, :], (start_cells + stencil)[:, None], extent)
-        wave_re = wave_re + coeff[stencil][:, None] * jnp.cos(angles)
-        wave_im = wave_im + coeff[stencil][:, None] * jnp.sin(angles)
-    return (wave_re, orient * wave_im)
-
-
-def cell_table(coeff, local_cells, cell_index):
-    table = jnp.zeros((local_cells.shape[0], cell_index.shape[0]), jnp.float32)
-    for stencil in range(4):
-        match = (cell_index[None, :] == (local_cells + stencil)[:, None]).astype(jnp.float32)
-        table = table + coeff[stencil][:, None] * match
+def spline_rows(fraction):
+    remainder = 1.0 - fraction
+    square = fraction * fraction
+    cube = square * fraction
+    weights = [
+        remainder * remainder * remainder / 6.0,
+        (3.0 * cube - 6.0 * square + 4.0) / 6.0,
+        (-3.0 * cube + 3.0 * square + 3.0 * fraction + 1.0) / 6.0,
+        cube / 6.0,
+    ]
+    slopes = [
+        -0.5 * remainder * remainder,
+        1.5 * square - 2.0 * fraction,
+        -1.5 * square + fraction + 0.5,
+        0.5 * square,
+    ]
+    return weights, slopes
+
+
+def turn(table_ref, steps, extent):
+    def look(index):
+        index = index % extent
+        rows, width = index.shape
+        found = []
+        for start in range(0, width, 128):
+            piece = index[:, start : start + 128]
+            result = None
+            for part in range(-(-extent // 128)):
+                line = jnp.broadcast_to(table_ref[part : part + 1, :], piece.shape)
+                here = jnp.take_along_axis(line, piece % 128, axis=1)
+                result = here if result is None else jnp.where(piece // 128 == part, here, result)
+            found.append(result)
+        return jnp.concatenate(found, axis=1) if len(found) > 1 else found[0]
+
+    return look(steps), look(steps + 3 * extent // 4)
+
+
+def wave_factors(table_ref, modes, base_row, extent):
+    rows = modes.shape[0]
+    width = base_row.shape[1]
+    wide = jnp.broadcast_to(modes[:, :1], (rows, width))
+    first = turn(table_ref, wide * base_row, extent)
+    steps = [turn(table_ref, modes * t, extent) for t in (1, 2, 3)]
+    steps = [tuple(jnp.concatenate([p] * (width // 128), axis=1) for p in pair) for pair in steps]
+    return first, steps
+
+
+def wave_of(factors, coeff):
+    (cos_first, sin_first), steps = factors
+    part_re = coeff[0] + coeff[1] * steps[0][0] + coeff[2] * steps[1][0] + coeff[3] * steps[2][0]
+    part_im = coeff[1] * steps[0][1] + coeff[2] * steps[1][1] + coeff[3] * steps[2][1]
+    return cos_first * part_re - sin_first * part_im, sin_first * part_re + cos_first * part_im
+
+
+def cell_rows(coeff, local_row, cells):
+    row_of = lax.broadcasted_iota(jnp.int32, (cells, local_row.shape[1]), 0)
+    away = row_of - local_row
+    table = jnp.where(away == 3, coeff[3], 0.0)
+    for stencil in (2, 1, 0):
+        table = jnp.where(away == stencil, coeff[stencil], table)
     return table
 
 
-def influence(modes_x, modes_y, modes_z, length_x, length_y, length_z):
-
-    def folded(wavenumber, extent):
-        return jnp.where(2 * wavenumber >= extent, wavenumber - extent, wavenumber).astype(
-            jnp.float32
-        ) / (cell_size * extent)
-
+def halves(values):
+    high = values.astype(jnp.bfloat16).astype(jnp.float32)
+    return high, values - high
+
+
+def wave_start():
+    return lax.axis_index("dy") * lax.axis_size("dz") + lax.axis_index("dz")
+
+
+def spread_kernel(sizes, atoms_ref, table_y_ref, table_z_ref, sums_ref):
+    length_y, length_z, waves, cells = sizes
+    groups, _, width = atoms_ref.shape
+    modes_y = wave_start() * waves + lax.broadcasted_iota(jnp.int32, (waves, 128), 0)
+    modes_z = 1 + lax.broadcasted_iota(jnp.int32, (KZW, 128), 0)
+    anchor = lax.axis_index("dx") * MB
+    total = jnp.zeros(sums_ref.shape, jnp.float32)
+    for group in range(groups):
+        chunk = atoms_ref[group]
+        base = chunk[1:4].astype(jnp.int32)
+        weights, _ = spline_rows(chunk[4:7])
+        row = lambda d: [w[d : d + 1] for w in weights]
+        y_re, y_im = wave_of(wave_factors(table_y_ref, modes_y, base[1:2], length_y), row(1))
+        z_re, z_im = wave_of(wave_factors(table_z_ref, modes_z, base[2:3], length_z), row(2))
+        mixed_re = []
+        mixed_im = []
+        for k in range(waves):
+            k_re = y_re[k : k + 1]
+            k_im = y_im[k : k + 1]
+            mixed_re.append(k_re * z_re - k_im * z_im)
+            mixed_im.append(-(k_re * z_im + k_im * z_re))
+        mixed = jnp.concatenate(mixed_re + mixed_im, axis=0)
+        table = cell_rows(row(0), base[0:1] - anchor, cells) * chunk[0:1]
+        table_high, table_low = halves(table)
+        mixed_high, mixed_low = halves(mixed)
+        both = jnp.concatenate([table_high, table_low], axis=0).astype(jnp.bfloat16)
+        main = lax.dot_general(
+            both,
+            mixed_high.astype(jnp.bfloat16),
+            (((1,), (1,)), ((), ())),
+            preferred_element_type=jnp.float32,
+        )
+        side = lax.dot_general(
+            table_high.astype(jnp.bfloat16),
+            mixed_low.astype(jnp.bfloat16),
+            (((1,), (1,)), ((), ())),
+            preferred_element_type=jnp.float32,
+        )
+        total = total + (main[:cells] + (main[cells:] + side))
+    sums_ref[...] = total
+
+
+def push_kernel(
+    sizes, atoms_ref, sums_ref, forward_ref, back_ref, table_y_ref, table_z_ref, force_ref
+):
+    length_x, length_y, length_z, waves, cells = sizes
+    groups, _, width = atoms_ref.shape
+    modes = waves * KZW
+    start = wave_start() * waves
+    modes_y = start + lax.broadcasted_iota(jnp.int32, (waves, 128), 0)
+    modes_z = 1 + lax.broadcasted_iota(jnp.int32, (KZW, 128), 0)
+    anchor = lax.axis_index("dx") * MB
+
+    turned = jnp.dot(
+        forward_ref[...], sums_ref[...], precision=highest, preferred_element_type=jnp.float32
+    )
+    cosine = turned[:length_x]
+    sine = turned[length_x:]
+
+    def folded(number, extent):
+        number = jnp.where(2 * number >= extent, number - extent, number)
+        return number.astype(jnp.float32) / (cell_size * extent)
+
+    mode_shape = (length_x, modes)
+    mode_x = lax.broadcasted_iota(jnp.int32, mode_shape, 0)
+    mode_lane = lax.broadcasted_iota(jnp.int32, mode_shape, 1)
     wave_square = (
-        jnp.square(folded(modes_x, length_x))
-        + jnp.square(folded(modes_y, length_y))
-        + jnp.square(folded(modes_z, length_z))
+        jnp.square(folded(mode_x, length_x))
+        + jnp.square(folded(start + mode_lane // KZW, length_y))
+        + jnp.square(folded(mode_lane % KZW + 1, length_z))
     )
     volume = cell_size**3 * length_x * length_y * length_z
-    return (
+    green = (
         coulomb
         / (math.pi * volume)
-        * jnp.exp(-math.pi**2 * wave_square / ewald_beta**2)
+        * jnp.exp(-(math.pi**2) * wave_square / ewald_beta**2)
         / wave_square
     )
-
-
-def projected(value_re, value_im, wave_y_re, wave_y_im, wave_z_re, wave_z_im):
-    inner_re = jnp.sum(value_re * wave_y_re[:, :, None] - value_im * wave_y_im[:, :, None], axis=1)
-    inner_im = jnp.sum(value_re * wave_y_im[:, :, None] + value_im * wave_y_re[:, :, None], axis=1)
-    return 2.0 * jnp.sum(inner_re * wave_z_re - inner_im * wave_z_im, axis=1)
+    scaled = jnp.concatenate(
+        [
+            green * (cosine[:, :modes] + sine[:, modes:]),
+            green * (cosine[:, modes:] - sine[:, :modes]),
+        ],
+        axis=1,
+    )
+    lines = back_ref[pl.ds(pl.multiple_of(lax.axis_index("dx") * cells, 8), cells), :]
+    lines = jnp.concatenate([lines[:, :length_x], lines[:, length_x:]], axis=0)
+    turned = jnp.dot(lines, scaled, precision=highest, preferred_element_type=jnp.float32)
+    cosine = turned[:cells]
+    sine = turned[cells:]
+    back = jnp.concatenate(
+        [cosine[:, :modes] - sine[:, modes:], sine[:, :modes] + cosine[:, modes:]], axis=1
+    )
+    back_high, back_low = halves(back)
+    spare = jnp.zeros((128 - 3 * cells, 2 * modes), jnp.float32)
+    stacked = jnp.concatenate([back_high, back_high, back_low, spare], axis=0)
+    stacked = jnp.transpose(stacked).astype(jnp.bfloat16)
+
+    for group in range(groups):
+        chunk = atoms_ref[group]
+        base = chunk[1:4].astype(jnp.int32)
+        weights, slopes = spline_rows(chunk[4:7])
+        row = lambda d: [w[d : d + 1] for w in weights]
+        tilt = lambda d: [w[d : d + 1] for w in slopes]
+        factors_y = wave_factors(table_y_ref, modes_y, base[1:2], length_y)
+        factors_z = wave_factors(table_z_ref, modes_z, base[2:3], length_z)
+        y_re, y_im = wave_of(factors_y, row(1))
+        dy_re, dy_im = wave_of(factors_y, tilt(1))
+        z_re, z_im = wave_of(factors_z, row(2))
+        dz_re, dz_im = wave_of(factors_z, tilt(2))
+
+        def on_atoms(coeff):
+            high, low = halves(cell_rows(coeff, base[0:1] - anchor, cells))
+            none = jnp.zeros((128 - 3 * cells, width), jnp.float32)
+            right = jnp.concatenate([high, low, high, none], axis=0).astype(jnp.bfloat16)
+            return jnp.dot(stacked, right, preferred_element_type=jnp.float32)
+
+        value = on_atoms(row(0))
+        slant = on_atoms(tilt(0))
+
+        def along(field, wave_re, wave_im):
+            sum_re = jnp.zeros((KZW, width), jnp.float32)
+            sum_im = jnp.zeros((KZW, width), jnp.float32)
+            for k in range(waves):
+                f_re = field[k * KZW : (k + 1) * KZW]
+                f_im = field[modes + k * KZW : modes + (k + 1) * KZW]
+                k_re = wave_re[k : k + 1]
+                k_im = wave_im[k : k + 1]
+                sum_re = sum_re + (f_re * k_re - f_im * k_im)
+                sum_im = sum_im + (f_re * k_im + f_im * k_re)
+            return sum_re, sum_im
+
+        def ended(pair, wave_re, wave_im):
+            return 2.0 * jnp.sum(pair[0] * wave_re - pair[1] * wave_im, axis=0, keepdims=True)
+
+        push_x = ended(along(slant, y_re, y_im), z_re, z_im)
+        push_y = ended(along(value, dy_re, dy_im), z_re, z_im)
+        push_z = ended(along(value, y_re, y_im), dz_re, dz_im)
+        force_ref[group] = jnp.concatenate([push_x, push_y, push_z], axis=0) * (
+            -chunk[0:1] / cell_size
+        )
+
+
+def cosine_period(extent):
+    lines = -(-extent // 128)
+    steps = np.arange(lines * 128).reshape(lines, 128)
+    return jnp.asarray(np.cos(2.0 * np.pi * steps / extent).astype(np.float32))
+
+
+def long_range(mesh_base, mesh_frac, charge):
+    count_x = lax.axis_size("dx")
+    count_y = lax.axis_size("dy")
+    count_z = lax.axis_size("dz")
+    atom_total = charge.size
+    groups = count_y * count_z
+    cells = -(-(MB + 3) // 8) * 8
+    length_x = MB * count_x
+    length_y = MB * count_y
+    length_z = MB * count_z
+    waves = MB // count_z
+    modes = waves * KZW
+    packed = jnp.concatenate(
+        [
+            charge.reshape(1, atom_total),
+            mesh_base.reshape(3, atom_total).astype(jnp.float32),
+            mesh_frac.reshape(3, atom_total),
+        ],
+        axis=0,
+    )
+    atoms = lax.all_to_all(
+        jnp.broadcast_to(packed[None], (groups, 7, atom_total)), ("dy", "dz"), 0, 0, tiled=True
+    )
+    table_y = cosine_period(length_y)
+    table_z = cosine_period(length_z)
+    sums = pl.pallas_call(
+        functools.partial(spread_kernel, (length_y, length_z, waves, cells)),
+        out_shape=jax.ShapeDtypeStruct((cells, 2 * modes), jnp.float32),
+    )(atoms, table_y, table_z)
+    received = lax.all_to_all(
+        jnp.broadcast_to(sums[None], (count_x,) + sums.shape), "dx", 0, 0, tiled=True
+    ).reshape(count_x * cells, 2 * modes)
+    places = (np.arange(count_x) * MB)[:, None] + np.arange(cells)[None, :]
+    angles = 2.0 * np.pi / length_x * (np.arange(length_x)[:, None] * places.reshape(1, -1) % length_x)
+    forward = np.concatenate([np.cos(angles), np.sin(angles)], axis=0).astype(np.float32)
+    parts = pl.pallas_call(
+        functools.partial(push_kernel, (length_x, length_y, length_z, waves, cells)),
+        out_shape=jax.ShapeDtypeStruct((groups, 3, atom_total), jnp.float32),
+    )(atoms, received, jnp.asarray(forward), jnp.asarray(forward.T.copy()), table_y, table_z)
+    parts = lax.all_to_all(parts, ("dy", "dz"), 0, 0, tiled=True)
+    return jnp.sum(parts, axis=0)
 
 
 def shards(
@@ -372,20 +565,8 @@
     mix_weight,
     force_weight,
 ):
-    count_x = lax.axis_size("dx")
-    count_y = lax.axis_size("dy")
-    count_z = lax.axis_size("dz")
-    index_x = lax.axis_index("dx")
-    index_y = lax.axis_index("dy")
-    index_z = lax.axis_index("dz")
     octants = node_state.shape[3]
-    channels = node_state.shape[4]
     atom_total = 8 * octants
-    half_block = MB // 2
-    block_cells = MB + 3
-    length_x = MB * count_x
-    length_y = MB * count_y
-    length_z = MB * count_z
     places = mesh_base.astype(jnp.float32) + mesh_frac
     packed_halo = spread_halo(pack_atoms(node_state, places), 1)
     own_rows = jnp.transpose(
@@ -396,125 +577,7 @@
     )
     node_next = updated.reshape(node_state.shape)
     short_force = jnp.transpose(pushes[:, 0].reshape(8, 3, octants), (1, 0, 2)).reshape(3, atom_total)
-    base_rows = mesh_base.reshape(3, atom_total)
-    frac_rows = mesh_frac.reshape(3, atom_total)
-    charge_rows = charge.reshape(atom_total)
-    anchor_x = index_x * MB
-    cell_index = jnp.arange(block_cells, dtype=jnp.int32)
-    planes = 1 + jnp.arange(KZW, dtype=jnp.int32)
-    rows_dev = MB * KZW // count_z
-    row_start = (index_y * count_z + index_z) * rows_dev
-    own_modes = row_start // KZW + jnp.arange(rows_dev // KZW, dtype=jnp.int32)
-    modes_x = jnp.arange(length_x, dtype=jnp.int32)
-    packed = jnp.concatenate([charge_rows[None], base_rows.astype(jnp.float32), frac_rows], axis=0)[
-        None
-    ]
-    gathered = lax.all_gather(packed, ("dy", "dz"), axis=0, tiled=True)
-    group_count = gathered.shape[0]
-    group_size = math.gcd(group_count, 4)
-
-    def bundle_modes(bundle):
-        flat_rows = jnp.transpose(bundle, (1, 0, 2)).reshape(7, -1)
-        charges_now = flat_rows[0]
-        base_now = flat_rows[1:4].astype(jnp.int32)
-        weights_now, slopes_now = spline_terms(flat_rows[4:7])
-        table_now = cell_table(weights_now[:, 0], base_now[0] - anchor_x, cell_index)
-        wave_y_re, wave_y_im = wave_sums(weights_now[:, 1], base_now[1], own_modes, length_y, -1.0)
-        wave_z_re, wave_z_im = wave_sums(weights_now[:, 2], base_now[2], planes, length_z, -1.0)
-        mixed_re = (
-            wave_y_re[:, :, None] * wave_z_re[:, None, :]
-            - wave_y_im[:, :, None] * wave_z_im[:, None, :]
-        ).reshape(-1, rows_dev)
-        mixed_im = (
-            wave_y_re[:, :, None] * wave_z_im[:, None, :]
-            + wave_y_im[:, :, None] * wave_z_re[:, None, :]
-        ).reshape(-1, rows_dev)
-        left_side = jnp.transpose(table_now * charges_now[:, None])
-        return jnp.stack(
-            [
-                jnp.dot(left_side, mixed_re, precision=highest),
-                jnp.dot(left_side, mixed_im, precision=highest),
-            ],
-            axis=1,
-        )
-
-    modes_sum = jnp.sum(
-        lax.map(
-            bundle_modes, gathered.reshape(group_count // group_size, group_size, 7, atom_total)
-        ),
-        axis=0,
-    )
-    slab_rows = jnp.transpose(modes_sum, (2, 1, 0))
-    received = lax.all_gather(slab_rows[None], "dx", axis=0, tiled=True)
-    shard_count = received.shape[0]
-    cells_now = (jnp.arange(shard_count, dtype=jnp.int32) * MB)[:, None] + cell_index[None, :]
-    angle_x = phases(cells_now.reshape(-1)[:, None], modes_x[None, :], length_x)
-    cos_x = jnp.cos(angle_x)
-    sin_x = jnp.sin(angle_x)
-    lined_up = jnp.transpose(received, (1, 2, 0, 3)).reshape(received.shape[1], 2, -1)
-    spec_re = jnp.dot(lined_up[:, 0], cos_x, precision=highest) + jnp.dot(
-        lined_up[:, 1], sin_x, precision=highest
-    )
-    spec_im = jnp.dot(lined_up[:, 1], cos_x, precision=highest) - jnp.dot(
-        lined_up[:, 0], sin_x, precision=highest
-    )
-    spectrum = jnp.stack([spec_re, spec_im], axis=1)
-    global_rows = row_start + jnp.arange(rows_dev, dtype=jnp.int32)
-    green_table = influence(
-        modes_x[None, :],
-        (global_rows // KZW)[:, None],
-        (global_rows % KZW + 1)[:, None],
-        length_x,
-        length_y,
-        length_z,
-    )
-    scaled = spectrum * green_table[:, None, :]
-    angle_back = phases(modes_x[:, None], (anchor_x + cell_index)[None, :], length_x)
-    cos_back = jnp.cos(angle_back)
-    sin_back = jnp.sin(angle_back)
-    back_re = jnp.dot(scaled[:, 0], cos_back, precision=highest) - jnp.dot(
-        scaled[:, 1], sin_back, precision=highest
-    )
-    back_im = jnp.dot(scaled[:, 0], sin_back, precision=highest) + jnp.dot(
-        scaled[:, 1], cos_back, precision=highest
-    )
-    back_re_cols = jnp.transpose(back_re)
-    back_im_cols = jnp.transpose(back_im)
-    wave_count = rows_dev // KZW
-    bundle_size = math.gcd(lax.axis_size(("dy", "dz")) * 1, 4)
-
-    def bundle_push(bundle):
-        flat_rows = jnp.transpose(bundle, (1, 0, 2)).reshape(7, -1)
-        charges_now = flat_rows[0]
-        base_now = flat_rows[1:4].astype(jnp.int32)
-        weights_now, slopes_now = spline_terms(flat_rows[4:7])
-        table_now = cell_table(weights_now[:, 0], base_now[0] - anchor_x, cell_index)
-        tilt_now = cell_table(slopes_now[:, 0], base_now[0] - anchor_x, cell_index)
-        value_re = jnp.dot(table_now, back_re_cols, precision=highest).reshape(-1, wave_count, KZW)
-        value_im = jnp.dot(table_now, back_im_cols, precision=highest).reshape(-1, wave_count, KZW)
-        tilt_re = jnp.dot(tilt_now, back_re_cols, precision=highest).reshape(-1, wave_count, KZW)
-        tilt_im = jnp.dot(tilt_now, back_im_cols, precision=highest).reshape(-1, wave_count, KZW)
-        wave_y = wave_sums(weights_now[:, 1], base_now[1], own_modes, length_y, 1.0)
-        slope_y = wave_sums(slopes_now[:, 1], base_now[1], own_modes, length_y, 1.0)
-        wave_z = wave_sums(weights_now[:, 2], base_now[2], planes, length_z, 1.0)
-        slope_z = wave_sums(slopes_now[:, 2], base_now[2], planes, length_z, 1.0)
-        grad_x = projected(tilt_re, tilt_im, wave_y[0], wave_y[1], wave_z[0], wave_z[1])
-        grad_y = projected(value_re, value_im, slope_y[0], slope_y[1], wave_z[0], wave_z[1])
-        grad_z = projected(value_re, value_im, wave_y[0], wave_y[1], slope_z[0], slope_z[1])
-        pushed = -(charges_now / cell_size) * jnp.stack([grad_x, grad_y, grad_z])
-        return jnp.transpose(pushed.reshape(3, bundle_size, atom_total), (1, 0, 2))
-
-    long_force = lax.psum_scatter(
-        lax.map(
-            bundle_push,
-            gathered.reshape(
-                lax.axis_size(("dy", "dz")) * 1 // bundle_size, bundle_size, 7, atom_total
-            ),
-        ).reshape(lax.axis_size(("dy", "dz")) * 1, 3, atom_total),
-        ("dy", "dz"),
-        scatter_dimension=0,
-        tiled=True,
-    )[0]
+    long_force = long_range(mesh_base, mesh_frac, charge)
     forces = (short_force + long_force).reshape(3, 2, 2, 2, octants)
     return (node_next, forces)
 

time: 144 us -> 88.7 us (0.62)
  blocking collectives: 45.3 us -> 8.08 us
  matrix products: 36.4 us -> 0 us
  waiting for transfers between devices: 0.02 us -> 9.69 us
  starting transfers between devices: 8.73 us -> 16.7 us
  Pallas kernels: 34.2 us -> 42.1 us
  other arithmetic: 11.7 us -> 4.86 us
    dot_general x20 -> x0, matrix products: 36.4 us -> none  [the longest x2 5.98 us: bundle_push(): jnp.dot(table_now, back_im_cols, precision=highest)]
    all_gather x2 -> x0, blocking collectives: 23 us -> none  [the longest x1 13.6 us: shards(): received = lax.all_gather(slab_rows[None], 'dx', axis=0, tiled=True)]
    unnamed x1 -> x0, blocking collectives: 22.3 us -> none
    all_to_all x0 -> x2, waiting for transfers between devices: none -> 9.53 us  [the longest x1 5.57 us: long_range(): lax.all_to_all(jnp.broadcast_to(sums[None], (count_x,) + sums.shape), 'dx...]
    all_to_all x0 -> x1, blocking collectives: none -> 8.08 us  [long_range(): lax.all_to_all(jnp.broadcast_to(packed[None], (groups, 7, atom_total)), (...]
    all_to_all x0 -> x2, starting transfers between devices: none -> 7.97 us  [the longest x1 4.63 us: long_range(): lax.all_to_all(jnp.broadcast_to(sums[None], (count_x,) + sums.shape), 'dx...]
    pallas_call x0 -> x2, Pallas kernels: none -> 7.84 us  [the longest x1 4.88 us: long_range(): pl.pallas_call(functools.partial(push_kernel, (length_x, length_y, length...]
    add x28 -> x0, other arithmetic: 5.95 us -> none  [the longest x4 3.48 us: wave_sums(): wave_re = wave_re + coeff[stencil][:, None] * jnp.cos(angles)]
  transfers between devices with their start and end apart: 6 -> 8, of which waited for: 0 -> 3; matrix products, arithmetic and copies ran while one was open for 35% -> 6% of each run, Pallas kernels for 0% -> 9%
where the time goes in v2:
time: 88.7 us; the launch traced here: 87.9 us
  Pallas kernels  42.1 us (47%)
  starting transfers between devices  16.7 us (19%)
  waiting for transfers between devices  9.69 us (11%)
  blocking collectives  8.08 us (9%)
  local copies, waits for them, and re-layouts  5.77 us (7%)
  other arithmetic  4.86 us (5%)
    pallas_call x1, Pallas kernels, neighbour_sums(): pl.pallas_call(functools.partial(neighbour_kernel, sizes), grid=(8,), in_...  34.2 us
    all_to_all x1, blocking collectives, long_range(): lax.all_to_all(jnp.broadcast_to(packed[None], (groups, 7, atom_total)), (...  8.08 us
    all_to_all x1, waiting for transfers between devices, long_range(): lax.all_to_all(jnp.broadcast_to(sums[None], (count_x,) + sums.shape), 'dx...  5.57 us
    pallas_call x1, Pallas kernels, long_range(): pl.pallas_call(functools.partial(push_kernel, (length_x, length_y, length...  4.88 us
    ppermute x3, starting transfers between devices, spread_halo(): lax.ppermute(tail, axis, [(i, (i + 1) % count) for i in range(count)])  4.78 us
    all_to_all x1, starting transfers between devices, long_range(): lax.all_to_all(jnp.broadcast_to(sums[None], (count_x,) + sums.shape), 'dx...  4.63 us
    all_to_all x1, waiting for transfers between devices, long_range(): parts = lax.all_to_all(parts, ('dy', 'dz'), 0, 0, tiled=True)  3.95 us
    ppermute x3, starting transfers between devices, spread_halo(): lax.ppermute(head, axis, [((i + 1) % count, i) for i in range(count)])  3.95 us
  transfers between devices with their start and end apart: 8, of which 3 were waited for; matrix products, arithmetic and copies ran while one was open for 6% of the time, Pallas kernels for 9%

profile of v2, /device:TPU:0, one launch (start us, length us, event | category | flops | bytes accessed | tf_op | source)
XLA Modules:
  0.0 87.9 jit_solution(14191957614478854220)
XLA Ops:
  0.6 0.7 reduce-precision_convert_fusion.1
  1.4 0.1 maximum_bitcast_fusion
  1.5 0.8 fusion
  2.3 3.1 %collective-permute-start = (bf16[1,2,2,48,128]{4,3,2,1,0:T(8,128)(2,1)S(1)}, bf16[1,2,2,48,128]{4,3,2,1,0:T(8,128)(2,1)S(1)}, u32[]{:S(2)}, u32[]{:S(2)}) collective-permute-start(bf16[1,2,2,48,128]{4,3,2,1,0:T(8,128)(2,1)S(1)} %get-tuple-element.12), channel_id=1, source_target_pairs={{0,8},{8,16},{16,24},{24,0},{1,9},{9,17},{17,25},{25,1},{2,10},{10... | collective-permute-start | bytes 147464 | tf_op jit(solution)/shard_map/ppermute | solution.py:33
  5.4 2.1 %collective-permute-start.1 = (bf16[1,2,2,48,128]{4,3,2,1,0:T(8,128)(2,1)S(1)}, bf16[1,2,2,48,128]{4,3,2,1,0:T(8,128)(2,1)S(1)}, u32[]{:S(2)}, u32[]{:S(2)}) collective-permute-start(bf16[1,2,2,48,128]{4,3,2,1,0:T(8,128)(2,1)S(1)} %get-tuple-element.13), channel_id=1, source_target_pairs={{8,0},{16,8},{24,16},{0,24},{9,1},{17,9},{25,17},{1,25},{10,2},{18... | collective-permute-start | bytes 147464 | tf_op jit(solution)/shard_map/ppermute | solution.py:35
  7.5 0.7 convert_element_type.21
  8.2 0.8 reshape.41
  9.0 0.1 convert_element_type.26
  9.1 0.8 reshape.40
  9.9 0.2 collective-permute-done.1
  10.0 0.9 pad_maximum_fusion.2
  10.9 1.6 %collective-permute-start.2 = (bf16[4,1,2,48,128]{4,3,2,1,0:T(8,128)(2,1)S(1)}, bf16[4,1,2,48,128]{4,3,2,1,0:T(8,128)(2,1)S(1)}, u32[]{:S(2)}, u32[]{:S(2)}) collective-permute-start(bf16[4,1,2,48,128]{4,3,2,1,0:T(8,128)(2,1)S(1)} %get-tuple-element.10), channel_id=1, source_target_pairs={{0,2},{2,4},{4,6},{6,0},{1,3},{3,5},{5,7},{7,1},{8,10},{10,12},{12... | collective-permute-start | bytes 294920 | tf_op jit(solution)/shard_map/ppermute | solution.py:33
  12.5 1.4 %collective-permute-start.3 = (bf16[4,1,2,48,128]{4,3,2,1,0:T(8,128)(2,1)S(1)}, bf16[4,1,2,48,128]{4,3,2,1,0:T(8,128)(2,1)S(1)}, u32[]{:S(2)}, u32[]{:S(2)}) collective-permute-start(bf16[4,1,2,48,128]{4,3,2,1,0:T(8,128)(2,1)S(1)} %get-tuple-element.11), channel_id=1, source_target_pairs={{2,0},{4,2},{6,4},{0,6},{3,1},{5,3},{7,5},{1,7},{10,8},{12,10},{14... | collective-permute-start | bytes 294920 | tf_op jit(solution)/shard_map/ppermute | solution.py:35
  13.9 8.1 %all_to_all.15.atoms_ref = f32[8,7,256]{2,1,0:T(8,128)} all-to-all(f32[8,7,256]{2,1,0:T(8,128)S(1)} %broadcast_in_dim.7), channel_id=1, replica_groups=mesh['dx'=4,'dy'=4,'dz'=2] {'dy','dz'}, dimensions={0} | all-to-all | bytes 114688 | tf_op jit(solution)/shard_map/all_to_all | solution.py:534
  22.0 3.0 %shard_map.141 = f32[40,256]{1,0:T(8,128)} custom-call(f32[8,7,256]{2,1,0:T(8,128)} %all_to_all.15.atoms_ref, f32[1,128]{1,0:T(1,128)} %constant.13.clone.table_y_ref, f32[1,128]{1,0:T(1,128)} %constant.14.clone.table_z_ref), custom_call_target="tpu_custom_call" | custom-call | tf_op jit(solution)/shard_map/pallas_call | solution.py:539
  24.9 1.5 %broadcast_in_dim.8 = f32[4,40,256]{2,1,0:T(8,128)} broadcast(f32[40,256]{1,0:T(8,128)} %shard_map.141), dimensions={1,2} | broadcast | bytes 204800 | tf_op jit(solution)/shard_map/broadcast_in_dim | solution.py:544
  26.4 4.6 %all-to-all-start.1 = ((f32[4,40,256]{2,1,0:T(8,128)}), f32[4,40,256]{2,1,0:T(8,128)S(1)}, u32[]{:S(2)}, u32[]{:S(2)}) async-start(f32[4,40,256]{2,1,0:T(8,128)} %broadcast_in_dim.8), calls=%async_computation.1 | async-start | bytes 327680 | tf_op jit(solution)/shard_map/all_to_all | solution.py:543
  31.2 0.5 collective-permute-start.5
  31.7 0.1 concatenate.31
  31.8 0.1 concatenate.32
  31.9 5.6 %all-to-all-done.1 = f32[4,40,256]{2,1,0:T(8,128)S(1)} async-done(((f32[4,40,256]{2,1,0:T(8,128)}), f32[4,40,256]{2,1,0:T(8,128)S(1)}, u32[]{:S(2)}, u32[]{:S(2)}) %all-to-all-start.1) | async-done | bytes 163872 | tf_op jit(solution)/shard_map/all_to_all | solution.py:543
  37.5 0.7 copy-done.1
  38.1 4.9 %shard_map.142 = f32[8,3,256]{2,1,0:T(4,128)} custom-call(f32[8,7,256]{2,1,0:T(8,128)} %all_to_all.15.atoms_ref, f32[160,256]{1,0:T(8,128)} %bitcast.12, f32[256,160]{1,0:T(8,128)} %constant.15.clone.forward_ref, f32[160,256]{1,0:T(8,128)} %constant.16.clone.back_ref, f32[1,128]{1,0:T(1,128)} %constant.13.clone.table_y_ref, f32[1,128]{1,0:T(1,128)} %constant.14.clone.table_z_ref), custom_call_target="tpu_custom_call" | custom-call | tf_op jit(solution)/shard_map/pallas_call | solution.py:549
  43.0 3.3 %all-to-all-start.2 = ((f32[8,3,256]{2,1,0:T(4,128)}), f32[8,3,256]{2,1,0:T(4,128)S(1)}, u32[]{:S(2)}, u32[]{:S(2)}) async-start(f32[8,3,256]{2,1,0:T(4,128)} %shard_map.142), calls=%async_computation.2 | async-start | bytes 65536 | tf_op jit(solution)/shard_map/all_to_all | solution.py:553
  46.4 0.8 copy.23
  47.2 4.0 %all-to-all-done.2 = f32[8,3,256]{2,1,0:T(4,128)S(1)} async-done(((f32[8,3,256]{2,1,0:T(4,128)}), f32[8,3,256]{2,1,0:T(4,128)S(1)}, u32[]{:S(2)}, u32[]{:S(2)}) %all-to-all-start.2) | async-done | bytes 24608 | tf_op jit(solution)/shard_map/all_to_all | solution.py:553
  51.1 0.1 reduce_sum.12
  51.3 1.0 %pad_maximum_fusion = bf16[4,4,4,48,128]{4,3,2,1,0:T(8,128)(2,1)} fusion(bf16[4,4,1,48,128]{4,3,2,1,0:T(8,128)(2,1)S(1)} %collective-permute-done.5, bf16[4,1,2,48,128]{4,3,2,1,0:T(8,128)(2,1)S(1)} %collective-permute-done.3, bf16[1,2,2,48,128]{4,3,2,1,0:T(8,128)(2,1)S(1)} %collective-permute-done.1, bf16[2,2,2,16,128]{4,3,2,1,0:T(8,128)(2,1)S(1)} %pad.4.clone, ...), kind=kLoop, calls=%fused_computation | loop fusion | flops 6291456 | bytes 1572864 | tf_op jit(solution)/shard_map/concatenate | solution.py:31
  52.2 34.2 %shard_map.140 = (bf16[256,128]{1,0:T(8,128)(2,1)}, f32[8,8,96]{2,1,0:T(8,128)}) custom-call(bf16[64,48,128]{2,1,0:T(8,128)(2,1)} %bitcast.11, s32[256,128]{1,0:T(8,128)} %bitcast.15, f32[256,4]{1,0:T(8,128)} %bitcast.13, f32[8,128]{1,0:T(8,128)} %radial_ref.1, bf16[3,128,128]{2,1,0:T(8,128)(2,1)} %mix_ref.1, f32[1,128]{1,0:T(1,128)} %bitcast.16), custom_call_target="tpu_custom_call" | custom-call | flops 4200000000 | bytes 2000000 | tf_op jit(solution)/shard_map/pallas_call | solution.py:253
  86.4 0.8 slice_reduce_fusion
  87.2 0.1 reshape_squeeze.3
  87.3 0.6 copy_add_fusion
  (22 shorter events, 0.2 us)
Async XLA Ops:
  2.3 7.6 %collective-permute-start = (bf16[1,2,2,48,128]{4,3,2,1,0:T(8,128)(2,1)S(1)}, bf16[1,2,2,48,128]{4,3,2,1,0:T(8,128)(2,1)S(1)}, u32[]{:S(2)}, u32[]{:S(2)}) collective-permute-start(bf16[1,2,2,48,128]{4,3,2,1,0:T(8,128)(2,1)S(1)} %get-tuple-element.12), channel_id=1, source_target_pairs={{0,8},{8,16},{16,24},{24,0},{1,9},{9,17},{17,25},{25,1},{2,10},{10... | collective-permute-start | bytes 147464 | tf_op jit(solution)/shard_map/ppermute | solution.py:33
  5.4 4.6 %collective-permute-start.1 = (bf16[1,2,2,48,128]{4,3,2,1,0:T(8,128)(2,1)S(1)}, bf16[1,2,2,48,128]{4,3,2,1,0:T(8,128)(2,1)S(1)}, u32[]{:S(2)}, u32[]{:S(2)}) collective-permute-start(bf16[1,2,2,48,128]{4,3,2,1,0:T(8,128)(2,1)S(1)} %get-tuple-element.13), channel_id=1, source_target_pairs={{8,0},{16,8},{24,16},{0,24},{9,1},{17,9},{25,17},{1,25},{10,2},{18... | collective-permute-start | bytes 147464 | tf_op jit(solution)/shard_map/ppermute | solution.py:35
  9.9 21.2 %copy-start = (bf16[2,2,2,32,128]{4,3,2,1,0:T(8,128)(2,1)S(1)}, bf16[2,2,2,32,128]{4,3,2,1,0:T(8,128)(2,1)}, u32[]{:S(2)}) copy-start(bf16[2,2,2,32,128]{4,3,2,1,0:T(8,128)(2,1)} %param.13) | copy-start | bytes 196612
  10.9 20.1 %collective-permute-start.2 = (bf16[4,1,2,48,128]{4,3,2,1,0:T(8,128)(2,1)S(1)}, bf16[4,1,2,48,128]{4,3,2,1,0:T(8,128)(2,1)S(1)}, u32[]{:S(2)}, u32[]{:S(2)}) collective-permute-start(bf16[4,1,2,48,128]{4,3,2,1,0:T(8,128)(2,1)S(1)} %get-tuple-element.10), channel_id=1, source_target_pairs={{0,2},{2,4},{4,6},{6,0},{1,3},{3,5},{5,7},{7,1},{8,10},{10,12},{12... | collective-permute-start | bytes 294920 | tf_op jit(solution)/shard_map/ppermute | solution.py:33
  12.5 18.5 %collective-permute-start.3 = (bf16[4,1,2,48,128]{4,3,2,1,0:T(8,128)(2,1)S(1)}, bf16[4,1,2,48,128]{4,3,2,1,0:T(8,128)(2,1)S(1)}, u32[]{:S(2)}, u32[]{:S(2)}) collective-permute-start(bf16[4,1,2,48,128]{4,3,2,1,0:T(8,128)(2,1)S(1)} %get-tuple-element.11), channel_id=1, source_target_pairs={{2,0},{4,2},{6,4},{0,6},{3,1},{5,3},{7,5},{1,7},{10,8},{12,10},{14... | collective-permute-start | bytes 294920 | tf_op jit(solution)/shard_map/ppermute | solution.py:35
  26.4 11.1 %all-to-all-start.1 = ((f32[4,40,256]{2,1,0:T(8,128)}), f32[4,40,256]{2,1,0:T(8,128)S(1)}, u32[]{:S(2)}, u32[]{:S(2)}) async-start(f32[4,40,256]{2,1,0:T(8,128)} %broadcast_in_dim.8), calls=%async_computation.1 | async-start | bytes 327680 | tf_op jit(solution)/shard_map/all_to_all | solution.py:543
  31.0 0.8 copy-start.2
  31.1 20.1 %collective-permute-start.4 = (bf16[4,4,1,48,128]{4,3,2,1,0:T(8,128)(2,1)S(1)}, bf16[4,4,1,48,128]{4,3,2,1,0:T(8,128)(2,1)S(1)}, u32[]{:S(2)}, u32[]{:S(2)}) collective-permute-start(bf16[4,4,1,48,128]{4,3,2,1,0:T(8,128)(2,1)S(1)} %get-tuple-element.8), channel_id=1, source_target_pairs={{0,1},{1,0},{2,3},{3,2},{4,5},{5,4},{6,7},{7,6},{8,9},{9,8},{10,11... | collective-permute-start | bytes 589832 | tf_op jit(solution)/shard_map/ppermute | solution.py:33
  31.2 20.0 %collective-permute-start.5 = (bf16[4,4,1,48,128]{4,3,2,1,0:T(8,128)(2,1)S(1)}, bf16[4,4,1,48,128]{4,3,2,1,0:T(8,128)(2,1)S(1)}, u32[]{:S(2)}, u32[]{:S(2)}) collective-permute-start(bf16[4,4,1,48,128]{4,3,2,1,0:T(8,128)(2,1)S(1)} %get-tuple-element.9), channel_id=1, source_target_pairs={{1,0},{0,1},{3,2},{2,3},{5,4},{4,5},{7,6},{6,7},{9,8},{8,9},{11,10... | collective-permute-start | bytes 589832 | tf_op jit(solution)/shard_map/ppermute | solution.py:35
  37.5 0.7 copy-start.1
  43.0 8.1 %all-to-all-start.2 = ((f32[8,3,256]{2,1,0:T(4,128)}), f32[8,3,256]{2,1,0:T(4,128)S(1)}, u32[]{:S(2)}, u32[]{:S(2)}) async-start(f32[8,3,256]{2,1,0:T(4,128)} %shard_map.142), calls=%async_computation.2 | async-start | bytes 65536 | tf_op jit(solution)/shard_map/all_to_all | solution.py:553

commit v3 on v2

--- a/solution.py
+++ b/solution.py
@@ -9,7 +9,7 @@
 from jax.experimental.pallas import tpu as pltpu
 from jax.sharding import PartitionSpec as P
 
-NB = 8
+
 NBR = 128
 MB = 32
 KZW = 8
@@ -28,14 +28,9 @@
         count = lax.axis_size(axis)
         head = lax.slice_in_dim(block, 0, width, axis=dim)
         tail = lax.slice_in_dim(block, block.shape[dim] - width, block.shape[dim], axis=dim)
-        block = jnp.concatenate(
-            [
-                lax.ppermute(tail, axis, [(i, (i + 1) % count) for i in range(count)]),
-                block,
-                lax.ppermute(head, axis, [((i + 1) % count, i) for i in range(count)]),
-            ],
-            axis=dim,
-        )
+        below = lax.ppermute(tail, axis, [(i, (i + 1) % count) for i in range(count)])
+        above = lax.ppermute(head, axis, [((i + 1) % count, i) for i in range(count)])
+        block = jnp.concatenate([below, block, above], axis=dim)
     return block
 
 
@@ -57,10 +52,56 @@
     return jnp.concatenate([node_state, cells], axis=3)
 
 
+def count_kernel(code_ref, own_ref, count_ref, chosen_ref):
+    slots = code_ref.shape[0]
+    tiles = count_ref.shape[1]
+    row_of = lax.broadcasted_iota(jnp.int32, (8, 128), 0)
+    lane_of = lax.broadcasted_iota(jnp.int32, (8, 128), 1)
+    cell_iota = lax.broadcasted_iota(jnp.int32, (128, 128), 0).astype(jnp.float32).astype(jnp.bfloat16)
+    one = jnp.ones((128, 128), jnp.bfloat16)
+    zero = jnp.zeros((128, 128), jnp.bfloat16)
+    lane_float = lane_of.astype(jnp.float32)
+    for block in range(slots // 8):
+        rows = slice(8 * block, 8 * block + 8)
+        codes = code_ref[rows, :]
+        live = lane_float < own_ref[rows, 3:4]
+        high = jnp.where(live, codes // 128, 64)
+        low = (codes % 128).astype(jnp.float32)
+        for atom in range(8):
+            low_row = jnp.broadcast_to(low[atom : atom + 1], (16, 128)).astype(jnp.bfloat16)
+            low_hot = jnp.where(cell_iota == jnp.concatenate([low_row] * 8, axis=0), one, zero)
+            high_hot = (row_of == high[atom : atom + 1]).astype(jnp.float32).astype(jnp.bfloat16)
+            counted = lax.dot_general(
+                high_hot, low_hot, (((1,), (1,)), ((), ())), preferred_element_type=jnp.float32
+            )
+            count_ref[0, :, 8 * block + atom, :] = counted[:tiles]
+    for block in range(slots // 8):
+        rows = slice(8 * block, 8 * block + 8)
+        best = jnp.full((8, 128), -1.0, jnp.float32)
+        for tile in range(tiles):
+            times = count_ref[0, tile, rows, :]
+            split = (times == 3.0) | ((times > 4.0) & (times < 8.0))
+            best = jnp.where(split, lane_float + 128.0 * tile, best)
+        chosen = jnp.max(best, axis=1, keepdims=True)
+        chosen_ref[rows, :] = jnp.broadcast_to(chosen, (8, 128))
+        rest = jnp.zeros((8, 128), jnp.float32)
+        for tile in range(tiles):
+            times = count_ref[0, tile, rows, :]
+            hot = lane_float + 128.0 * tile == chosen
+            part = jnp.where(times > 4.0, times - 4.0, times - 2.0)
+            rest = rest + jnp.where(hot, part, 0.0)
+            count_ref[0, tile, rows, :] = jnp.where(hot, times - part, times)
+        total = jnp.sum(rest, axis=1, keepdims=True)
+        spare = lane_of - (128 - slots) == row_of + 8 * block
+        last = count_ref[0, tiles - 1, rows, :]
+        count_ref[0, tiles - 1, rows, :] = jnp.where(spare, total, last)
+
+
 def neighbour_kernel(
     sizes,
     packed_ref,
-    code_ref,
+    count_ref,
+    chosen_ref,
     own_ref,
     radial_ref,
     mix_ref,
@@ -70,25 +111,29 @@
     place_ref,
     state_ref,
     table_ref,
-    count_ref,
-    hot_ref,
     message_ref,
     *edge_refs,
 ):
     count_x, count_y, count_z, slots, basis = sizes
     octant = pl.program_id(0)
-    columns = state_ref.shape[0]
+    columns = state_ref.shape[1]
     tiles = columns // 128
     per_tile = 128 // slots
+    blocks = slots // 8
+    atoms = 8 * slots
     corner = ((octant // 4) * 4 + octant // 2 % 2) * 4 + octant % 2
     sides = [(side // 9 * 4 + side // 3 % 3) * 4 + side % 3 for side in range(27)]
     row_of = lax.broadcasted_iota(jnp.int32, (8, 128), 0)
     lane_of = lax.broadcasted_iota(jnp.int32, (8, 128), 1)
+    lane_float = lane_of.astype(jnp.float32)
+    here = octant % 2
+    before = 1 - here
 
     @pl.when(octant == 0)
     def _():
         half = MB // 2
-        state_ref[27 * slots :, :] = jnp.zeros((slots, 128), jnp.bfloat16)
+        for parity in range(2):
+            state_ref[parity, 27 * slots :, :] = jnp.zeros((slots, 128), jnp.bfloat16)
         starts = [2 * lax.axis_index(axis) - 1 for axis in ("dx", "dy", "dz")]
 
         def unwrapped(place, start, count):
@@ -96,7 +141,7 @@
             below = jnp.where(reach < 0, -2 * count * half, 0)
             return jnp.where(reach >= 2 * count, 2 * count * half, below).astype(jnp.float32)
 
-        @pl.loop(0, 64)
+        @pl.loop(0, 64, unroll=8)
         def _(cell):
             rows = packed_ref[cell, slots : slots + 16, :].astype(jnp.float32)[:8]
             total = (rows + pltpu.roll(rows, 128 - slots, 1)) + pltpu.roll(rows, 128 - 2 * slots, 1)
@@ -107,7 +152,9 @@
             place_ref[cell] = total + shift
 
     for side in range(27):
-        state_ref[side * slots : (side + 1) * slots, :] = packed_ref[corner + sides[side], :slots, :]
+        state_ref[here, side * slots : (side + 1) * slots, :] = packed_ref[
+            corner + sides[side], :slots, :
+        ]
     for tile in range(tiles):
         joined = jnp.zeros((8, 128), jnp.float32)
         for part in range(per_tile):
@@ -119,51 +166,25 @@
                 joined = jnp.where(lane_of // slots == part, moved, joined)
         table_ref[tile] = joined
 
-    cell_iota = lax.broadcasted_iota(jnp.int32, (128, 128), 0).astype(jnp.float32).astype(jnp.bfloat16)
-    one = jnp.ones((128, 128), jnp.bfloat16)
-    zero = jnp.zeros((128, 128), jnp.bfloat16)
-    for block in range(slots // 8):
-        rows = slice(8 * block, 8 * block + 8)
-        codes = code_ref[rows, :]
-        live = lane_of.astype(jnp.float32) < own_ref[rows, 3:4]
-        high = jnp.where(live, codes // 128, 64)
-        low = (codes % 128).astype(jnp.float32)
-        for atom in range(8):
-            low_row = jnp.broadcast_to(low[atom : atom + 1], (16, 128)).astype(jnp.bfloat16)
-            low_hot = jnp.where(cell_iota == jnp.concatenate([low_row] * 8, axis=0), one, zero)
-            high_hot = (row_of == high[atom : atom + 1]).astype(jnp.float32).astype(jnp.bfloat16)
-            count_ref[:, 8 * block + atom, :] = lax.dot_general(
-                high_hot, low_hot, (((1,), (1,)), ((), ())), preferred_element_type=jnp.float32
-            )
-    lane_float = lane_of.astype(jnp.float32)
-    for block in range(slots // 8):
-        rows = slice(8 * block, 8 * block + 8)
-        best = jnp.full((8, 128), -1.0, jnp.float32)
-        for tile in range(tiles):
-            times = count_ref[tile, rows, :]
-            split = (times == 3.0) | ((times > 4.0) & (times < 8.0))
-            best = jnp.where(split, lane_float + 128.0 * tile, best)
-        chosen = jnp.max(best, axis=1, keepdims=True)
-        rest = jnp.zeros((8, 128), jnp.float32)
-        for tile in range(tiles):
-            times = count_ref[tile, rows, :]
-            hot = lane_float + 128.0 * tile == chosen
-            part = jnp.where(times > 4.0, times - 4.0, times - 2.0)
-            rest = rest + jnp.where(hot, part, 0.0)
-            count_ref[tile, rows, :] = jnp.where(hot, times - part, times)
-            hot_ref[rows, tile * 128 : tile * 128 + 128] = jnp.where(hot, 1.0, 0.0)
-        total = jnp.sum(rest, axis=1, keepdims=True)
-        spare = lane_of - (128 - slots) == row_of + 8 * block
-        last = count_ref[tiles - 1, rows, :]
-        count_ref[tiles - 1, rows, :] = jnp.where(spare, total, last)
-    hots = hot_ref[...]
-    state_ref[27 * slots :, :] = jnp.dot(
-        hots.astype(jnp.bfloat16), state_ref[...], preferred_element_type=jnp.float32
+    chosen = chosen_ref[...]
+    wide_lane = lax.broadcasted_iota(jnp.int32, (slots, 128), 1).astype(jnp.float32)
+    hots = jnp.concatenate(
+        [jnp.where(wide_lane + 128.0 * tile == chosen, 1.0, 0.0) for tile in range(tiles)], axis=1
     ).astype(jnp.bfloat16)
+    state_ref[here, 27 * slots :, :] = jnp.dot(
+        hots, state_ref[here], preferred_element_type=jnp.float32
+    ).astype(jnp.bfloat16)
+    pieces = []
     spots = jnp.concatenate([table_ref[tile] for tile in range(tiles)], axis=1)
+    for _ in range(3):
+        piece = spots.astype(jnp.bfloat16).astype(jnp.float32)
+        pieces.append(piece)
+        spots = spots - piece
+    pieces = jnp.concatenate(pieces + [jnp.zeros_like(spots)], axis=0).astype(jnp.bfloat16)
     found = lax.dot_general(
-        spots, hots, (((1,), (1,)), ((), ())), precision=highest, preferred_element_type=jnp.float32
-    )
+        pieces, hots, (((1,), (1,)), ((), ())), preferred_element_type=jnp.float32
+    )
+    found = (found[:8] + found[8:16]) + found[16:24]
     table_ref[tiles - 1] = jnp.where(
         lane_of < 128 - slots, table_ref[tiles - 1], jnp.concatenate([found] * per_tile, axis=1)
     )
@@ -174,12 +195,13 @@
     rates = [
         -(cell_size**2) / (sigma_low * sigma_rate**b) ** 2 * math.log2(math.e) for b in range(basis)
     ]
-    for block in range(slots // 8):
+
+    def fill_edges(block):
         rows = slice(8 * block, 8 * block + 8)
-        edge_ref = edge_refs[block % len(edge_refs)]
+        edge_ref = edge_refs[block % 2]
         own = own_ref[rows, :]
         for tile in range(tiles):
-            times = count_ref[tile, rows, :]
+            times = count_ref[0, tile, rows, :]
             spots = table_ref[tile]
             dx = spots[0:1] - own[:, 0:1]
             dy = spots[1:2] - own[:, 1:2]
@@ -210,79 +232,128 @@
                     else:
                         parts = [first, second]
                     at = (degree * basis + 2 * pair) * 8
-                    edge_ref[at : at + 16, tile * 128 : tile * 128 + 128] = jnp.concatenate(
-                        parts, axis=0
-                    ).astype(jnp.bfloat16)
-        summed = jnp.dot(edge_ref[...], state_ref[...], preferred_element_type=jnp.float32)
+                    edge_ref[tile, at : at + 16, :] = jnp.concatenate(parts, axis=0).astype(
+                        jnp.bfloat16
+                    )
+
+    def add_up(block, parity, first_row):
+        edge_ref = edge_refs[block % 2]
+        edges = jnp.concatenate([edge_ref[tile] for tile in range(tiles)], axis=1)
+        summed = jnp.dot(edges, state_ref[parity], preferred_element_type=jnp.float32)
         for degree in range(9):
             total = summed[degree * basis * 8 : degree * basis * 8 + 8] * radial_ref[0:1, :]
             for b in range(1, basis):
                 at = (degree * basis + b) * 8
                 total = total + summed[at : at + 8] * radial_ref[b : b + 1, :]
-            message_ref[degree, rows, :] = total / math.sqrt(NBR)
-    message = message_ref[...].astype(jnp.bfloat16).reshape(9 * slots, 128)
-    scalar = jnp.dot(message[:slots], mix_ref[0], preferred_element_type=jnp.float32)
-    vector = jnp.dot(message[slots : 4 * slots], mix_ref[1], preferred_element_type=jnp.float32)
-    tensor = jnp.dot(message[4 * slots :], mix_ref[2], preferred_element_type=jnp.float32)
-    invariant = scalar
-    squares = tensor * tensor
-    for m in range(5):
-        invariant = invariant + squares[m * slots : (m + 1) * slots]
-    gating = 1.0 / (1.0 + jnp.exp(-invariant))
-    own_state = packed_ref[corner + 21, :slots, :].astype(jnp.float32)
-    next_ref[...] = (own_state + invariant * gating).astype(jnp.bfloat16)
-    weighted = gating * force_ref[...]
-    pushes = vector * jnp.concatenate([weighted] * 3, axis=0)
-    push_ref[0] = lax.dot_general(
-        jnp.ones((8, 128), jnp.float32),
-        pushes,
-        (((1,), (1,)), ((), ())),
-        precision=highest,
-        preferred_element_type=jnp.float32,
-    )
-
-
-def neighbour_sums(packed, nbr_code, own_rows, radial_weight, mix_weight, force_weight):
+            message_ref[degree, pl.ds(first_row, 8), :] = total * (1.0 / math.sqrt(NBR))
+
+    def row_start(block):
+        return pl.multiple_of(octant * slots + 8 * block, 8)
+
+    fill_edges(0)
+    add_up(blocks - 1, before, pl.multiple_of((octant * slots + atoms - 8) % atoms, 8))
+    for block in range(1, blocks):
+        fill_edges(block)
+        add_up(block - 1, here, row_start(block - 1))
+
+    @pl.when(octant == 7)
+    def _():
+        add_up(blocks - 1, here, row_start(blocks - 1))
+        invariant = jnp.dot(
+            message_ref[0].astype(jnp.bfloat16), mix_ref[0], preferred_element_type=jnp.float32
+        )
+        for degree in range(4, 9):
+            tensor = jnp.dot(
+                message_ref[degree].astype(jnp.bfloat16), mix_ref[2], preferred_element_type=jnp.float32
+            )
+            invariant = invariant + tensor * tensor
+        gating = 1.0 / (1.0 + jnp.exp(-invariant))
+        lifted = invariant * gating
+        for own in range(8):
+            at = ((1 + own // 4) * 4 + 1 + own // 2 % 2) * 4 + 1 + own % 2
+            rows = slice(own * slots, (own + 1) * slots)
+            next_ref[rows, :] = (packed_ref[at, :slots, :].astype(jnp.float32) + lifted[rows]).astype(
+                jnp.bfloat16
+            )
+        weighted = gating * force_ref[...]
+        for k in range(3):
+            vector = jnp.dot(
+                message_ref[1 + k].astype(jnp.bfloat16), mix_ref[1], preferred_element_type=jnp.float32
+            )
+            high, low = halves(vector * weighted)
+            pushed = lax.dot_general(
+                jnp.ones((8, 256), jnp.bfloat16),
+                jnp.concatenate([high, low], axis=1).astype(jnp.bfloat16),
+                (((1,), (1,)), ((), ())),
+                preferred_element_type=jnp.float32,
+            )
+            push_ref[k : k + 1, :] = pushed[0:1]
+
+
+def list_counts(nbr_code, own_rows):
     slots = nbr_code.shape[3]
+    tiles = 28 * slots // 128
+    return pl.pallas_call(
+        count_kernel,
+        grid=(8,),
+        in_specs=[
+            pl.BlockSpec((slots, NBR), lambda o: (o, 0)),
+            pl.BlockSpec((slots, 4), lambda o: (o, 0)),
+        ],
+        out_specs=[
+            pl.BlockSpec((1, tiles, slots, 128), lambda o: (o, 0, 0, 0)),
+            pl.BlockSpec((slots, 128), lambda o: (o, 0)),
+        ],
+        out_shape=[
+            jax.ShapeDtypeStruct((8, tiles, slots, 128), jnp.float32),
+            jax.ShapeDtypeStruct((8 * slots, 128), jnp.float32),
+        ],
+        cost_estimate=pl.CostEstimate(
+            flops=2_000_000_000, bytes_accessed=1_300_000, transcendentals=0
+        ),
+    )(nbr_code.reshape(8 * slots, NBR), own_rows)
+
+
+def neighbour_sums(packed, counts, chosen, own_rows, radial_weight, mix_weight, force_weight):
+    tiles, slots = counts.shape[1:3]
     channels = packed.shape[-1]
     basis = radial_weight.shape[0]
     columns = 28 * slots
     sizes = (lax.axis_size("dx"), lax.axis_size("dy"), lax.axis_size("dz"), slots, basis)
-    edges = pltpu.VMEM((9 * basis * 8, columns), jnp.bfloat16)
+    edges = pltpu.VMEM((tiles, 9 * basis * 8, 128), jnp.bfloat16)
     whole = lambda *shape: pl.BlockSpec(shape, lambda o: (0,) * len(shape))
     return pl.pallas_call(
         functools.partial(neighbour_kernel, sizes),
         grid=(8,),
         in_specs=[
             whole(64, slots + 16, channels),
-            pl.BlockSpec((slots, NBR), lambda o: (o, 0)),
+            pl.BlockSpec((1, tiles, slots, 128), lambda o: (o, 0, 0, 0)),
+            pl.BlockSpec((slots, 128), lambda o: (o, 0)),
             pl.BlockSpec((slots, 4), lambda o: (o, 0)),
             whole(basis, channels),
             whole(3, channels, channels),
             whole(1, channels),
         ],
-        out_specs=[
-            pl.BlockSpec((slots, channels), lambda o: (o, 0)),
-            pl.BlockSpec((1, 8, 3 * slots), lambda o: (o, 0, 0)),
-        ],
+        out_specs=[whole(8 * slots, channels), whole(3, 8 * slots)],
         out_shape=[
             jax.ShapeDtypeStruct((8 * slots, channels), jnp.bfloat16),
-            jax.ShapeDtypeStruct((8, 8, 3 * slots), jnp.float32),
+            jax.ShapeDtypeStruct((3, 8 * slots), jnp.float32),
         ],
         scratch_shapes=[
             pltpu.VMEM((64, 8, 128), jnp.float32),
-            pltpu.VMEM((columns, channels), jnp.bfloat16),
-            pltpu.VMEM((columns // 128, 8, 128), jnp.float32),
-            pltpu.VMEM((8, slots, 128), jnp.float32),
-            pltpu.VMEM((slots, columns), jnp.float32),
-            pltpu.VMEM((9, slots, channels), jnp.float32),
+            pltpu.VMEM((2, columns, channels), jnp.bfloat16),
+            pltpu.VMEM((tiles, 8, 128), jnp.float32),
+            pltpu.VMEM((9, 8 * slots, channels), jnp.float32),
             edges,
             edges,
         ],
-        cost_estimate=pl.CostEstimate(flops=4_200_000_000, bytes_accessed=2_000_000, transcendentals=2_000_000),
+        cost_estimate=pl.CostEstimate(
+            flops=8_000_000_000, bytes_accessed=2_000_000, transcendentals=2_000_000
+        ),
     )(
         packed.reshape(64, slots + 16, channels),
-        nbr_code.reshape(8 * slots, NBR),
+        counts,
+        chosen,
         own_rows,
         radial_weight,
         mix_weight,
@@ -310,17 +381,23 @@
 
 
 def turn(table_ref, steps, extent):
+    parts = -(-extent // 128)
+
     def look(index):
-        index = index % extent
-        rows, width = index.shape
+        if extent & (extent - 1):
+            index = index % extent
+        else:
+            index = index & (extent - 1)
+        _, width = index.shape
         found = []
         for start in range(0, width, 128):
             piece = index[:, start : start + 128]
             result = None
-            for part in range(-(-extent // 128)):
+            for part in range(parts):
                 line = jnp.broadcast_to(table_ref[part : part + 1, :], piece.shape)
-                here = jnp.take_along_axis(line, piece % 128, axis=1)
-                result = here if result is None else jnp.where(piece // 128 == part, here, result)
+                lane = piece & 127 if parts > 1 else piece
+                here = jnp.take_along_axis(line, lane, axis=1)
+                result = here if result is None else jnp.where(piece >> 7 == part, here, result)
             found.append(result)
         return jnp.concatenate(found, axis=1) if len(found) > 1 else found[0]
 
@@ -364,11 +441,11 @@
 
 def spread_kernel(sizes, atoms_ref, table_y_ref, table_z_ref, sums_ref):
     length_y, length_z, waves, cells = sizes
-    groups, _, width = atoms_ref.shape
+    groups, _, _ = atoms_ref.shape
     modes_y = wave_start() * waves + lax.broadcasted_iota(jnp.int32, (waves, 128), 0)
     modes_z = 1 + lax.broadcasted_iota(jnp.int32, (KZW, 128), 0)
     anchor = lax.axis_index("dx") * MB
-    total = jnp.zeros(sums_ref.shape, jnp.float32)
+    total = jnp.zeros(sums_ref.shape[1:], jnp.float32)
     for group in range(groups):
         chunk = atoms_ref[group]
         base = chunk[1:4].astype(jnp.int32)
@@ -401,7 +478,8 @@
             preferred_element_type=jnp.float32,
         )
         total = total + (main[:cells] + (main[cells:] + side))
-    sums_ref[...] = total
+    for copy in range(sums_ref.shape[0]):
+        sums_ref[copy] = total
 
 
 def push_kernel(
@@ -511,7 +589,7 @@
     return jnp.asarray(np.cos(2.0 * np.pi * steps / extent).astype(np.float32))
 
 
-def long_range(mesh_base, mesh_frac, charge):
+def long_range(mesh_base, mesh_frac, charge, counts):
     count_x = lax.axis_size("dx")
     count_y = lax.axis_size("dy")
     count_z = lax.axis_size("dz")
@@ -531,18 +609,17 @@
         ],
         axis=0,
     )
-    atoms = lax.all_to_all(
-        jnp.broadcast_to(packed[None], (groups, 7, atom_total)), ("dy", "dz"), 0, 0, tiled=True
-    )
+    packed = jnp.broadcast_to(packed[None], (groups, 7, atom_total))
+    atoms = lax.all_to_all(packed, ("dy", "dz"), 0, 0, tiled=True)
     table_y = cosine_period(length_y)
     table_z = cosine_period(length_z)
     sums = pl.pallas_call(
         functools.partial(spread_kernel, (length_y, length_z, waves, cells)),
-        out_shape=jax.ShapeDtypeStruct((cells, 2 * modes), jnp.float32),
+        out_shape=jax.ShapeDtypeStruct((count_x, cells, 2 * modes), jnp.float32),
     )(atoms, table_y, table_z)
-    received = lax.all_to_all(
-        jnp.broadcast_to(sums[None], (count_x,) + sums.shape), "dx", 0, 0, tiled=True
-    ).reshape(count_x * cells, 2 * modes)
+    received = lax.all_to_all(sums, "dx", 0, 0, tiled=True)
+    received = received.reshape(count_x * cells, 2 * modes)
+    received, counts = lax.optimization_barrier((received, counts))
     places = (np.arange(count_x) * MB)[:, None] + np.arange(cells)[None, :]
     angles = 2.0 * np.pi / length_x * (np.arange(length_x)[:, None] * places.reshape(1, -1) % length_x)
     forward = np.concatenate([np.cos(angles), np.sin(angles)], axis=0).astype(np.float32)
@@ -551,7 +628,7 @@
         out_shape=jax.ShapeDtypeStruct((groups, 3, atom_total), jnp.float32),
     )(atoms, received, jnp.asarray(forward), jnp.asarray(forward.T.copy()), table_y, table_z)
     parts = lax.all_to_all(parts, ("dy", "dz"), 0, 0, tiled=True)
-    return jnp.sum(parts, axis=0)
+    return jnp.sum(parts, axis=0), counts
 
 
 def shards(
@@ -568,16 +645,16 @@
     octants = node_state.shape[3]
     atom_total = 8 * octants
     places = mesh_base.astype(jnp.float32) + mesh_frac
-    packed_halo = spread_halo(pack_atoms(node_state, places), 1)
     own_rows = jnp.transpose(
         jnp.concatenate([places, nbr_count.astype(jnp.float32)[None]], axis=0).reshape(4, atom_total)
     )
-    updated, pushes = neighbour_sums(
-        packed_halo, nbr_code, own_rows, radial_weight, mix_weight, force_weight
+    counts, chosen = list_counts(nbr_code, own_rows)
+    long_force, counts = long_range(mesh_base, mesh_frac, charge, counts)
+    packed_halo = spread_halo(pack_atoms(node_state, places), 1)
+    updated, short_force = neighbour_sums(
+        packed_halo, counts, chosen, own_rows, radial_weight, mix_weight, force_weight
     )
     node_next = updated.reshape(node_state.shape)
-    short_force = jnp.transpose(pushes[:, 0].reshape(8, 3, octants), (1, 0, 2)).reshape(3, atom_total)
-    long_force = long_range(mesh_base, mesh_frac, charge)
     forces = (short_force + long_force).reshape(3, 2, 2, 2, octants)
     return (node_next, forces)
 
@@ -594,6 +671,7 @@
         P(),
         P(),
     )
+
     return jax.shard_map(
         shards,
         mesh=mesh,

time: 88.7 us -> 71.6 us (0.81)
  waiting for transfers between devices: 9.69 us -> 0.02 us
  Pallas kernels: 42.1 us -> 34.7 us
    pallas_call x1, Pallas kernels: 34.2 us -> 19 us  [neighbour_sums(): pl.pallas_call(functools.partial(neighbour_kernel, sizes), grid=(8,), in_...]
    all_to_all x2, waiting for transfers between devices: 9.53 us -> 0.01 us  [the longest x1 0.01 us: long_range(): atoms = lax.all_to_all(packed, ('dy', 'dz'), 0, 0, tiled=True)]
    pallas_call x0 -> x1, Pallas kernels: none -> 8.5 us  [list_counts(): pl.pallas_call(count_kernel, grid=(8,), in_specs=[pl.BlockSpec((slots, NB...]
  transfers between devices with their start and end apart: 8 -> 8, of which waited for: 3 -> 0; matrix products, arithmetic and copies ran while one was open for 6% -> 8% of each run, Pallas kernels for 9% -> 22%
where the time goes in v3:
time: 71.6 us; the launch traced here: 70.5 us
  Pallas kernels  34.7 us (48%)
  starting transfers between devices  16 us (22%)
  blocking collectives  8.07 us (11%)
  other arithmetic  5.66 us (8%)
  local copies, waits for them, and re-layouts  5.28 us (7%)
  between operations  0.76 us (1%)
    pallas_call x1, Pallas kernels, neighbour_sums(): pl.pallas_call(functools.partial(neighbour_kernel, sizes), grid=(8,), in_...  19 us
    pallas_call x1, Pallas kernels, list_counts(): pl.pallas_call(count_kernel, grid=(8,), in_specs=[pl.BlockSpec((slots, NB...  8.5 us
    all_to_all x1, blocking collectives, long_range(): parts = lax.all_to_all(parts, ('dy', 'dz'), 0, 0, tiled=True)  8.07 us
    ppermute x3, starting transfers between devices, spread_halo(): lax.ppermute(tail, axis, [(i, (i + 1) % count) for i in range(count)])  5.25 us
    pallas_call x1, Pallas kernels, long_range(): pl.pallas_call(functools.partial(push_kernel, (length_x, length_y, length...  4.55 us
    all_to_all x1, starting transfers between devices, long_range(): atoms = lax.all_to_all(packed, ('dy', 'dz'), 0, 0, tiled=True)  3.88 us
    ppermute x3, starting transfers between devices, spread_halo(): lax.ppermute(head, axis, [((i + 1) % count, i) for i in range(count)])  3.55 us
    all_to_all x1, starting transfers between devices, long_range(): received = lax.all_to_all(sums, 'dx', 0, 0, tiled=True)  3.34 us
  transfers between devices with their start and end apart: 8, of which 0 were waited for; matrix products, arithmetic and copies ran while one was open for 8% of the time, Pallas kernels for 22%

profile of v3, /device:TPU:0, one launch (start us, length us, event | category | flops | bytes accessed | tf_op | source)
XLA Modules:
  0.0 70.5 jit_solution(11482567646099992795)
XLA Ops:
  0.6 0.7 %reduce-precision_convert_fusion.1 = (bf16[3,2,2,2,32]{4,3,2,1,0:T(2,128)(2,1)S(1)}, f32[3,2,2,2,32]{4,3,2,1,0:T(2,128)S(1)}) fusion(f32[3,2,2,2,32]{4,3,2,1,0:T(2,128)} %param.15, s32[3,2,2,2,32]{4,3,2,1,0:T(2,128)} %param.14), kind=kLoop, calls=%fused_computation.10 | loop fusion | flops 3072 | bytes 10752 | tf_op jit(solution)/shard_map/convert_element_type | solution.py:41
  1.4 0.1 maximum_bitcast_fusion
  1.5 0.8 %fusion = (bf16[1,2,2,48,128]{4,3,2,1,0:T(8,128)(2,1)S(1)}, bf16[1,2,2,48,128]{4,3,2,1,0:T(8,128)(2,1)S(1)}) fusion(bf16[2,2,2,32,128]{4,3,2,1,0:T(8,128)(2,1)} %param.13, bf16[2,2,2,16,128]{4,3,2,1,0:T(8,128)(2,1)S(1)} %pad.4.clone), kind=kLoop, calls=%fused_computation.5 | loop fusion | flops 196608 | bytes 196608 | tf_op jit(solution)/shard_map/concatenate | solution.py:52
  2.3 3.1 %collective-permute-start = (bf16[1,2,2,48,128]{4,3,2,1,0:T(8,128)(2,1)S(1)}, bf16[1,2,2,48,128]{4,3,2,1,0:T(8,128)(2,1)S(1)}, u32[]{:S(2)}, u32[]{:S(2)}) collective-permute-start(bf16[1,2,2,48,128]{4,3,2,1,0:T(8,128)(2,1)S(1)} %get-tuple-element.20), channel_id=1, source_target_pairs={{0,8},{8,16},{16,24},{24,0},{1,9},{9,17},{17,25},{25,1},{2,10},{10... | collective-permute-start | bytes 147464 | tf_op jit(solution)/shard_map/ppermute | solution.py:31
  5.4 2.1 %collective-permute-start.1 = (bf16[1,2,2,48,128]{4,3,2,1,0:T(8,128)(2,1)S(1)}, bf16[1,2,2,48,128]{4,3,2,1,0:T(8,128)(2,1)S(1)}, u32[]{:S(2)}, u32[]{:S(2)}) collective-permute-start(bf16[1,2,2,48,128]{4,3,2,1,0:T(8,128)(2,1)S(1)} %get-tuple-element.21), channel_id=1, source_target_pairs={{8,0},{16,8},{24,16},{0,24},{9,1},{17,9},{25,17},{1,25},{10,2},{18... | collective-permute-start | bytes 147464 | tf_op jit(solution)/shard_map/ppermute | solution.py:32
  7.5 0.8 %reshape.34 = f32[3,256]{1,0:T(4,128)S(1)} reshape(f32[3,2,2,2,32]{4,3,2,1,0:T(2,128)} %param.15) | data formatting | bytes 6144 | tf_op jit(solution)/shard_map/reshape | solution.py:608
  8.3 0.7 %convert_element_type.21 = f32[3,2,2,2,32]{4,3,2,1,0:T(2,128)S(1)} convert(s32[3,2,2,2,32]{4,3,2,1,0:T(2,128)} %param.14) | non-fusion elementwise | flops 768 | bytes 6144 | tf_op jit(solution)/shard_map/convert_element_type | solution.py:647
  9.0 0.8 %reshape.33 = f32[1,256]{1,0:T(1,128)S(1)} reshape(f32[2,2,2,32]{3,2,1,0:T(2,128)} %param.16) | data formatting | bytes 2048 | tf_op jit(solution)/shard_map/reshape | solution.py:606
  9.8 0.1 convert_element_type.25
  9.9 0.6 broadcast_in_dim.4
  10.5 3.9 %all-to-all-start = ((f32[8,7,256]{2,1,0:T(8,128)}), f32[8,7,256]{2,1,0:T(8,128)S(1)}, u32[]{:S(2)}, u32[]{:S(2)}) async-start(f32[8,7,256]{2,1,0:T(8,128)} %broadcast_in_dim.4), calls=%async_computation | async-start | bytes 131072 | tf_op jit(solution)/shard_map/all_to_all | solution.py:613
  14.4 0.1 concatenate.32
  14.5 0.7 convert_element_type.26
  15.2 0.1 concatenate.33
  15.3 0.0 collective-permute-done
  15.3 0.9 %pad_maximum_fusion.2 = bf16[4,2,2,48,128]{4,3,2,1,0:T(8,128)(2,1)S(1)} fusion(bf16[1,2,2,48,128]{4,3,2,1,0:T(8,128)(2,1)S(1)} %collective-permute-done.1, bf16[2,2,2,16,128]{4,3,2,1,0:T(8,128)(2,1)S(1)} %pad.4.clone, bf16[2,2,2,32,128]{4,3,2,1,0:T(8,128)(2,1)} %param.13, bf16[1,2,2,48,128]{4,3,2,1,0:T(8,128)(2,1)S(1)} %collective-permute-done), kind=kLoop, calls=%fused_computation.2 | loop fusion | flops 786432 | bytes 393216 | tf_op jit(solution)/shard_map/concatenate | solution.py:33
  16.2 2.1 %collective-permute-start.2 = (bf16[4,1,2,48,128]{4,3,2,1,0:T(8,128)(2,1)S(1)}, bf16[4,1,2,48,128]{4,3,2,1,0:T(8,128)(2,1)S(1)}, u32[]{:S(2)}, u32[]{:S(2)}) collective-permute-start(bf16[4,1,2,48,128]{4,3,2,1,0:T(8,128)(2,1)S(1)} %get-tuple-element.18), channel_id=1, source_target_pairs={{0,2},{2,4},{4,6},{6,0},{1,3},{3,5},{5,7},{7,1},{8,10},{10,12},{12... | collective-permute-start | bytes 294920 | tf_op jit(solution)/shard_map/ppermute | solution.py:31
  18.2 1.0 %collective-permute-start.3 = (bf16[4,1,2,48,128]{4,3,2,1,0:T(8,128)(2,1)S(1)}, bf16[4,1,2,48,128]{4,3,2,1,0:T(8,128)(2,1)S(1)}, u32[]{:S(2)}, u32[]{:S(2)}) collective-permute-start(bf16[4,1,2,48,128]{4,3,2,1,0:T(8,128)(2,1)S(1)} %get-tuple-element.19), channel_id=1, source_target_pairs={{2,0},{4,2},{6,4},{0,6},{3,1},{5,3},{7,5},{1,7},{10,8},{12,10},{14... | collective-permute-start | bytes 294920 | tf_op jit(solution)/shard_map/ppermute | solution.py:32
  19.2 0.8 %copy.21 = f32[4,256]{0,1:T(8,128)} copy(f32[4,256]{1,0:T(4,128)S(1)} %pad_maximum_fusion.5) | data formatting | bytes 8192 | tf_op jit(solution)/shard_map/concatenate | solution.py:649
  20.0 0.6 copy-done.2
  20.6 2.7 %shard_map.140 = f32[4,40,256]{2,1,0:T(8,128)} custom-call(f32[8,7,256]{2,1,0:T(8,128)} %copy-done.2, f32[1,128]{1,0:T(1,128)} %constant.13.clone.table_y_ref, f32[1,128]{1,0:T(1,128)} %constant.14.clone.table_z_ref), custom_call_target="tpu_custom_call" | custom-call | tf_op jit(solution)/shard_map/pallas_call | solution.py:616
  23.3 3.3 %all-to-all-start.1 = ((f32[4,40,256]{2,1,0:T(8,128)}), f32[4,40,256]{2,1,0:T(8,128)S(1)}, u32[]{:S(2)}, u32[]{:S(2)}) async-start(f32[4,40,256]{2,1,0:T(8,128)} %shard_map.140), calls=%async_computation.1 | async-start | bytes 327680 | tf_op jit(solution)/shard_map/all_to_all | solution.py:620
  26.8 0.1 collective-permute-start.4
  26.9 0.5 collective-permute-start.5
  27.4 8.5 %shard_map.141 = (f32[8,7,32,128]{3,2,1,0:T(8,128)}, f32[256,128]{1,0:T(8,128)}) custom-call(s32[256,128]{1,0:T(8,128)} %bitcast.12, f32[256,4]{1,0:T(8,128)} %bitcast.10), custom_call_target="tpu_custom_call" | custom-call | flops 2000000000 | bytes 1300000 | tf_op jit(solution)/shard_map/pallas_call | solution.py:296
  35.9 0.7 copy-done.1
  36.5 4.6 %shard_map.143 = f32[8,3,256]{2,1,0:T(4,128)} custom-call(f32[8,7,256]{2,1,0:T(8,128)} %copy-done.2, f32[160,256]{1,0:T(8,128)} %bitcast.9, f32[256,160]{1,0:T(8,128)} %constant.15.clone.forward_ref, f32[160,256]{1,0:T(8,128)} %constant.16.clone.back_ref, f32[1,128]{1,0:T(1,128)} %constant.13.clone.table_y_ref, f32[1,128]{1,0:T(1,128)} %constant.14.clone.table_z_ref), custom_call_target="tpu_custom_call" | custom-call | tf_op jit(solution)/shard_map/pallas_call | solution.py:626
  41.1 8.1 %all_to_all.15 = f32[8,3,256]{2,1,0:T(4,128)S(1)} all-to-all(f32[8,3,256]{2,1,0:T(4,128)} %shard_map.143), channel_id=1, replica_groups=mesh['dx'=4,'dy'=4,'dz'=2] {'dy','dz'}, dimensions={0} | all-to-all | bytes 49152 | tf_op jit(solution)/shard_map/all_to_all | solution.py:630
  49.2 1.0 %pad_maximum_fusion = bf16[4,4,4,48,128]{4,3,2,1,0:T(8,128)(2,1)} fusion(bf16[4,4,1,48,128]{4,3,2,1,0:T(8,128)(2,1)S(1)} %collective-permute-done.5, bf16[4,1,2,48,128]{4,3,2,1,0:T(8,128)(2,1)S(1)} %collective-permute-done.3, bf16[1,2,2,48,128]{4,3,2,1,0:T(8,128)(2,1)S(1)} %collective-permute-done.1, bf16[2,2,2,16,128]{4,3,2,1,0:T(8,128)(2,1)S(1)} %pad.4.clone, ...), kind=kLoop, calls=%fused_computation | loop fusion | flops 6291456 | bytes 1572864 | tf_op jit(solution)/shard_map/concatenate | solution.py:33
  50.2 19.0 %shard_map.142 = (bf16[256,128]{1,0:T(8,128)(2,1)}, f32[3,256]{1,0:T(4,128)}) custom-call(bf16[64,48,128]{2,1,0:T(8,128)(2,1)} %bitcast.8, f32[8,7,32,128]{3,2,1,0:T(8,128)} %get-tuple-element.9.count_ref, f32[256,128]{1,0:T(8,128)} %get-tuple-element.10.chosen_ref, f32[256,4]{1,0:T(8,128)} %bitcast.11, f32[8,128]{1,0:T(8,128)} %radial_ref.1, ...), custom_call_target="tpu_custom_call" | custom-call | flops 8000000000 | bytes 2000000 | tf_op jit(solution)/shard_map/pallas_call | solution.py:325
  69.2 0.7 add.9
  69.9 0.7 reshape.38
  (20 shorter events, 0.2 us)
Async XLA Ops:
  2.3 24.4 %copy-start = (bf16[2,2,2,32,128]{4,3,2,1,0:T(8,128)(2,1)S(1)}, bf16[2,2,2,32,128]{4,3,2,1,0:T(8,128)(2,1)}, u32[]{:S(2)}) copy-start(bf16[2,2,2,32,128]{4,3,2,1,0:T(8,128)(2,1)} %param.13) | copy-start | bytes 196612
  2.3 13.0 %collective-permute-start = (bf16[1,2,2,48,128]{4,3,2,1,0:T(8,128)(2,1)S(1)}, bf16[1,2,2,48,128]{4,3,2,1,0:T(8,128)(2,1)S(1)}, u32[]{:S(2)}, u32[]{:S(2)}) collective-permute-start(bf16[1,2,2,48,128]{4,3,2,1,0:T(8,128)(2,1)S(1)} %get-tuple-element.20), channel_id=1, source_target_pairs={{0,8},{8,16},{16,24},{24,0},{1,9},{9,17},{17,25},{25,1},{2,10},{10... | collective-permute-start | bytes 147464 | tf_op jit(solution)/shard_map/ppermute | solution.py:31
  5.4 9.9 %collective-permute-start.1 = (bf16[1,2,2,48,128]{4,3,2,1,0:T(8,128)(2,1)S(1)}, bf16[1,2,2,48,128]{4,3,2,1,0:T(8,128)(2,1)S(1)}, u32[]{:S(2)}, u32[]{:S(2)}) collective-permute-start(bf16[1,2,2,48,128]{4,3,2,1,0:T(8,128)(2,1)S(1)} %get-tuple-element.21), channel_id=1, source_target_pairs={{8,0},{16,8},{24,16},{0,24},{9,1},{17,9},{25,17},{1,25},{10,2},{18... | collective-permute-start | bytes 147464 | tf_op jit(solution)/shard_map/ppermute | solution.py:32
  10.5 9.5 %all-to-all-start = ((f32[8,7,256]{2,1,0:T(8,128)}), f32[8,7,256]{2,1,0:T(8,128)S(1)}, u32[]{:S(2)}, u32[]{:S(2)}) async-start(f32[8,7,256]{2,1,0:T(8,128)} %broadcast_in_dim.4), calls=%async_computation | async-start | bytes 131072 | tf_op jit(solution)/shard_map/all_to_all | solution.py:613
  16.2 10.5 %collective-permute-start.2 = (bf16[4,1,2,48,128]{4,3,2,1,0:T(8,128)(2,1)S(1)}, bf16[4,1,2,48,128]{4,3,2,1,0:T(8,128)(2,1)S(1)}, u32[]{:S(2)}, u32[]{:S(2)}) collective-permute-start(bf16[4,1,2,48,128]{4,3,2,1,0:T(8,128)(2,1)S(1)} %get-tuple-element.18), channel_id=1, source_target_pairs={{0,2},{2,4},{4,6},{6,0},{1,3},{3,5},{5,7},{7,1},{8,10},{10,12},{12... | collective-permute-start | bytes 294920 | tf_op jit(solution)/shard_map/ppermute | solution.py:31
  18.2 8.5 %collective-permute-start.3 = (bf16[4,1,2,48,128]{4,3,2,1,0:T(8,128)(2,1)S(1)}, bf16[4,1,2,48,128]{4,3,2,1,0:T(8,128)(2,1)S(1)}, u32[]{:S(2)}, u32[]{:S(2)}) collective-permute-start(bf16[4,1,2,48,128]{4,3,2,1,0:T(8,128)(2,1)S(1)} %get-tuple-element.19), channel_id=1, source_target_pairs={{2,0},{4,2},{6,4},{0,6},{3,1},{5,3},{7,5},{1,7},{10,8},{12,10},{14... | collective-permute-start | bytes 294920 | tf_op jit(solution)/shard_map/ppermute | solution.py:32
  20.0 0.6 copy-start.2
  23.3 12.5 %all-to-all-start.1 = ((f32[4,40,256]{2,1,0:T(8,128)}), f32[4,40,256]{2,1,0:T(8,128)S(1)}, u32[]{:S(2)}, u32[]{:S(2)}) async-start(f32[4,40,256]{2,1,0:T(8,128)} %shard_map.140), calls=%async_computation.1 | async-start | bytes 327680 | tf_op jit(solution)/shard_map/all_to_all | solution.py:620
  26.8 22.4 %collective-permute-start.4 = (bf16[4,4,1,48,128]{4,3,2,1,0:T(8,128)(2,1)S(1)}, bf16[4,4,1,48,128]{4,3,2,1,0:T(8,128)(2,1)S(1)}, u32[]{:S(2)}, u32[]{:S(2)}) collective-permute-start(bf16[4,4,1,48,128]{4,3,2,1,0:T(8,128)(2,1)S(1)} %get-tuple-element.16), channel_id=1, source_target_pairs={{0,1},{1,0},{2,3},{3,2},{4,5},{5,4},{6,7},{7,6},{8,9},{9,8},{10,11... | collective-permute-start | bytes 589832 | tf_op jit(solution)/shard_map/ppermute | solution.py:31
  26.9 22.3 %collective-permute-start.5 = (bf16[4,4,1,48,128]{4,3,2,1,0:T(8,128)(2,1)S(1)}, bf16[4,4,1,48,128]{4,3,2,1,0:T(8,128)(2,1)S(1)}, u32[]{:S(2)}, u32[]{:S(2)}) collective-permute-start(bf16[4,4,1,48,128]{4,3,2,1,0:T(8,128)(2,1)S(1)} %get-tuple-element.17), channel_id=1, source_target_pairs={{1,0},{0,1},{3,2},{2,3},{5,4},{4,5},{7,6},{6,7},{9,8},{8,9},{11,10... | collective-permute-start | bytes 589832 | tf_op jit(solution)/shard_map/ppermute | solution.py:32
  35.9 0.7 copy-start.1

commit v4 on v3

--- a/solution.py
+++ b/solution.py
@@ -3,7 +3,6 @@
 
 import jax
 import jax.numpy as jnp
-import numpy as np
 from jax import lax
 from jax.experimental import pallas as pl
 from jax.experimental.pallas import tpu as pltpu
@@ -23,50 +22,115 @@
 highest = lax.Precision.HIGHEST
 
 
-def spread_halo(block, width):
-    for axis, dim in (("dx", 0), ("dy", 1), ("dz", 2)):
-        count = lax.axis_size(axis)
-        head = lax.slice_in_dim(block, 0, width, axis=dim)
-        tail = lax.slice_in_dim(block, block.shape[dim] - width, block.shape[dim], axis=dim)
-        below = lax.ppermute(tail, axis, [(i, (i + 1) % count) for i in range(count)])
-        above = lax.ppermute(head, axis, [((i + 1) % count, i) for i in range(count)])
+def neighbours_along(block, axis, dim):
+    count = lax.axis_size(axis)
+    if count == 2:
+        other = lax.ppermute(block, axis, [(0, 1), (1, 0)])
+        return other, other
+    head = lax.slice_in_dim(block, 0, 1, axis=dim)
+    tail = lax.slice_in_dim(block, block.shape[dim] - 1, block.shape[dim], axis=dim)
+    below = lax.ppermute(tail, axis, [(i, (i + 1) % count) for i in range(count)])
+    above = lax.ppermute(head, axis, [((i + 1) % count, i) for i in range(count)])
+    return below, above
+
+
+def spread_halo(block):
+    for axis, dim in (("dx", 0), ("dy", 1)):
+        below, above = neighbours_along(block, axis, dim)
+        below = lax.slice_in_dim(below, below.shape[dim] - 1, below.shape[dim], axis=dim)
+        above = lax.slice_in_dim(above, 0, 1, axis=dim)
         block = jnp.concatenate([below, block, above], axis=dim)
-    return block
-
-
-def exact_pieces(values):
-    pieces = []
-    for _ in range(3):
-        piece = lax.reduce_precision(values, 8, 7)
-        pieces.append(piece.astype(jnp.bfloat16))
-        values = values - piece
-    return pieces
-
-
-def pack_atoms(node_state, places):
-    slots = node_state.shape[3]
-    channels = node_state.shape[4]
-    cells = jnp.concatenate(exact_pieces(places), axis=4)
-    cells = jnp.transpose(cells, (1, 2, 3, 0, 4))
-    cells = jnp.pad(cells, ((0, 0),) * 3 + ((0, 13), (0, channels - 3 * slots)))
-    return jnp.concatenate([node_state, cells], axis=3)
-
-
-def count_kernel(code_ref, own_ref, count_ref, chosen_ref):
-    slots = code_ref.shape[0]
-    tiles = count_ref.shape[1]
+    return (block,) + neighbours_along(block, "dz", 2)
+
+
+def pack_kernel(*refs):
+    sources, held, fetched = refs[:7], refs[11:18], refs[18]
+    atoms_ref, block_ref, own_ref, channel_ref = refs[7:11]
+    copies = [
+        pltpu.make_async_copy(source, here, fetched.at[at])
+        for at, (source, here) in enumerate(zip(sources, held))
+    ]
+    for copy in copies:
+        copy.start()
+    for copy in copies:
+        copy.wait()
+    state_ref, base_ref, frac_ref, charge_ref, live_ref, radial_ref, force_ref = held
+    channel_ref[...] = jnp.concatenate([radial_ref[...], force_ref[...]], axis=0)
+    slots = state_ref.shape[3]
+    sevens = []
+    fours = []
+    for octant in range(8):
+        at = (octant // 4, octant // 2 % 2, slice(octant % 2, octant % 2 + 1))
+        charge = charge_ref[at]
+        base = jnp.concatenate([base_ref[(d,) + at] for d in range(3)], axis=0).astype(jnp.float32)
+        frac = jnp.concatenate([frac_ref[(d,) + at] for d in range(3)], axis=0)
+        places = base + frac
+        sevens.append(jnp.concatenate([charge, base, frac], axis=0))
+        fours.append(jnp.concatenate([places, live_ref[at].astype(jnp.float32)], axis=0))
+        pieces = []
+        rest = places
+        for _ in range(3):
+            piece = rest.astype(jnp.bfloat16).astype(jnp.float32)
+            pieces.append(piece)
+            rest = rest - piece
+        pieces.append(jnp.zeros((3, 128 - 3 * slots), jnp.float32))
+        cells = jnp.concatenate(pieces, axis=1)
+        cells = jnp.concatenate([cells, jnp.zeros((13, 128), jnp.float32)], axis=0)
+        block_ref[octant, slots:, :] = cells.astype(jnp.bfloat16)
+        block_ref[octant, :slots, :] = state_ref[octant // 4, octant // 2 % 2, octant % 2]
+    seven = jnp.concatenate(sevens, axis=1)
+    for copy in range(atoms_ref.shape[0]):
+        atoms_ref[copy] = seven
+    four = jnp.concatenate(fours, axis=1)
+    four = jnp.concatenate([four, jnp.zeros_like(four)], axis=0)
+    own_ref[...] = jnp.transpose(four)
+
+
+def pack_atoms(node_state, mesh_base, mesh_frac, charge, nbr_count, radial_weight, force_weight):
+    slots, channels = node_state.shape[3:]
+    groups = lax.axis_size("dy") * lax.axis_size("dz")
+    arrays = (
+        node_state,
+        mesh_base,
+        mesh_frac,
+        charge,
+        nbr_count,
+        radial_weight,
+        force_weight[None],
+    )
+    atoms, block, own_rows, channel_rows = pl.pallas_call(
+        pack_kernel,
+        out_shape=[
+            jax.ShapeDtypeStruct((groups, 7, 8 * slots), jnp.float32),
+            jax.ShapeDtypeStruct((8, slots + 16, channels), jnp.bfloat16),
+            jax.ShapeDtypeStruct((8 * slots, 8), jnp.float32),
+            jax.ShapeDtypeStruct((radial_weight.shape[0] + 1, channels), jnp.float32),
+        ],
+        in_specs=[pl.BlockSpec(memory_space=pltpu.HBM)] * len(arrays),
+        scratch_shapes=[pltpu.VMEM(array.shape, array.dtype) for array in arrays]
+        + [pltpu.SemaphoreType.DMA((len(arrays),))],
+        compiler_params=pltpu.CompilerParams(vmem_limit_bytes=4 << 20),
+    )(*[pltpu.with_memory_space_constraint(array, pltpu.HBM) for array in arrays])
+    block = block.reshape(2, 2, 2, slots + 16, channels)
+    return atoms, block, own_rows, channel_rows
+
+
+def count_kernel(code_ref, own_ref, *refs):
+    count_ref, chosen_ref = refs[-2:]
+    octants, tiles, slots, _ = count_ref.shape
     row_of = lax.broadcasted_iota(jnp.int32, (8, 128), 0)
     lane_of = lax.broadcasted_iota(jnp.int32, (8, 128), 1)
     cell_iota = lax.broadcasted_iota(jnp.int32, (128, 128), 0).astype(jnp.float32).astype(jnp.bfloat16)
     one = jnp.ones((128, 128), jnp.bfloat16)
     zero = jnp.zeros((128, 128), jnp.bfloat16)
     lane_float = lane_of.astype(jnp.float32)
-    for block in range(slots // 8):
-        rows = slice(8 * block, 8 * block + 8)
+    pieces = [(octant, block) for octant in range(octants) for block in range(slots // 8)]
+    for octant, block in pieces:
+        rows = slice(octant * slots + 8 * block, octant * slots + 8 * block + 8)
         codes = code_ref[rows, :]
         live = lane_float < own_ref[rows, 3:4]
-        high = jnp.where(live, codes // 128, 64)
-        low = (codes % 128).astype(jnp.float32)
+        high = jnp.where(live, codes >> 7, 64)
+        low = (codes & 127).astype(jnp.float32)
         for atom in range(8):
             low_row = jnp.broadcast_to(low[atom : atom + 1], (16, 128)).astype(jnp.bfloat16)
             low_hot = jnp.where(cell_iota == jnp.concatenate([low_row] * 8, axis=0), one, zero)
@@ -74,40 +138,43 @@
             counted = lax.dot_general(
                 high_hot, low_hot, (((1,), (1,)), ((), ())), preferred_element_type=jnp.float32
             )
-            count_ref[0, :, 8 * block + atom, :] = counted[:tiles]
-    for block in range(slots // 8):
-        rows = slice(8 * block, 8 * block + 8)
+            count_ref[octant, :, 8 * block + atom, :] = counted[:tiles]
+    for octant, block in pieces:
+        own = slice(8 * block, 8 * block + 8)
         best = jnp.full((8, 128), -1.0, jnp.float32)
         for tile in range(tiles):
-            times = count_ref[0, tile, rows, :]
+            times = count_ref[octant, tile, own, :]
             split = (times == 3.0) | ((times > 4.0) & (times < 8.0))
             best = jnp.where(split, lane_float + 128.0 * tile, best)
         chosen = jnp.max(best, axis=1, keepdims=True)
+        rows = slice(octant * slots + 8 * block, octant * slots + 8 * block + 8)
         chosen_ref[rows, :] = jnp.broadcast_to(chosen, (8, 128))
         rest = jnp.zeros((8, 128), jnp.float32)
         for tile in range(tiles):
-            times = count_ref[0, tile, rows, :]
+            times = count_ref[octant, tile, own, :]
             hot = lane_float + 128.0 * tile == chosen
             part = jnp.where(times > 4.0, times - 4.0, times - 2.0)
             rest = rest + jnp.where(hot, part, 0.0)
-            count_ref[0, tile, rows, :] = jnp.where(hot, times - part, times)
+            count_ref[octant, tile, own, :] = jnp.where(hot, times - part, times)
         total = jnp.sum(rest, axis=1, keepdims=True)
         spare = lane_of - (128 - slots) == row_of + 8 * block
-        last = count_ref[0, tiles - 1, rows, :]
-        count_ref[0, tiles - 1, rows, :] = jnp.where(spare, total, last)
+        last = count_ref[octant, tiles - 1, own, :]
+        count_ref[octant, tiles - 1, own, :] = jnp.where(spare, total, last)
 
 
 def neighbour_kernel(
     sizes,
-    packed_ref,
+    block_ref,
+    below_ref,
+    above_ref,
     count_ref,
     chosen_ref,
     own_ref,
     radial_ref,
     mix_ref,
-    force_ref,
     next_ref,
     push_ref,
+    halo_ref,
     place_ref,
     state_ref,
     table_ref,
@@ -141,20 +208,28 @@
             below = jnp.where(reach < 0, -2 * count * half, 0)
             return jnp.where(reach >= 2 * count, 2 * count * half, below).astype(jnp.float32)
 
-        @pl.loop(0, 64, unroll=8)
-        def _(cell):
-            rows = packed_ref[cell, slots : slots + 16, :].astype(jnp.float32)[:8]
-            total = (rows + pltpu.roll(rows, 128 - slots, 1)) + pltpu.roll(rows, 128 - 2 * slots, 1)
-            shift_x = unwrapped(cell // 16, starts[0], count_x)
-            shift_y = unwrapped(cell // 4 % 4, starts[1], count_y)
-            shift_z = unwrapped(cell % 4, starts[2], count_z)
-            shift = jnp.where(row_of == 0, shift_x, jnp.where(row_of == 1, shift_y, shift_z))
-            place_ref[cell] = total + shift
+        @pl.loop(0, 16, unroll=2)
+        def _(column):
+            shift_x = unwrapped(column // 4, starts[0], count_x)
+            shift_y = unwrapped(column % 4, starts[1], count_y)
+            for level in range(4):
+                if level == 0:
+                    source = below_ref.at[column, below_ref.shape[1] - 1]
+                elif level == 3:
+                    source = above_ref.at[column, 0]
+                else:
+                    source = block_ref.at[column, level - 1]
+                cell = column * 4 + level
+                halo_ref[cell] = source[:slots, :]
+                rows = source[slots:, :].astype(jnp.float32)[:8]
+                total = rows + pltpu.roll(rows, 128 - slots, 1)
+                total = total + pltpu.roll(rows, 128 - 2 * slots, 1)
+                shift_z = unwrapped(level, starts[2], count_z)
+                shift = jnp.where(row_of == 0, shift_x, jnp.where(row_of == 1, shift_y, shift_z))
+                place_ref[cell] = total + shift
 
     for side in range(27):
-        state_ref[here, side * slots : (side + 1) * slots, :] = packed_ref[
-            corner + sides[side], :slots, :
-        ]
+        state_ref[here, side * slots : (side + 1) * slots, :] = halo_ref[corner + sides[side]]
     for tile in range(tiles):
         joined = jnp.zeros((8, 128), jnp.float32)
         for part in range(per_tile):
@@ -272,10 +347,8 @@
         for own in range(8):
             at = ((1 + own // 4) * 4 + 1 + own // 2 % 2) * 4 + 1 + own % 2
             rows = slice(own * slots, (own + 1) * slots)
-            next_ref[rows, :] = (packed_ref[at, :slots, :].astype(jnp.float32) + lifted[rows]).astype(
-                jnp.bfloat16
-            )
-        weighted = gating * force_ref[...]
+            next_ref[rows, :] = (halo_ref[at].astype(jnp.float32) + lifted[rows]).astype(jnp.bfloat16)
+        weighted = gating * radial_ref[basis : basis + 1, :]
         for k in range(3):
             vector = jnp.dot(
                 message_ref[1 + k].astype(jnp.bfloat16), mix_ref[1], preferred_element_type=jnp.float32
@@ -290,34 +363,40 @@
             push_ref[k : k + 1, :] = pushed[0:1]
 
 
-def list_counts(nbr_code, own_rows):
+def list_counts(nbr_code, own_rows, first, earlier):
     slots = nbr_code.shape[3]
     tiles = 28 * slots // 128
+    together = 2
+    start = first // together
     return pl.pallas_call(
         count_kernel,
-        grid=(8,),
+        grid=(4 // together,),
         in_specs=[
-            pl.BlockSpec((slots, NBR), lambda o: (o, 0)),
-            pl.BlockSpec((slots, 4), lambda o: (o, 0)),
-        ],
+            pl.BlockSpec((together * slots, NBR), lambda o: (o + start, 0)),
+            pl.BlockSpec((together * slots, 8), lambda o: (o + start, 0)),
+        ]
+        + [pl.BlockSpec(memory_space=pl.ANY)] * len(earlier),
         out_specs=[
-            pl.BlockSpec((1, tiles, slots, 128), lambda o: (o, 0, 0, 0)),
-            pl.BlockSpec((slots, 128), lambda o: (o, 0)),
+            pl.BlockSpec((together, tiles, slots, 128), lambda o: (o + start, 0, 0, 0)),
+            pl.BlockSpec((together * slots, 128), lambda o: (o + start, 0)),
         ],
         out_shape=[
             jax.ShapeDtypeStruct((8, tiles, slots, 128), jnp.float32),
             jax.ShapeDtypeStruct((8 * slots, 128), jnp.float32),
         ],
+        input_output_aliases={2: 0, 3: 1} if earlier else {},
         cost_estimate=pl.CostEstimate(
-            flops=2_000_000_000, bytes_accessed=1_300_000, transcendentals=0
+            flops=1_000_000_000, bytes_accessed=700_000, transcendentals=0
         ),
-    )(nbr_code.reshape(8 * slots, NBR), own_rows)
-
-
-def neighbour_sums(packed, counts, chosen, own_rows, radial_weight, mix_weight, force_weight):
+        compiler_params=pltpu.CompilerParams(vmem_limit_bytes=6 << 20),
+    )(nbr_code.reshape(8 * slots, NBR), own_rows, *earlier)
+
+
+def neighbour_sums(packed, counts, chosen, own_rows, channel_rows, mix_weight):
     tiles, slots = counts.shape[1:3]
-    channels = packed.shape[-1]
-    basis = radial_weight.shape[0]
+    channels = packed[0].shape[-1]
+    packed = [block.reshape((16, -1) + block.shape[3:]) for block in packed]
+    basis = channel_rows.shape[0] - 1
     columns = 28 * slots
     sizes = (lax.axis_size("dx"), lax.axis_size("dy"), lax.axis_size("dz"), slots, basis)
     edges = pltpu.VMEM((tiles, 9 * basis * 8, 128), jnp.bfloat16)
@@ -326,13 +405,12 @@
         functools.partial(neighbour_kernel, sizes),
         grid=(8,),
         in_specs=[
-            whole(64, slots + 16, channels),
+            *[whole(*block.shape) for block in packed],
             pl.BlockSpec((1, tiles, slots, 128), lambda o: (o, 0, 0, 0)),
             pl.BlockSpec((slots, 128), lambda o: (o, 0)),
-            pl.BlockSpec((slots, 4), lambda o: (o, 0)),
-            whole(basis, channels),
+            pl.BlockSpec((slots, 8), lambda o: (o, 0)),
+            whole(basis + 1, channels),
             whole(3, channels, channels),
-            whole(1, channels),
         ],
         out_specs=[whole(8 * slots, channels), whole(3, 8 * slots)],
         out_shape=[
@@ -340,6 +418,7 @@
             jax.ShapeDtypeStruct((3, 8 * slots), jnp.float32),
         ],
         scratch_shapes=[
+            pltpu.VMEM((64, slots, channels), jnp.bfloat16),
             pltpu.VMEM((64, 8, 128), jnp.float32),
             pltpu.VMEM((2, columns, channels), jnp.bfloat16),
             pltpu.VMEM((tiles, 8, 128), jnp.float32),
@@ -347,17 +426,17 @@
             edges,
             edges,
         ],
+        compiler_params=pltpu.CompilerParams(vmem_limit_bytes=16 << 20),
         cost_estimate=pl.CostEstimate(
             flops=8_000_000_000, bytes_accessed=2_000_000, transcendentals=2_000_000
         ),
     )(
-        packed.reshape(64, slots + 16, channels),
+        *packed,
         counts,
         chosen,
         own_rows,
-        radial_weight,
+        channel_rows,
         mix_weight,
-        force_weight[None],
     )
 
 
@@ -380,23 +459,28 @@
     return weights, slopes
 
 
-def turn(table_ref, steps, extent):
+def turn(steps, extent):
+    _, width = steps.shape
     parts = -(-extent // 128)
+    lane = lax.broadcasted_iota(jnp.int32, (8, 128), 1)
+    lines = [
+        jnp.cos((lane + 128 * part).astype(jnp.float32) * (2.0 * math.pi / extent))[:1]
+        for part in range(parts)
+    ]
 
     def look(index):
         if extent & (extent - 1):
             index = index % extent
         else:
             index = index & (extent - 1)
-        _, width = index.shape
         found = []
         for start in range(0, width, 128):
             piece = index[:, start : start + 128]
             result = None
             for part in range(parts):
-                line = jnp.broadcast_to(table_ref[part : part + 1, :], piece.shape)
-                lane = piece & 127 if parts > 1 else piece
-                here = jnp.take_along_axis(line, lane, axis=1)
+                line = jnp.broadcast_to(lines[part], piece.shape)
+                at = piece & 127 if parts > 1 else piece
+                here = jnp.take_along_axis(line, at, axis=1)
                 result = here if result is None else jnp.where(piece >> 7 == part, here, result)
             found.append(result)
         return jnp.concatenate(found, axis=1) if len(found) > 1 else found[0]
@@ -404,12 +488,12 @@
     return look(steps), look(steps + 3 * extent // 4)
 
 
-def wave_factors(table_ref, modes, base_row, extent):
+def wave_factors(modes, base_row, extent):
     rows = modes.shape[0]
     width = base_row.shape[1]
     wide = jnp.broadcast_to(modes[:, :1], (rows, width))
-    first = turn(table_ref, wide * base_row, extent)
-    steps = [turn(table_ref, modes * t, extent) for t in (1, 2, 3)]
+    first = turn(wide * base_row, extent)
+    steps = [turn(modes * t, extent) for t in (1, 2, 3)]
     steps = [tuple(jnp.concatenate([p] * (width // 128), axis=1) for p in pair) for pair in steps]
     return first, steps
 
@@ -439,7 +523,7 @@
     return lax.axis_index("dy") * lax.axis_size("dz") + lax.axis_index("dz")
 
 
-def spread_kernel(sizes, atoms_ref, table_y_ref, table_z_ref, sums_ref):
+def spread_kernel(sizes, atoms_ref, sums_ref):
     length_y, length_z, waves, cells = sizes
     groups, _, _ = atoms_ref.shape
     modes_y = wave_start() * waves + lax.broadcasted_iota(jnp.int32, (waves, 128), 0)
@@ -451,8 +535,8 @@
         base = chunk[1:4].astype(jnp.int32)
         weights, _ = spline_rows(chunk[4:7])
         row = lambda d: [w[d : d + 1] for w in weights]
-        y_re, y_im = wave_of(wave_factors(table_y_ref, modes_y, base[1:2], length_y), row(1))
-        z_re, z_im = wave_of(wave_factors(table_z_ref, modes_z, base[2:3], length_z), row(2))
+        y_re, y_im = wave_of(wave_factors(modes_y, base[1:2], length_y), row(1))
+        z_re, z_im = wave_of(wave_factors(modes_z, base[2:3], length_z), row(2))
         mixed_re = []
         mixed_im = []
         for k in range(waves):
@@ -482,9 +566,7 @@
         sums_ref[copy] = total
 
 
-def push_kernel(
-    sizes, atoms_ref, sums_ref, forward_ref, back_ref, table_y_ref, table_z_ref, force_ref
-):
+def push_kernel(sizes, atoms_ref, sums_ref, force_ref):
     length_x, length_y, length_z, waves, cells = sizes
     groups, _, width = atoms_ref.shape
     modes = waves * KZW
@@ -493,8 +575,14 @@
     modes_z = 1 + lax.broadcasted_iota(jnp.int32, (KZW, 128), 0)
     anchor = lax.axis_index("dx") * MB
 
+    count_x = length_x // MB
+    lined = -(-count_x * cells // 128) * 128
+    place = lax.broadcasted_iota(jnp.int32, (1, lined), 1)
+    place = place + (MB - cells) * (place // cells)
+    mode = lax.broadcasted_iota(jnp.int32, (length_x, lined), 0)
+    forward = jnp.concatenate(turn(mode * place, length_x), axis=0)[:, : count_x * cells]
     turned = jnp.dot(
-        forward_ref[...], sums_ref[...], precision=highest, preferred_element_type=jnp.float32
+        forward, sums_ref[...], precision=highest, preferred_element_type=jnp.float32
     )
     cosine = turned[:length_x]
     sine = turned[length_x:]
@@ -525,8 +613,9 @@
         ],
         axis=1,
     )
-    lines = back_ref[pl.ds(pl.multiple_of(lax.axis_index("dx") * cells, 8), cells), :]
-    lines = jnp.concatenate([lines[:, :length_x], lines[:, length_x:]], axis=0)
+    cell = anchor + lax.broadcasted_iota(jnp.int32, (cells, length_x), 0)
+    mode = lax.broadcasted_iota(jnp.int32, (cells, length_x), 1)
+    lines = jnp.concatenate(turn(cell * mode, length_x), axis=0)
     turned = jnp.dot(lines, scaled, precision=highest, preferred_element_type=jnp.float32)
     cosine = turned[:cells]
     sine = turned[cells:]
@@ -544,8 +633,8 @@
         weights, slopes = spline_rows(chunk[4:7])
         row = lambda d: [w[d : d + 1] for w in weights]
         tilt = lambda d: [w[d : d + 1] for w in slopes]
-        factors_y = wave_factors(table_y_ref, modes_y, base[1:2], length_y)
-        factors_z = wave_factors(table_z_ref, modes_z, base[2:3], length_z)
+        factors_y = wave_factors(modes_y, base[1:2], length_y)
+        factors_z = wave_factors(modes_z, base[2:3], length_z)
         y_re, y_im = wave_of(factors_y, row(1))
         dy_re, dy_im = wave_of(factors_y, tilt(1))
         z_re, z_im = wave_of(factors_z, row(2))
@@ -583,50 +672,31 @@
         )
 
 
-def cosine_period(extent):
-    lines = -(-extent // 128)
-    steps = np.arange(lines * 128).reshape(lines, 128)
-    return jnp.asarray(np.cos(2.0 * np.pi * steps / extent).astype(np.float32))
-
-
-def long_range(mesh_base, mesh_frac, charge, counts):
+def long_range(packed, counts):
     count_x = lax.axis_size("dx")
     count_y = lax.axis_size("dy")
     count_z = lax.axis_size("dz")
-    atom_total = charge.size
-    groups = count_y * count_z
+    groups, _, atom_total = packed.shape
     cells = -(-(MB + 3) // 8) * 8
     length_x = MB * count_x
     length_y = MB * count_y
     length_z = MB * count_z
     waves = MB // count_z
     modes = waves * KZW
-    packed = jnp.concatenate(
-        [
-            charge.reshape(1, atom_total),
-            mesh_base.reshape(3, atom_total).astype(jnp.float32),
-            mesh_frac.reshape(3, atom_total),
-        ],
-        axis=0,
-    )
-    packed = jnp.broadcast_to(packed[None], (groups, 7, atom_total))
     atoms = lax.all_to_all(packed, ("dy", "dz"), 0, 0, tiled=True)
-    table_y = cosine_period(length_y)
-    table_z = cosine_period(length_z)
     sums = pl.pallas_call(
         functools.partial(spread_kernel, (length_y, length_z, waves, cells)),
         out_shape=jax.ShapeDtypeStruct((count_x, cells, 2 * modes), jnp.float32),
-    )(atoms, table_y, table_z)
+        compiler_params=pltpu.CompilerParams(vmem_limit_bytes=8 << 20),
+    )(atoms)
     received = lax.all_to_all(sums, "dx", 0, 0, tiled=True)
     received = received.reshape(count_x * cells, 2 * modes)
     received, counts = lax.optimization_barrier((received, counts))
-    places = (np.arange(count_x) * MB)[:, None] + np.arange(cells)[None, :]
-    angles = 2.0 * np.pi / length_x * (np.arange(length_x)[:, None] * places.reshape(1, -1) % length_x)
-    forward = np.concatenate([np.cos(angles), np.sin(angles)], axis=0).astype(np.float32)
     parts = pl.pallas_call(
         functools.partial(push_kernel, (length_x, length_y, length_z, waves, cells)),
         out_shape=jax.ShapeDtypeStruct((groups, 3, atom_total), jnp.float32),
-    )(atoms, received, jnp.asarray(forward), jnp.asarray(forward.T.copy()), table_y, table_z)
+        compiler_params=pltpu.CompilerParams(vmem_limit_bytes=16 << 20),
+    )(atoms, received)
     parts = lax.all_to_all(parts, ("dy", "dz"), 0, 0, tiled=True)
     return jnp.sum(parts, axis=0), counts
 
@@ -643,16 +713,15 @@
     force_weight,
 ):
     octants = node_state.shape[3]
-    atom_total = 8 * octants
-    places = mesh_base.astype(jnp.float32) + mesh_frac
-    own_rows = jnp.transpose(
-        jnp.concatenate([places, nbr_count.astype(jnp.float32)[None]], axis=0).reshape(4, atom_total)
-    )
-    counts, chosen = list_counts(nbr_code, own_rows)
-    long_force, counts = long_range(mesh_base, mesh_frac, charge, counts)
-    packed_halo = spread_halo(pack_atoms(node_state, places), 1)
+    packed, block, own_rows, channel_rows = pack_atoms(
+        node_state, mesh_base, mesh_frac, charge, nbr_count, radial_weight, force_weight
+    )
+    earlier = list_counts(nbr_code, own_rows, 0, ())
+    counts, chosen = list_counts(nbr_code, own_rows, 4, earlier)
+    long_force, counts = long_range(packed, counts)
+    packed_halo = spread_halo(block)
     updated, short_force = neighbour_sums(
-        packed_halo, counts, chosen, own_rows, radial_weight, mix_weight, force_weight
+        packed_halo, counts, chosen, own_rows, channel_rows, mix_weight
     )
     node_next = updated.reshape(node_state.shape)
     forces = (short_force + long_force).reshape(3, 2, 2, 2, octants)

time: 71.6 us -> 66.2 us (0.925)
  blocking collectives: 8.07 us -> 15.4 us
  waiting for transfers between devices: 0.02 us -> 6.59 us
  Pallas kernels: 34.7 us -> 29.1 us
  other arithmetic: 5.66 us -> 0.1 us
  local copies, waits for them, and re-layouts: 5.28 us -> 0.72 us
  starting transfers between devices: 16 us -> 13.2 us
    all_to_all x0 -> x1, blocking collectives: none -> 8.05 us  [long_range(): atoms = lax.all_to_all(packed, ('dy', 'dz'), 0, 0, tiled=True)]
    ppermute x6 -> x5, waiting for transfers between devices: 0.02 us -> 6.23 us  [the longest x2 4.69 us: neighbours_along(): lax.ppermute(tail, axis, [(i, (i + 1) % count) for i in range(count)])]
    all_to_all x1 -> x0, starting transfers between devices: 3.88 us -> none  [long_range(): atoms = lax.all_to_all(packed, ('dy', 'dz'), 0, 0, tiled=True)]
    convert_element_type x4 -> x0, other arithmetic: 2.16 us -> none  [the longest x2 0.75 us: exact_pieces(): pieces.append(piece.astype(jnp.bfloat16))]
    pallas_call x1, Pallas kernels: 19 us -> 17.1 us  [neighbour_sums(): pl.pallas_call(functools.partial(neighbour_kernel, sizes), grid=(8,), in_...]
    concatenate x3 -> x2, other arithmetic: 1.89 us -> 0.08 us  [spread_halo(): block = jnp.concatenate([below, block, above], axis=dim)]
    all_to_all x1, starting transfers between devices: 3.34 us -> 4.92 us  [long_range(): received = lax.all_to_all(sums, 'dx', 0, 0, tiled=True)]
    reshape x2 -> x0, local copies, waits for them, and re-layouts: 1.56 us -> none  [the longest x1 0.79 us: long_range(): mesh_frac.reshape(3, atom_total)]
  transfers between devices with their start and end apart: 8 -> 6, of which waited for: 0 -> 5; matrix products, arithmetic and copies ran while one was open for 8% -> 0% of each run, Pallas kernels for 22% -> 17%
where the time goes in v4:
time: 66.2 us; the launch traced here: 65.8 us
  Pallas kernels  29.1 us (44%)
  blocking collectives  15.4 us (23%)
  starting transfers between devices  13.2 us (20%)
  waiting for transfers between devices  6.59 us (10%)
  local copies, waits for them, and re-layouts  0.72 us (1%)
  between operations  0.71 us (1%)
    pallas_call x1, Pallas kernels, neighbour_sums(): pl.pallas_call(functools.partial(neighbour_kernel, sizes), grid=(8,), in_...  17.1 us
    all_to_all x1, blocking collectives, long_range(): atoms = lax.all_to_all(packed, ('dy', 'dz'), 0, 0, tiled=True)  8.05 us
    all_to_all x1, blocking collectives, long_range(): parts = lax.all_to_all(parts, ('dy', 'dz'), 0, 0, tiled=True)  7.35 us
    pallas_call x2, Pallas kernels, list_counts(): pl.pallas_call(count_kernel, grid=(4 // together,), in_specs=[pl.BlockSpe...  6.06 us
    all_to_all x1, starting transfers between devices, long_range(): received = lax.all_to_all(sums, 'dx', 0, 0, tiled=True)  4.92 us
    ppermute x2, waiting for transfers between devices, neighbours_along(): lax.ppermute(tail, axis, [(i, (i + 1) % count) for i in range(count)])  4.69 us
    ppermute x2, starting transfers between devices, neighbours_along(): lax.ppermute(tail, axis, [(i, (i + 1) % count) for i in range(count)])  4.65 us
    ppermute x2, starting transfers between devices, neighbours_along(): lax.ppermute(head, axis, [((i + 1) % count, i) for i in range(count)])  3.52 us
  transfers between devices with their start and end apart: 6, of which 5 were waited for; matrix products, arithmetic and copies ran while one was open for 0% of the time, Pallas kernels for 17%

profile of v4, /device:TPU:0, one launch (start us, length us, event | category | flops | bytes accessed | tf_op | source)
XLA Modules:
  0.0 65.8 jit_solution(5392281032217547051)
XLA Ops:
  0.6 1.1 %shard_map.104 = (f32[8,7,256]{2,1,0:T(8,128)S(1)}, bf16[8,48,128]{2,1,0:T(8,128)(2,1)S(1)}, f32[256,8]{1,0:T(8,128)S(1)}, f32[9,128]{1,0:T(8,128)S(1)}) custom-call(bf16[2,2,2,32,128]{4,3,2,1,0:T(8,128)(2,1)} %refs_0_.1, s32[3,2,2,2,32]{4,3,2,1,0:T(2,128)} %refs_1_.1, f32[3,2,2,2,32]{4,3,2,1,0:T(2,128)} %refs_2_.1, f32[2,2,2,32]{3,2,1,0:T(2,128)} %refs_3_.1, ...), custom_call_target="tpu_custom_call" | custom-call | tf_op jit(solution)/shard_map/pallas_call | solution.py:101
  1.8 3.1 %collective-permute-start = (bf16[1,2,2,48,128]{4,3,2,1,0:T(8,128)(2,1)S(1)}, bf16[1,2,2,48,128]{4,3,2,1,0:T(8,128)(2,1)S(1)}, u32[]{:S(2)}, u32[]{:S(2)}) collective-permute-start(bf16[1,2,2,48,128]{4,3,2,1,0:T(8,128)(2,1)S(1)} %bitcast.18), channel_id=1, source_target_pairs={{0,8},{8,16},{16,24},{24,0},{1,9},{9,17},{17,25},{25,1},{2,10},{10... | collective-permute-start | bytes 147464 | tf_op jit(solution)/shard_map/ppermute | solution.py:32
  4.9 2.1 %collective-permute-start.1 = (bf16[1,2,2,48,128]{4,3,2,1,0:T(8,128)(2,1)S(1)}, bf16[1,2,2,48,128]{4,3,2,1,0:T(8,128)(2,1)S(1)}, u32[]{:S(2)}, u32[]{:S(2)}) collective-permute-start(bf16[1,2,2,48,128]{4,3,2,1,0:T(8,128)(2,1)S(1)} %bitcast.17), channel_id=1, source_target_pairs={{8,0},{16,8},{24,16},{0,24},{9,1},{17,9},{25,17},{1,25},{10,2},{18... | collective-permute-start | bytes 147464 | tf_op jit(solution)/shard_map/ppermute | solution.py:33
  7.0 2.1 %collective-permute-done = bf16[1,2,2,48,128]{4,3,2,1,0:T(8,128)(2,1)S(1)} collective-permute-done((bf16[1,2,2,48,128]{4,3,2,1,0:T(8,128)(2,1)S(1)}, bf16[1,2,2,48,128]{4,3,2,1,0:T(8,128)(2,1)S(1)}, u32[]{:S(2)}, u32[]{:S(2)}) %collective-permute-start) | collective-permute-done | bytes 49184 | tf_op jit(solution)/shard_map/ppermute | solution.py:32
  9.1 0.4 collective-permute-done.1
  9.5 1.5 %collective-permute-start.2 = (bf16[4,1,2,48,128]{4,3,2,1,0:T(8,128)(2,1)S(1)}, bf16[4,1,2,48,128]{4,3,2,1,0:T(8,128)(2,1)S(1)}, u32[]{:S(2)}, u32[]{:S(2)}) collective-permute-start(bf16[4,1,2,48,128]{4,3,2,1,0:T(8,128)(2,1)S(1)} %get-tuple-element.26), channel_id=1, source_target_pairs={{0,2},{2,4},{4,6},{6,0},{1,3},{3,5},{5,7},{7,1},{8,10},{10,12},{12... | collective-permute-start | bytes 294920 | tf_op jit(solution)/shard_map/ppermute | solution.py:32
  11.1 1.4 %collective-permute-start.3 = (bf16[4,1,2,48,128]{4,3,2,1,0:T(8,128)(2,1)S(1)}, bf16[4,1,2,48,128]{4,3,2,1,0:T(8,128)(2,1)S(1)}, u32[]{:S(2)}, u32[]{:S(2)}) collective-permute-start(bf16[4,1,2,48,128]{4,3,2,1,0:T(8,128)(2,1)S(1)} %get-tuple-element.27), channel_id=1, source_target_pairs={{2,0},{4,2},{6,4},{0,6},{3,1},{5,3},{7,5},{1,7},{10,8},{12,10},{14... | collective-permute-start | bytes 294920 | tf_op jit(solution)/shard_map/ppermute | solution.py:33
  12.5 2.6 %collective-permute-done.2 = bf16[4,1,2,48,128]{4,3,2,1,0:T(8,128)(2,1)S(1)} collective-permute-done((bf16[4,1,2,48,128]{4,3,2,1,0:T(8,128)(2,1)S(1)}, bf16[4,1,2,48,128]{4,3,2,1,0:T(8,128)(2,1)S(1)}, u32[]{:S(2)}, u32[]{:S(2)}) %collective-permute-start.2) | collective-permute-done | bytes 98336 | tf_op jit(solution)/shard_map/ppermute | solution.py:32
  15.1 1.1 %collective-permute-done.3 = bf16[4,1,2,48,128]{4,3,2,1,0:T(8,128)(2,1)S(1)} collective-permute-done((bf16[4,1,2,48,128]{4,3,2,1,0:T(8,128)(2,1)S(1)}, bf16[4,1,2,48,128]{4,3,2,1,0:T(8,128)(2,1)S(1)}, u32[]{:S(2)}, u32[]{:S(2)}) %collective-permute-start.3) | collective-permute-done | bytes 98336 | tf_op jit(solution)/shard_map/ppermute | solution.py:33
  16.2 0.1 pad_maximum_fusion
  16.3 0.1 collective-permute-start.4
  16.3 8.1 %all_to_all.15.atoms_ref = f32[8,7,256]{2,1,0:T(8,128)S(1)} all-to-all(f32[8,7,256]{2,1,0:T(8,128)S(1)} %get-tuple-element.15), channel_id=1, replica_groups=mesh['dx'=4,'dy'=4,'dz'=2] {'dy','dz'}, dimensions={0} | all-to-all | bytes 114688 | tf_op jit(solution)/shard_map/all_to_all | solution.py:686
  24.4 1.9 %shard_map.105 = f32[4,40,256]{2,1,0:T(8,128)} custom-call(f32[8,7,256]{2,1,0:T(8,128)S(1)} %all_to_all.15.atoms_ref), custom_call_target="tpu_custom_call" | custom-call | tf_op jit(solution)/shard_map/pallas_call | solution.py:687
  26.3 0.0 copy-start
  26.3 4.9 %all-to-all-start.1 = ((f32[4,40,256]{2,1,0:T(8,128)}), f32[4,40,256]{2,1,0:T(8,128)S(1)}, u32[]{:S(2)}, u32[]{:S(2)}) async-start(f32[4,40,256]{2,1,0:T(8,128)} %shard_map.105), calls=%async_computation.1 | async-start | bytes 327680 | tf_op jit(solution)/shard_map/all_to_all | solution.py:692
  31.2 0.0 copy-done
  31.2 3.2 %shard_map.106 = (f32[8,7,32,128]{3,2,1,0:T(8,128)S(1)}, f32[256,128]{1,0:T(8,128)S(1)}) custom-call(s32[256,128]{1,0:T(8,128)S(1)} %bitcast.15, f32[256,8]{1,0:T(8,128)S(1)} %get-tuple-element.16.own_ref), custom_call_target="tpu_custom_call" | custom-call | flops 1000000000 | bytes 700000 | tf_op jit(solution)/shard_map/pallas_call | solution.py:371
  34.4 2.9 %shard_map.107 = (f32[8,7,32,128]{3,2,1,0:T(8,128)S(1)}, f32[256,128]{1,0:T(8,128)S(1)}) custom-call(s32[256,128]{1,0:T(8,128)S(1)} %bitcast.16, f32[256,8]{1,0:T(8,128)S(1)} %get-tuple-element.16.own_ref, f32[8,7,32,128]{3,2,1,0:T(8,128)S(1)} %get-tuple-element.17.refs_0_, ...), custom_call_target="tpu_custom_call", output_to_operand_aliasing={{0}: (2, {}), {1}: (3, {})} | custom-call | flops 1000000000 | bytes 700000 | tf_op jit(solution)/shard_map/pallas_call | solution.py:371
  37.3 0.4 all-to-all-done.1
  37.6 3.0 %shard_map.109 = f32[8,3,256]{2,1,0:T(4,128)S(1)} custom-call(f32[8,7,256]{2,1,0:T(8,128)S(1)} %all_to_all.15.atoms_ref, f32[160,256]{1,0:T(8,128)S(1)} %bitcast.11), custom_call_target="tpu_custom_call" | custom-call | tf_op jit(solution)/shard_map/pallas_call | solution.py:695
  40.7 0.0 copy-start.1
  40.7 7.3 %all_to_all.16 = f32[8,3,256]{2,1,0:T(4,128)S(1)} all-to-all(f32[8,3,256]{2,1,0:T(4,128)S(1)} %shard_map.109), channel_id=1, replica_groups=mesh['dx'=4,'dy'=4,'dz'=2] {'dy','dz'}, dimensions={0} | all-to-all | bytes 49152 | tf_op jit(solution)/shard_map/all_to_all | solution.py:700
  48.0 0.0 collective-permute-done.4
  48.1 0.0 copy-done.1
  48.1 17.1 %shard_map.108 = (bf16[256,128]{1,0:T(8,128)(2,1)}, f32[3,256]{1,0:T(4,128)S(1)}) custom-call(bf16[16,2,48,128]{3,2,1,0:T(8,128)(2,1)S(1)} %bitcast.12, bf16[16,2,48,128]{3,2,1,0:T(8,128)(2,1)S(1)} %bitcast.13, bf16[16,2,48,128]{3,2,1,0:T(8,128)(2,1)S(1)} %bitcast.14, f32[8,7,32,128]{3,2,1,0:T(8,128)S(1)} %get-tuple-element.20.count_ref, ...), custom_call_target="tpu_custom_call" | custom-call | flops 8000000000 | bytes 2000000 | tf_op jit(solution)/shard_map/pallas_call | solution.py:404
  65.1 0.7 %reshape.35 = f32[3,2,2,2,32]{4,3,2,1,0:T(2,128)} reshape(f32[3,256]{1,0:T(4,128)S(1)} %add.3) | data formatting | bytes 6144 | tf_op jit(solution)/shard_map/reshape | solution.py:727
  (5 shorter events, 0.1 us)
Async XLA Ops:
  1.8 7.3 %collective-permute-start = (bf16[1,2,2,48,128]{4,3,2,1,0:T(8,128)(2,1)S(1)}, bf16[1,2,2,48,128]{4,3,2,1,0:T(8,128)(2,1)S(1)}, u32[]{:S(2)}, u32[]{:S(2)}) collective-permute-start(bf16[1,2,2,48,128]{4,3,2,1,0:T(8,128)(2,1)S(1)} %bitcast.18), channel_id=1, source_target_pairs={{0,8},{8,16},{16,24},{24,0},{1,9},{9,17},{17,25},{25,1},{2,10},{10... | collective-permute-start | bytes 147464 | tf_op jit(solution)/shard_map/ppermute | solution.py:32
  4.9 4.6 %collective-permute-start.1 = (bf16[1,2,2,48,128]{4,3,2,1,0:T(8,128)(2,1)S(1)}, bf16[1,2,2,48,128]{4,3,2,1,0:T(8,128)(2,1)S(1)}, u32[]{:S(2)}, u32[]{:S(2)}) collective-permute-start(bf16[1,2,2,48,128]{4,3,2,1,0:T(8,128)(2,1)S(1)} %bitcast.17), channel_id=1, source_target_pairs={{8,0},{16,8},{24,16},{0,24},{9,1},{17,9},{25,17},{1,25},{10,2},{18... | collective-permute-start | bytes 147464 | tf_op jit(solution)/shard_map/ppermute | solution.py:33
  9.5 5.6 %collective-permute-start.2 = (bf16[4,1,2,48,128]{4,3,2,1,0:T(8,128)(2,1)S(1)}, bf16[4,1,2,48,128]{4,3,2,1,0:T(8,128)(2,1)S(1)}, u32[]{:S(2)}, u32[]{:S(2)}) collective-permute-start(bf16[4,1,2,48,128]{4,3,2,1,0:T(8,128)(2,1)S(1)} %get-tuple-element.26), channel_id=1, source_target_pairs={{0,2},{2,4},{4,6},{6,0},{1,3},{3,5},{5,7},{7,1},{8,10},{10,12},{12... | collective-permute-start | bytes 294920 | tf_op jit(solution)/shard_map/ppermute | solution.py:32
  11.1 5.1 %collective-permute-start.3 = (bf16[4,1,2,48,128]{4,3,2,1,0:T(8,128)(2,1)S(1)}, bf16[4,1,2,48,128]{4,3,2,1,0:T(8,128)(2,1)S(1)}, u32[]{:S(2)}, u32[]{:S(2)}) collective-permute-start(bf16[4,1,2,48,128]{4,3,2,1,0:T(8,128)(2,1)S(1)} %get-tuple-element.27), channel_id=1, source_target_pairs={{2,0},{4,2},{6,4},{0,6},{3,1},{5,3},{7,5},{1,7},{10,8},{12,10},{14... | collective-permute-start | bytes 294920 | tf_op jit(solution)/shard_map/ppermute | solution.py:33
  16.3 31.8 %collective-permute-start.4 = (bf16[4,4,2,48,128]{4,3,2,1,0:T(8,128)(2,1)S(1)}, bf16[4,4,2,48,128]{4,3,2,1,0:T(8,128)(2,1)S(1)}, u32[]{:S(2)}, u32[]{:S(2)}) collective-permute-start(bf16[4,4,2,48,128]{4,3,2,1,0:T(8,128)(2,1)S(1)} %pad_maximum_fusion), channel_id=1, source_target_pairs={{0,1},{1,0},{2,3},{3,2},{4,5},{5,4},{6,7},{7,6},{8,9},{9,8},{10,11... | collective-permute-start | bytes 1179656 | tf_op jit(solution)/shard_map/ppermute | solution.py:28
  26.3 4.9 %copy-start = (s32[2,2,2,32,128]{4,3,2,1,0:T(8,128)S(1)}, s32[2,2,2,32,128]{4,3,2,1,0:T(8,128)}, u32[]{:S(2)}) copy-start(s32[2,2,2,32,128]{4,3,2,1,0:T(8,128)} %param.13) | copy-start | bytes 393220
  26.3 11.3 %all-to-all-start.1 = ((f32[4,40,256]{2,1,0:T(8,128)}), f32[4,40,256]{2,1,0:T(8,128)S(1)}, u32[]{:S(2)}, u32[]{:S(2)}) async-start(f32[4,40,256]{2,1,0:T(8,128)} %shard_map.105), calls=%async_computation.1 | async-start | bytes 327680 | tf_op jit(solution)/shard_map/all_to_all | solution.py:692
  40.7 7.4 %copy-start.1 = (bf16[3,128,128]{2,1,0:T(8,128)(2,1)S(1)}, bf16[3,128,128]{2,1,0:T(8,128)(2,1)}, u32[]{:S(2)}) copy-start(bf16[3,128,128]{2,1,0:T(8,128)(2,1)} %mix_ref.1) | copy-start | bytes 294916

commit v5 on v4

--- a/solution.py
+++ b/solution.py
@@ -120,6 +120,7 @@
     octants, tiles, slots, _ = count_ref.shape
     row_of = lax.broadcasted_iota(jnp.int32, (8, 128), 0)
     lane_of = lax.broadcasted_iota(jnp.int32, (8, 128), 1)
+    row_pair = lax.broadcasted_iota(jnp.int32, (16, 128), 0)
     cell_iota = lax.broadcasted_iota(jnp.int32, (128, 128), 0).astype(jnp.float32).astype(jnp.bfloat16)
     one = jnp.ones((128, 128), jnp.bfloat16)
     zero = jnp.zeros((128, 128), jnp.bfloat16)
@@ -131,14 +132,23 @@
         live = lane_float < own_ref[rows, 3:4]
         high = jnp.where(live, codes >> 7, 64)
         low = (codes & 127).astype(jnp.float32)
-        for atom in range(8):
-            low_row = jnp.broadcast_to(low[atom : atom + 1], (16, 128)).astype(jnp.bfloat16)
-            low_hot = jnp.where(cell_iota == jnp.concatenate([low_row] * 8, axis=0), one, zero)
-            high_hot = (row_of == high[atom : atom + 1]).astype(jnp.float32).astype(jnp.bfloat16)
+        for pair in range(0, 8, 2):
+            low_hot = []
+            high_hot = []
+            for atom in (pair, pair + 1):
+                low_row = jnp.broadcast_to(low[atom : atom + 1], (16, 128)).astype(jnp.bfloat16)
+                low_row = jnp.concatenate([low_row] * 8, axis=0)
+                low_hot.append(jnp.where(cell_iota == low_row, one, zero))
+                hot = row_pair == high[atom : atom + 1] + 8 * (atom - pair)
+                high_hot.append(hot.astype(jnp.float32).astype(jnp.bfloat16))
             counted = lax.dot_general(
-                high_hot, low_hot, (((1,), (1,)), ((), ())), preferred_element_type=jnp.float32
+                jnp.concatenate(high_hot, axis=1),
+                jnp.concatenate(low_hot, axis=1),
+                (((1,), (1,)), ((), ())),
+                preferred_element_type=jnp.float32,
             )
-            count_ref[octant, :, 8 * block + atom, :] = counted[:tiles]
+            count_ref[octant, :, 8 * block + pair, :] = counted[:tiles]
+            count_ref[octant, :, 8 * block + pair + 1, :] = counted[8 : 8 + tiles]
     for octant, block in pieces:
         own = slice(8 * block, 8 * block + 8)
         best = jnp.full((8, 128), -1.0, jnp.float32)
@@ -186,7 +196,7 @@
     columns = state_ref.shape[1]
     tiles = columns // 128
     per_tile = 128 // slots
-    blocks = slots // 8
+    couples = slots // 16
     atoms = 8 * slots
     corner = ((octant // 4) * 4 + octant // 2 % 2) * 4 + octant % 2
     sides = [(side // 9 * 4 + side // 3 % 3) * 4 + side % 3 for side in range(27)]
@@ -228,8 +238,6 @@
                 shift = jnp.where(row_of == 0, shift_x, jnp.where(row_of == 1, shift_y, shift_z))
                 place_ref[cell] = total + shift
 
-    for side in range(27):
-        state_ref[here, side * slots : (side + 1) * slots, :] = halo_ref[corner + sides[side]]
     for tile in range(tiles):
         joined = jnp.zeros((8, 128), jnp.float32)
         for part in range(per_tile):
@@ -246,9 +254,6 @@
     hots = jnp.concatenate(
         [jnp.where(wide_lane + 128.0 * tile == chosen, 1.0, 0.0) for tile in range(tiles)], axis=1
     ).astype(jnp.bfloat16)
-    state_ref[here, 27 * slots :, :] = jnp.dot(
-        hots, state_ref[here], preferred_element_type=jnp.float32
-    ).astype(jnp.bfloat16)
     pieces = []
     spots = jnp.concatenate([table_ref[tile] for tile in range(tiles)], axis=1)
     for _ in range(3):
@@ -273,7 +278,8 @@
 
     def fill_edges(block):
         rows = slice(8 * block, 8 * block + 8)
-        edge_ref = edge_refs[block % 2]
+        edge_ref = edge_refs[block // 2 % 2]
+        offset = block % 2 * 9 * basis * 8
         own = own_ref[rows, :]
         for tile in range(tiles):
             times = count_ref[0, tile, rows, :]
@@ -306,34 +312,46 @@
                         parts = [first * angular[degree], second * angular[degree]]
                     else:
                         parts = [first, second]
-                    at = (degree * basis + 2 * pair) * 8
+                    at = offset + (degree * basis + 2 * pair) * 8
                     edge_ref[tile, at : at + 16, :] = jnp.concatenate(parts, axis=0).astype(
                         jnp.bfloat16
                     )
 
-    def add_up(block, parity, first_row):
-        edge_ref = edge_refs[block % 2]
+    def add_up(couple, parity, first_row):
+        edge_ref = edge_refs[couple % 2]
         edges = jnp.concatenate([edge_ref[tile] for tile in range(tiles)], axis=1)
         summed = jnp.dot(edges, state_ref[parity], preferred_element_type=jnp.float32)
-        for degree in range(9):
-            total = summed[degree * basis * 8 : degree * basis * 8 + 8] * radial_ref[0:1, :]
-            for b in range(1, basis):
-                at = (degree * basis + b) * 8
-                total = total + summed[at : at + 8] * radial_ref[b : b + 1, :]
-            message_ref[degree, pl.ds(first_row, 8), :] = total * (1.0 / math.sqrt(NBR))
-
-    def row_start(block):
-        return pl.multiple_of(octant * slots + 8 * block, 8)
+        for half in range(2):
+            offset = half * 9 * basis * 8
+            for degree in range(9):
+                at = offset + degree * basis * 8
+                total = summed[at : at + 8] * radial_ref[0:1, :]
+                for b in range(1, basis):
+                    at = offset + (degree * basis + b) * 8
+                    total = total + summed[at : at + 8] * radial_ref[b : b + 1, :]
+                message_ref[degree, pl.ds(first_row + 8 * half, 8), :] = total * (
+                    1.0 / math.sqrt(NBR)
+                )
+
+    def row_start(couple):
+        return pl.multiple_of(octant * slots + 16 * couple, 8)
 
     fill_edges(0)
-    add_up(blocks - 1, before, pl.multiple_of((octant * slots + atoms - 8) % atoms, 8))
-    for block in range(1, blocks):
-        fill_edges(block)
-        add_up(block - 1, here, row_start(block - 1))
+    fill_edges(1)
+    add_up(couples - 1, before, pl.multiple_of((octant * slots + atoms - 16) % atoms, 8))
+    for side in range(27):
+        state_ref[here, side * slots : (side + 1) * slots, :] = halo_ref[corner + sides[side]]
+    state_ref[here, 27 * slots :, :] = jnp.dot(
+        hots, state_ref[here], preferred_element_type=jnp.float32
+    ).astype(jnp.bfloat16)
+    for couple in range(1, couples):
+        fill_edges(2 * couple)
+        fill_edges(2 * couple + 1)
+        add_up(couple - 1, here, row_start(couple - 1))
 
     @pl.when(octant == 7)
     def _():
-        add_up(blocks - 1, here, row_start(blocks - 1))
+        add_up(couples - 1, here, row_start(couples - 1))
         invariant = jnp.dot(
             message_ref[0].astype(jnp.bfloat16), mix_ref[0], preferred_element_type=jnp.float32
         )
@@ -363,14 +381,14 @@
             push_ref[k : k + 1, :] = pushed[0:1]
 
 
-def list_counts(nbr_code, own_rows, first, earlier):
+def list_counts(nbr_code, own_rows, first, number, earlier):
     slots = nbr_code.shape[3]
     tiles = 28 * slots // 128
     together = 2
     start = first // together
     return pl.pallas_call(
         count_kernel,
-        grid=(4 // together,),
+        grid=(number // together,),
         in_specs=[
             pl.BlockSpec((together * slots, NBR), lambda o: (o + start, 0)),
             pl.BlockSpec((together * slots, 8), lambda o: (o + start, 0)),
@@ -399,7 +417,7 @@
     basis = channel_rows.shape[0] - 1
     columns = 28 * slots
     sizes = (lax.axis_size("dx"), lax.axis_size("dy"), lax.axis_size("dz"), slots, basis)
-    edges = pltpu.VMEM((tiles, 9 * basis * 8, 128), jnp.bfloat16)
+    edges = pltpu.VMEM((tiles, 9 * basis * 16, 128), jnp.bfloat16)
     whole = lambda *shape: pl.BlockSpec(shape, lambda o: (0,) * len(shape))
     return pl.pallas_call(
         functools.partial(neighbour_kernel, sizes),
@@ -716,8 +734,8 @@
     packed, block, own_rows, channel_rows = pack_atoms(
         node_state, mesh_base, mesh_frac, charge, nbr_count, radial_weight, force_weight
     )
-    earlier = list_counts(nbr_code, own_rows, 0, ())
-    counts, chosen = list_counts(nbr_code, own_rows, 4, earlier)
+    earlier = list_counts(nbr_code, own_rows, 0, 2, ())
+    counts, chosen = list_counts(nbr_code, own_rows, 2, 6, earlier)
     long_force, counts = long_range(packed, counts)
     packed_halo = spread_halo(block)
     updated, short_force = neighbour_sums(

time: 66.2 us -> 65.7 us (level)
  Pallas kernels: 29.1 us -> 26.1 us
  waiting for transfers between devices: 6.59 us -> 9.05 us
    all_to_all x1, waiting for transfers between devices: 0.36 us -> 2.83 us  [long_range(): received = lax.all_to_all(sums, 'dx', 0, 0, tiled=True)]
    pallas_call x2, Pallas kernels: 6.06 us -> 3.6 us  [list_counts(): pl.pallas_call(count_kernel, grid=(number // together,), in_specs=[pl.Blo...]
  transfers between devices with their start and end apart: 6 -> 6, of which waited for: 5 -> 5; matrix products, arithmetic and copies ran while one was open for 0% -> 0% of each run, Pallas kernels for 17% -> 13%
where the time goes in v5:
time: 65.7 us; the launch traced here: 65.3 us
  Pallas kernels  26.1 us (40%)
  blocking collectives  15.4 us (23%)
  starting transfers between devices  13.2 us (20%)
  waiting for transfers between devices  9.05 us (14%)
  local copies, waits for them, and re-layouts  0.72 us (1%)
  between operations  0.71 us (1%)
    pallas_call x1, Pallas kernels, neighbour_sums(): pl.pallas_call(functools.partial(neighbour_kernel, sizes), grid=(8,), in_...  16.5 us
    all_to_all x1, blocking collectives, long_range(): atoms = lax.all_to_all(packed, ('dy', 'dz'), 0, 0, tiled=True)  8.05 us
    all_to_all x1, blocking collectives, long_range(): parts = lax.all_to_all(parts, ('dy', 'dz'), 0, 0, tiled=True)  7.35 us
    all_to_all x1, starting transfers between devices, long_range(): received = lax.all_to_all(sums, 'dx', 0, 0, tiled=True)  4.92 us
    ppermute x2, waiting for transfers between devices, neighbours_along(): lax.ppermute(tail, axis, [(i, (i + 1) % count) for i in range(count)])  4.69 us
    ppermute x2, starting transfers between devices, neighbours_along(): lax.ppermute(tail, axis, [(i, (i + 1) % count) for i in range(count)])  4.65 us
    pallas_call x2, Pallas kernels, list_counts(): pl.pallas_call(count_kernel, grid=(number // together,), in_specs=[pl.Blo...  3.6 us
    ppermute x2, starting transfers between devices, neighbours_along(): lax.ppermute(head, axis, [((i + 1) % count, i) for i in range(count)])  3.52 us
  transfers between devices with their start and end apart: 6, of which 5 were waited for; matrix products, arithmetic and copies ran while one was open for 0% of the time, Pallas kernels for 13%

profile of v5, /device:TPU:0, one launch (start us, length us, event | category | flops | bytes accessed | tf_op | source)
XLA Modules:
  0.0 65.3 jit_solution(6200370816278012482)
XLA Ops:
  0.6 1.1 %shard_map.104 = (f32[8,7,256]{2,1,0:T(8,128)S(1)}, bf16[8,48,128]{2,1,0:T(8,128)(2,1)S(1)}, f32[256,8]{1,0:T(8,128)S(1)}, f32[9,128]{1,0:T(8,128)S(1)}) custom-call(bf16[2,2,2,32,128]{4,3,2,1,0:T(8,128)(2,1)} %refs_0_.1, s32[3,2,2,2,32]{4,3,2,1,0:T(2,128)} %refs_1_.1, f32[3,2,2,2,32]{4,3,2,1,0:T(2,128)} %refs_2_.1, f32[2,2,2,32]{3,2,1,0:T(2,128)} %refs_3_.1, ...), custom_call_target="tpu_custom_call" | custom-call | tf_op jit(solution)/shard_map/pallas_call | solution.py:101
  1.8 3.1 %collective-permute-start = (bf16[1,2,2,48,128]{4,3,2,1,0:T(8,128)(2,1)S(1)}, bf16[1,2,2,48,128]{4,3,2,1,0:T(8,128)(2,1)S(1)}, u32[]{:S(2)}, u32[]{:S(2)}) collective-permute-start(bf16[1,2,2,48,128]{4,3,2,1,0:T(8,128)(2,1)S(1)} %bitcast.18), channel_id=1, source_target_pairs={{0,8},{8,16},{16,24},{24,0},{1,9},{9,17},{17,25},{25,1},{2,10},{10... | collective-permute-start | bytes 147464 | tf_op jit(solution)/shard_map/ppermute | solution.py:32
  4.9 2.1 %collective-permute-start.1 = (bf16[1,2,2,48,128]{4,3,2,1,0:T(8,128)(2,1)S(1)}, bf16[1,2,2,48,128]{4,3,2,1,0:T(8,128)(2,1)S(1)}, u32[]{:S(2)}, u32[]{:S(2)}) collective-permute-start(bf16[1,2,2,48,128]{4,3,2,1,0:T(8,128)(2,1)S(1)} %bitcast.17), channel_id=1, source_target_pairs={{8,0},{16,8},{24,16},{0,24},{9,1},{17,9},{25,17},{1,25},{10,2},{18... | collective-permute-start | bytes 147464 | tf_op jit(solution)/shard_map/ppermute | solution.py:33
  7.0 2.1 %collective-permute-done = bf16[1,2,2,48,128]{4,3,2,1,0:T(8,128)(2,1)S(1)} collective-permute-done((bf16[1,2,2,48,128]{4,3,2,1,0:T(8,128)(2,1)S(1)}, bf16[1,2,2,48,128]{4,3,2,1,0:T(8,128)(2,1)S(1)}, u32[]{:S(2)}, u32[]{:S(2)}) %collective-permute-start) | collective-permute-done | bytes 49184 | tf_op jit(solution)/shard_map/ppermute | solution.py:32
  9.1 0.4 collective-permute-done.1
  9.5 1.5 %collective-permute-start.2 = (bf16[4,1,2,48,128]{4,3,2,1,0:T(8,128)(2,1)S(1)}, bf16[4,1,2,48,128]{4,3,2,1,0:T(8,128)(2,1)S(1)}, u32[]{:S(2)}, u32[]{:S(2)}) collective-permute-start(bf16[4,1,2,48,128]{4,3,2,1,0:T(8,128)(2,1)S(1)} %get-tuple-element.26), channel_id=1, source_target_pairs={{0,2},{2,4},{4,6},{6,0},{1,3},{3,5},{5,7},{7,1},{8,10},{10,12},{12... | collective-permute-start | bytes 294920 | tf_op jit(solution)/shard_map/ppermute | solution.py:32
  11.1 1.4 %collective-permute-start.3 = (bf16[4,1,2,48,128]{4,3,2,1,0:T(8,128)(2,1)S(1)}, bf16[4,1,2,48,128]{4,3,2,1,0:T(8,128)(2,1)S(1)}, u32[]{:S(2)}, u32[]{:S(2)}) collective-permute-start(bf16[4,1,2,48,128]{4,3,2,1,0:T(8,128)(2,1)S(1)} %get-tuple-element.27), channel_id=1, source_target_pairs={{2,0},{4,2},{6,4},{0,6},{3,1},{5,3},{7,5},{1,7},{10,8},{12,10},{14... | collective-permute-start | bytes 294920 | tf_op jit(solution)/shard_map/ppermute | solution.py:33
  12.5 2.6 %collective-permute-done.2 = bf16[4,1,2,48,128]{4,3,2,1,0:T(8,128)(2,1)S(1)} collective-permute-done((bf16[4,1,2,48,128]{4,3,2,1,0:T(8,128)(2,1)S(1)}, bf16[4,1,2,48,128]{4,3,2,1,0:T(8,128)(2,1)S(1)}, u32[]{:S(2)}, u32[]{:S(2)}) %collective-permute-start.2) | collective-permute-done | bytes 98336 | tf_op jit(solution)/shard_map/ppermute | solution.py:32
  15.1 1.1 %collective-permute-done.3 = bf16[4,1,2,48,128]{4,3,2,1,0:T(8,128)(2,1)S(1)} collective-permute-done((bf16[4,1,2,48,128]{4,3,2,1,0:T(8,128)(2,1)S(1)}, bf16[4,1,2,48,128]{4,3,2,1,0:T(8,128)(2,1)S(1)}, u32[]{:S(2)}, u32[]{:S(2)}) %collective-permute-start.3) | collective-permute-done | bytes 98336 | tf_op jit(solution)/shard_map/ppermute | solution.py:33
  16.2 0.1 pad_maximum_fusion
  16.3 0.1 collective-permute-start.4
  16.3 8.1 %all_to_all.15.atoms_ref = f32[8,7,256]{2,1,0:T(8,128)S(1)} all-to-all(f32[8,7,256]{2,1,0:T(8,128)S(1)} %get-tuple-element.15), channel_id=1, replica_groups=mesh['dx'=4,'dy'=4,'dz'=2] {'dy','dz'}, dimensions={0} | all-to-all | bytes 114688 | tf_op jit(solution)/shard_map/all_to_all | solution.py:704
  24.4 1.9 %shard_map.105 = f32[4,40,256]{2,1,0:T(8,128)} custom-call(f32[8,7,256]{2,1,0:T(8,128)S(1)} %all_to_all.15.atoms_ref), custom_call_target="tpu_custom_call" | custom-call | tf_op jit(solution)/shard_map/pallas_call | solution.py:705
  26.3 0.0 copy-start
  26.3 4.9 %all-to-all-start.1 = ((f32[4,40,256]{2,1,0:T(8,128)}), f32[4,40,256]{2,1,0:T(8,128)S(1)}, u32[]{:S(2)}, u32[]{:S(2)}) async-start(f32[4,40,256]{2,1,0:T(8,128)} %shard_map.105), calls=%async_computation.1 | async-start | bytes 327680 | tf_op jit(solution)/shard_map/all_to_all | solution.py:710
  31.2 0.0 copy-done
  31.2 0.9 %shard_map.106 = (f32[8,7,32,128]{3,2,1,0:T(8,128)S(1)}, f32[256,128]{1,0:T(8,128)S(1)}) custom-call(s32[256,128]{1,0:T(8,128)S(1)} %bitcast.15, f32[256,8]{1,0:T(8,128)S(1)} %get-tuple-element.16.own_ref), custom_call_target="tpu_custom_call" | custom-call | flops 1000000000 | bytes 700000 | tf_op jit(solution)/shard_map/pallas_call | solution.py:389
  32.1 2.7 %shard_map.107 = (f32[8,7,32,128]{3,2,1,0:T(8,128)S(1)}, f32[256,128]{1,0:T(8,128)S(1)}) custom-call(s32[256,128]{1,0:T(8,128)S(1)} %bitcast.16, f32[256,8]{1,0:T(8,128)S(1)} %get-tuple-element.16.own_ref, f32[8,7,32,128]{3,2,1,0:T(8,128)S(1)} %get-tuple-element.17.refs_0_, ...), custom_call_target="tpu_custom_call", output_to_operand_aliasing={{0}: (2, {}), {1}: (3, {})} | custom-call | flops 1000000000 | bytes 700000 | tf_op jit(solution)/shard_map/pallas_call | solution.py:389
  34.8 2.8 %all-to-all-done.1 = f32[4,40,256]{2,1,0:T(8,128)S(1)} async-done(((f32[4,40,256]{2,1,0:T(8,128)}), f32[4,40,256]{2,1,0:T(8,128)S(1)}, u32[]{:S(2)}, u32[]{:S(2)}) %all-to-all-start.1) | async-done | bytes 163872 | tf_op jit(solution)/shard_map/all_to_all | solution.py:710
  37.6 3.0 %shard_map.109 = f32[8,3,256]{2,1,0:T(4,128)S(1)} custom-call(f32[8,7,256]{2,1,0:T(8,128)S(1)} %all_to_all.15.atoms_ref, f32[160,256]{1,0:T(8,128)S(1)} %bitcast.11), custom_call_target="tpu_custom_call" | custom-call | tf_op jit(solution)/shard_map/pallas_call | solution.py:713
  40.7 0.0 copy-start.1
  40.7 7.3 %all_to_all.16 = f32[8,3,256]{2,1,0:T(4,128)S(1)} all-to-all(f32[8,3,256]{2,1,0:T(4,128)S(1)} %shard_map.109), channel_id=1, replica_groups=mesh['dx'=4,'dy'=4,'dz'=2] {'dy','dz'}, dimensions={0} | all-to-all | bytes 49152 | tf_op jit(solution)/shard_map/all_to_all | solution.py:718
  48.0 0.0 collective-permute-done.4
  48.1 0.0 copy-done.1
  48.1 16.5 %shard_map.108 = (bf16[256,128]{1,0:T(8,128)(2,1)}, f32[3,256]{1,0:T(4,128)S(1)}) custom-call(bf16[16,2,48,128]{3,2,1,0:T(8,128)(2,1)S(1)} %bitcast.12, bf16[16,2,48,128]{3,2,1,0:T(8,128)(2,1)S(1)} %bitcast.13, bf16[16,2,48,128]{3,2,1,0:T(8,128)(2,1)S(1)} %bitcast.14, f32[8,7,32,128]{3,2,1,0:T(8,128)S(1)} %get-tuple-element.20.count_ref, ...), custom_call_target="tpu_custom_call" | custom-call | flops 8000000000 | bytes 2000000 | tf_op jit(solution)/shard_map/pallas_call | solution.py:422
  64.6 0.7 %reshape.35 = f32[3,2,2,2,32]{4,3,2,1,0:T(2,128)} reshape(f32[3,256]{1,0:T(4,128)S(1)} %add.3) | data formatting | bytes 6144 | tf_op jit(solution)/shard_map/reshape | solution.py:745
  (5 shorter events, 0.1 us)
Async XLA Ops:
  1.8 7.3 %collective-permute-start = (bf16[1,2,2,48,128]{4,3,2,1,0:T(8,128)(2,1)S(1)}, bf16[1,2,2,48,128]{4,3,2,1,0:T(8,128)(2,1)S(1)}, u32[]{:S(2)}, u32[]{:S(2)}) collective-permute-start(bf16[1,2,2,48,128]{4,3,2,1,0:T(8,128)(2,1)S(1)} %bitcast.18), channel_id=1, source_target_pairs={{0,8},{8,16},{16,24},{24,0},{1,9},{9,17},{17,25},{25,1},{2,10},{10... | collective-permute-start | bytes 147464 | tf_op jit(solution)/shard_map/ppermute | solution.py:32
  4.9 4.6 %collective-permute-start.1 = (bf16[1,2,2,48,128]{4,3,2,1,0:T(8,128)(2,1)S(1)}, bf16[1,2,2,48,128]{4,3,2,1,0:T(8,128)(2,1)S(1)}, u32[]{:S(2)}, u32[]{:S(2)}) collective-permute-start(bf16[1,2,2,48,128]{4,3,2,1,0:T(8,128)(2,1)S(1)} %bitcast.17), channel_id=1, source_target_pairs={{8,0},{16,8},{24,16},{0,24},{9,1},{17,9},{25,17},{1,25},{10,2},{18... | collective-permute-start | bytes 147464 | tf_op jit(solution)/shard_map/ppermute | solution.py:33
  9.5 5.6 %collective-permute-start.2 = (bf16[4,1,2,48,128]{4,3,2,1,0:T(8,128)(2,1)S(1)}, bf16[4,1,2,48,128]{4,3,2,1,0:T(8,128)(2,1)S(1)}, u32[]{:S(2)}, u32[]{:S(2)}) collective-permute-start(bf16[4,1,2,48,128]{4,3,2,1,0:T(8,128)(2,1)S(1)} %get-tuple-element.26), channel_id=1, source_target_pairs={{0,2},{2,4},{4,6},{6,0},{1,3},{3,5},{5,7},{7,1},{8,10},{10,12},{12... | collective-permute-start | bytes 294920 | tf_op jit(solution)/shard_map/ppermute | solution.py:32
  11.1 5.1 %collective-permute-start.3 = (bf16[4,1,2,48,128]{4,3,2,1,0:T(8,128)(2,1)S(1)}, bf16[4,1,2,48,128]{4,3,2,1,0:T(8,128)(2,1)S(1)}, u32[]{:S(2)}, u32[]{:S(2)}) collective-permute-start(bf16[4,1,2,48,128]{4,3,2,1,0:T(8,128)(2,1)S(1)} %get-tuple-element.27), channel_id=1, source_target_pairs={{2,0},{4,2},{6,4},{0,6},{3,1},{5,3},{7,5},{1,7},{10,8},{12,10},{14... | collective-permute-start | bytes 294920 | tf_op jit(solution)/shard_map/ppermute | solution.py:33
  16.3 31.8 %collective-permute-start.4 = (bf16[4,4,2,48,128]{4,3,2,1,0:T(8,128)(2,1)S(1)}, bf16[4,4,2,48,128]{4,3,2,1,0:T(8,128)(2,1)S(1)}, u32[]{:S(2)}, u32[]{:S(2)}) collective-permute-start(bf16[4,4,2,48,128]{4,3,2,1,0:T(8,128)(2,1)S(1)} %pad_maximum_fusion), channel_id=1, source_target_pairs={{0,1},{1,0},{2,3},{3,2},{4,5},{5,4},{6,7},{7,6},{8,9},{9,8},{10,11... | collective-permute-start | bytes 1179656 | tf_op jit(solution)/shard_map/ppermute | solution.py:28
  26.3 4.9 %copy-start = (s32[2,2,2,32,128]{4,3,2,1,0:T(8,128)S(1)}, s32[2,2,2,32,128]{4,3,2,1,0:T(8,128)}, u32[]{:S(2)}) copy-start(s32[2,2,2,32,128]{4,3,2,1,0:T(8,128)} %param.13) | copy-start | bytes 393220
  26.3 11.3 %all-to-all-start.1 = ((f32[4,40,256]{2,1,0:T(8,128)}), f32[4,40,256]{2,1,0:T(8,128)S(1)}, u32[]{:S(2)}, u32[]{:S(2)}) async-start(f32[4,40,256]{2,1,0:T(8,128)} %shard_map.105), calls=%async_computation.1 | async-start | bytes 327680 | tf_op jit(solution)/shard_map/all_to_all | solution.py:710
  40.7 7.4 %copy-start.1 = (bf16[3,128,128]{2,1,0:T(8,128)(2,1)S(1)}, bf16[3,128,128]{2,1,0:T(8,128)(2,1)}, u32[]{:S(2)}) copy-start(bf16[3,128,128]{2,1,0:T(8,128)(2,1)} %mix_ref.1) | copy-start | bytes 294916

commit v6 on v5

--- a/solution.py
+++ b/solution.py
@@ -19,7 +19,6 @@
 coulomb = 332.0637
 sigma_low = 8.0
 sigma_rate = 1.5
-highest = lax.Precision.HIGHEST
 
 
 def neighbours_along(block, axis, dim):
@@ -537,6 +536,20 @@
     return high, values - high
 
 
+def split_dot(left, right):
+    rows = left.shape[0]
+    left_high, left_low = halves(left)
+    right_high, right_low = halves(right)
+    both = jnp.concatenate([left_high, left_low], axis=0).astype(jnp.bfloat16)
+    main = jnp.dot(both, right_high.astype(jnp.bfloat16), preferred_element_type=jnp.float32)
+    side = jnp.dot(
+        left_high.astype(jnp.bfloat16),
+        right_low.astype(jnp.bfloat16),
+        preferred_element_type=jnp.float32,
+    )
+    return main[:rows] + (main[rows:] + side)
+
+
 def wave_start():
     return lax.axis_index("dy") * lax.axis_size("dz") + lax.axis_index("dz")
 
@@ -584,7 +597,46 @@
         sums_ref[copy] = total
 
 
-def push_kernel(sizes, atoms_ref, sums_ref, force_ref):
+def mesh_tables_kernel(sizes, forward_ref, lines_ref, green_ref):
+    length_x, length_y, length_z, waves, cells = sizes
+    modes = waves * KZW
+    start = wave_start() * waves
+    anchor = lax.axis_index("dx") * MB
+    count_x = length_x // MB
+    lined = -(-count_x * cells // 128) * 128
+    place = lax.broadcasted_iota(jnp.int32, (1, lined), 1)
+    place = place + (MB - cells) * (place // cells)
+    mode = lax.broadcasted_iota(jnp.int32, (length_x, lined), 0)
+    forward = jnp.concatenate(turn(mode * place, length_x), axis=0)[:, : count_x * cells]
+    forward_ref[...] = forward
+
+    def folded(number, extent):
+        number = jnp.where(2 * number >= extent, number - extent, number)
+        return number.astype(jnp.float32) / (cell_size * extent)
+
+    mode_shape = (length_x, modes)
+    mode_x = lax.broadcasted_iota(jnp.int32, mode_shape, 0)
+    mode_lane = lax.broadcasted_iota(jnp.int32, mode_shape, 1)
+    wave_square = (
+        jnp.square(folded(mode_x, length_x))
+        + jnp.square(folded(start + mode_lane // KZW, length_y))
+        + jnp.square(folded(mode_lane % KZW + 1, length_z))
+    )
+    volume = cell_size**3 * length_x * length_y * length_z
+    green = (
+        coulomb
+        / (math.pi * volume)
+        * jnp.exp(-(math.pi**2) * wave_square / ewald_beta**2)
+        / wave_square
+    )
+    green_ref[...] = green
+    cell = anchor + lax.broadcasted_iota(jnp.int32, (cells, length_x), 0)
+    mode = lax.broadcasted_iota(jnp.int32, (cells, length_x), 1)
+    lines = jnp.concatenate(turn(cell * mode, length_x), axis=0)
+    lines_ref[...] = lines
+
+
+def push_kernel(sizes, atoms_ref, sums_ref, forward_ref, lines_ref, green_ref, force_ref):
     length_x, length_y, length_z, waves, cells = sizes
     groups, _, width = atoms_ref.shape
     modes = waves * KZW
@@ -593,37 +645,11 @@
     modes_z = 1 + lax.broadcasted_iota(jnp.int32, (KZW, 128), 0)
     anchor = lax.axis_index("dx") * MB
 
-    count_x = length_x // MB
-    lined = -(-count_x * cells // 128) * 128
-    place = lax.broadcasted_iota(jnp.int32, (1, lined), 1)
-    place = place + (MB - cells) * (place // cells)
-    mode = lax.broadcasted_iota(jnp.int32, (length_x, lined), 0)
-    forward = jnp.concatenate(turn(mode * place, length_x), axis=0)[:, : count_x * cells]
-    turned = jnp.dot(
-        forward, sums_ref[...], precision=highest, preferred_element_type=jnp.float32
-    )
+    turned = split_dot(forward_ref[...], sums_ref[...])
     cosine = turned[:length_x]
     sine = turned[length_x:]
 
-    def folded(number, extent):
-        number = jnp.where(2 * number >= extent, number - extent, number)
-        return number.astype(jnp.float32) / (cell_size * extent)
-
-    mode_shape = (length_x, modes)
-    mode_x = lax.broadcasted_iota(jnp.int32, mode_shape, 0)
-    mode_lane = lax.broadcasted_iota(jnp.int32, mode_shape, 1)
-    wave_square = (
-        jnp.square(folded(mode_x, length_x))
-        + jnp.square(folded(start + mode_lane // KZW, length_y))
-        + jnp.square(folded(mode_lane % KZW + 1, length_z))
-    )
-    volume = cell_size**3 * length_x * length_y * length_z
-    green = (
-        coulomb
-        / (math.pi * volume)
-        * jnp.exp(-(math.pi**2) * wave_square / ewald_beta**2)
-        / wave_square
-    )
+    green = green_ref[...]
     scaled = jnp.concatenate(
         [
             green * (cosine[:, :modes] + sine[:, modes:]),
@@ -631,10 +657,7 @@
         ],
         axis=1,
     )
-    cell = anchor + lax.broadcasted_iota(jnp.int32, (cells, length_x), 0)
-    mode = lax.broadcasted_iota(jnp.int32, (cells, length_x), 1)
-    lines = jnp.concatenate(turn(cell * mode, length_x), axis=0)
-    turned = jnp.dot(lines, scaled, precision=highest, preferred_element_type=jnp.float32)
+    turned = split_dot(lines_ref[...], scaled)
     cosine = turned[:cells]
     sine = turned[cells:]
     back = jnp.concatenate(
@@ -709,12 +732,21 @@
     )(atoms)
     received = lax.all_to_all(sums, "dx", 0, 0, tiled=True)
     received = received.reshape(count_x * cells, 2 * modes)
-    received, counts = lax.optimization_barrier((received, counts))
+    tables = pl.pallas_call(
+        functools.partial(mesh_tables_kernel, (length_x, length_y, length_z, waves, cells)),
+        out_shape=[
+            jax.ShapeDtypeStruct((2 * length_x, count_x * cells), jnp.float32),
+            jax.ShapeDtypeStruct((2 * cells, length_x), jnp.float32),
+            jax.ShapeDtypeStruct((length_x, modes), jnp.float32),
+        ],
+        compiler_params=pltpu.CompilerParams(vmem_limit_bytes=4 << 20),
+    )()
+    received, counts, tables = lax.optimization_barrier((received, counts, tables))
     parts = pl.pallas_call(
         functools.partial(push_kernel, (length_x, length_y, length_z, waves, cells)),
         out_shape=jax.ShapeDtypeStruct((groups, 3, atom_total), jnp.float32),
         compiler_params=pltpu.CompilerParams(vmem_limit_bytes=16 << 20),
-    )(atoms, received)
+    )(atoms, received, *tables)
     parts = lax.all_to_all(parts, ("dy", "dz"), 0, 0, tiled=True)
     return jnp.sum(parts, axis=0), counts
 

time: 65.7 us -> 65.3 us (level)
  no operation moved by 1% of the time
where the time goes in v6:
time: 65.3 us; the launch traced here: 64.9 us
  Pallas kernels  26.1 us (40%)
  blocking collectives  15.4 us (24%)
  starting transfers between devices  13.2 us (20%)
  waiting for transfers between devices  8.74 us (13%)
  local copies, waits for them, and re-layouts  0.72 us (1%)
  between operations  0.71 us (1%)
    pallas_call x1, Pallas kernels, neighbour_sums(): pl.pallas_call(functools.partial(neighbour_kernel, sizes), grid=(8,), in_...  16.6 us
    all_to_all x1, blocking collectives, long_range(): atoms = lax.all_to_all(packed, ('dy', 'dz'), 0, 0, tiled=True)  8.05 us
    all_to_all x1, blocking collectives, long_range(): parts = lax.all_to_all(parts, ('dy', 'dz'), 0, 0, tiled=True)  7.35 us
    all_to_all x1, starting transfers between devices, long_range(): received = lax.all_to_all(sums, 'dx', 0, 0, tiled=True)  4.92 us
    ppermute x2, waiting for transfers between devices, neighbours_along(): lax.ppermute(tail, axis, [(i, (i + 1) % count) for i in range(count)])  4.69 us
    ppermute x2, starting transfers between devices, neighbours_along(): lax.ppermute(tail, axis, [(i, (i + 1) % count) for i in range(count)])  4.65 us
    pallas_call x2, Pallas kernels, list_counts(): pl.pallas_call(count_kernel, grid=(number // together,), in_specs=[pl.Blo...  3.61 us
    ppermute x2, starting transfers between devices, neighbours_along(): lax.ppermute(head, axis, [((i + 1) % count, i) for i in range(count)])  3.52 us
  transfers between devices with their start and end apart: 6, of which 5 were waited for; matrix products, arithmetic and copies ran while one was open for 0% of the time, Pallas kernels for 13%

profile of v6, /device:TPU:0, one launch (start us, length us, event | category | flops | bytes accessed | tf_op | source)
XLA Modules:
  0.0 64.9 jit_solution(5513277985048495699)
XLA Ops:
  0.6 1.1 %shard_map.104 = (f32[8,7,256]{2,1,0:T(8,128)S(1)}, bf16[8,48,128]{2,1,0:T(8,128)(2,1)S(1)}, f32[256,8]{1,0:T(8,128)S(1)}, f32[9,128]{1,0:T(8,128)S(1)}) custom-call(bf16[2,2,2,32,128]{4,3,2,1,0:T(8,128)(2,1)} %refs_0_.1, s32[3,2,2,2,32]{4,3,2,1,0:T(2,128)} %refs_1_.1, f32[3,2,2,2,32]{4,3,2,1,0:T(2,128)} %refs_2_.1, f32[2,2,2,32]{3,2,1,0:T(2,128)} %refs_3_.1, ...), custom_call_target="tpu_custom_call" | custom-call | tf_op jit(solution)/shard_map/pallas_call | solution.py:100
  1.8 3.1 %collective-permute-start = (bf16[1,2,2,48,128]{4,3,2,1,0:T(8,128)(2,1)S(1)}, bf16[1,2,2,48,128]{4,3,2,1,0:T(8,128)(2,1)S(1)}, u32[]{:S(2)}, u32[]{:S(2)}) collective-permute-start(bf16[1,2,2,48,128]{4,3,2,1,0:T(8,128)(2,1)S(1)} %bitcast.18), channel_id=1, source_target_pairs={{0,8},{8,16},{16,24},{24,0},{1,9},{9,17},{17,25},{25,1},{2,10},{10... | collective-permute-start | bytes 147464 | tf_op jit(solution)/shard_map/ppermute | solution.py:31
  4.9 2.1 %collective-permute-start.1 = (bf16[1,2,2,48,128]{4,3,2,1,0:T(8,128)(2,1)S(1)}, bf16[1,2,2,48,128]{4,3,2,1,0:T(8,128)(2,1)S(1)}, u32[]{:S(2)}, u32[]{:S(2)}) collective-permute-start(bf16[1,2,2,48,128]{4,3,2,1,0:T(8,128)(2,1)S(1)} %bitcast.17), channel_id=1, source_target_pairs={{8,0},{16,8},{24,16},{0,24},{9,1},{17,9},{25,17},{1,25},{10,2},{18... | collective-permute-start | bytes 147464 | tf_op jit(solution)/shard_map/ppermute | solution.py:32
  7.0 2.1 %collective-permute-done = bf16[1,2,2,48,128]{4,3,2,1,0:T(8,128)(2,1)S(1)} collective-permute-done((bf16[1,2,2,48,128]{4,3,2,1,0:T(8,128)(2,1)S(1)}, bf16[1,2,2,48,128]{4,3,2,1,0:T(8,128)(2,1)S(1)}, u32[]{:S(2)}, u32[]{:S(2)}) %collective-permute-start) | collective-permute-done | bytes 49184 | tf_op jit(solution)/shard_map/ppermute | solution.py:31
  9.1 0.4 collective-permute-done.1
  9.5 1.5 %collective-permute-start.2 = (bf16[4,1,2,48,128]{4,3,2,1,0:T(8,128)(2,1)S(1)}, bf16[4,1,2,48,128]{4,3,2,1,0:T(8,128)(2,1)S(1)}, u32[]{:S(2)}, u32[]{:S(2)}) collective-permute-start(bf16[4,1,2,48,128]{4,3,2,1,0:T(8,128)(2,1)S(1)} %get-tuple-element.38), channel_id=1, source_target_pairs={{0,2},{2,4},{4,6},{6,0},{1,3},{3,5},{5,7},{7,1},{8,10},{10,12},{12... | collective-permute-start | bytes 294920 | tf_op jit(solution)/shard_map/ppermute | solution.py:31
  11.1 1.4 %collective-permute-start.3 = (bf16[4,1,2,48,128]{4,3,2,1,0:T(8,128)(2,1)S(1)}, bf16[4,1,2,48,128]{4,3,2,1,0:T(8,128)(2,1)S(1)}, u32[]{:S(2)}, u32[]{:S(2)}) collective-permute-start(bf16[4,1,2,48,128]{4,3,2,1,0:T(8,128)(2,1)S(1)} %get-tuple-element.39), channel_id=1, source_target_pairs={{2,0},{4,2},{6,4},{0,6},{3,1},{5,3},{7,5},{1,7},{10,8},{12,10},{14... | collective-permute-start | bytes 294920 | tf_op jit(solution)/shard_map/ppermute | solution.py:32
  12.5 2.6 %collective-permute-done.2 = bf16[4,1,2,48,128]{4,3,2,1,0:T(8,128)(2,1)S(1)} collective-permute-done((bf16[4,1,2,48,128]{4,3,2,1,0:T(8,128)(2,1)S(1)}, bf16[4,1,2,48,128]{4,3,2,1,0:T(8,128)(2,1)S(1)}, u32[]{:S(2)}, u32[]{:S(2)}) %collective-permute-start.2) | collective-permute-done | bytes 98336 | tf_op jit(solution)/shard_map/ppermute | solution.py:31
  15.1 1.1 %collective-permute-done.3 = bf16[4,1,2,48,128]{4,3,2,1,0:T(8,128)(2,1)S(1)} collective-permute-done((bf16[4,1,2,48,128]{4,3,2,1,0:T(8,128)(2,1)S(1)}, bf16[4,1,2,48,128]{4,3,2,1,0:T(8,128)(2,1)S(1)}, u32[]{:S(2)}, u32[]{:S(2)}) %collective-permute-start.3) | collective-permute-done | bytes 98336 | tf_op jit(solution)/shard_map/ppermute | solution.py:32
  16.2 0.1 pad_maximum_fusion
  16.3 0.1 collective-permute-start.4
  16.3 8.1 %all_to_all.15.atoms_ref = f32[8,7,256]{2,1,0:T(8,128)S(1)} all-to-all(f32[8,7,256]{2,1,0:T(8,128)S(1)} %get-tuple-element.21), channel_id=1, replica_groups=mesh['dx'=4,'dy'=4,'dz'=2] {'dy','dz'}, dimensions={0} | all-to-all | bytes 114688 | tf_op jit(solution)/shard_map/all_to_all | solution.py:727
  24.4 1.9 %shard_map.105 = f32[4,40,256]{2,1,0:T(8,128)} custom-call(f32[8,7,256]{2,1,0:T(8,128)S(1)} %all_to_all.15.atoms_ref), custom_call_target="tpu_custom_call" | custom-call | tf_op jit(solution)/shard_map/pallas_call | solution.py:728
  26.3 0.0 copy-start
  26.3 4.9 %all-to-all-start.1 = ((f32[4,40,256]{2,1,0:T(8,128)}), f32[4,40,256]{2,1,0:T(8,128)S(1)}, u32[]{:S(2)}, u32[]{:S(2)}) async-start(f32[4,40,256]{2,1,0:T(8,128)} %shard_map.105), calls=%async_computation.1 | async-start | bytes 327680 | tf_op jit(solution)/shard_map/all_to_all | solution.py:733
  31.2 0.3 shard_map.108
  31.5 0.0 copy-done
  31.5 0.9 %shard_map.106 = (f32[8,7,32,128]{3,2,1,0:T(8,128)S(1)}, f32[256,128]{1,0:T(8,128)S(1)}) custom-call(s32[256,128]{1,0:T(8,128)S(1)} %bitcast.15, f32[256,8]{1,0:T(8,128)S(1)} %get-tuple-element.22.own_ref), custom_call_target="tpu_custom_call" | custom-call | flops 1000000000 | bytes 700000 | tf_op jit(solution)/shard_map/pallas_call | solution.py:388
  32.4 2.7 %shard_map.107 = (f32[8,7,32,128]{3,2,1,0:T(8,128)S(1)}, f32[256,128]{1,0:T(8,128)S(1)}) custom-call(s32[256,128]{1,0:T(8,128)S(1)} %bitcast.16, f32[256,8]{1,0:T(8,128)S(1)} %get-tuple-element.22.own_ref, f32[8,7,32,128]{3,2,1,0:T(8,128)S(1)} %get-tuple-element.23.refs_0_, ...), custom_call_target="tpu_custom_call", output_to_operand_aliasing={{0}: (2, {}), {1}: (3, {})} | custom-call | flops 1000000000 | bytes 700000 | tf_op jit(solution)/shard_map/pallas_call | solution.py:388
  35.1 2.5 %all-to-all-done.1 = f32[4,40,256]{2,1,0:T(8,128)S(1)} async-done(((f32[4,40,256]{2,1,0:T(8,128)}), f32[4,40,256]{2,1,0:T(8,128)S(1)}, u32[]{:S(2)}, u32[]{:S(2)}) %all-to-all-start.1) | async-done | bytes 163872 | tf_op jit(solution)/shard_map/all_to_all | solution.py:733
  37.6 2.6 %shard_map.110 = f32[8,3,256]{2,1,0:T(4,128)S(1)} custom-call(f32[8,7,256]{2,1,0:T(8,128)S(1)} %all_to_all.15.atoms_ref, f32[160,256]{1,0:T(8,128)S(1)} %bitcast.11, f32[256,160]{1,0:T(8,128)S(1)} %get-tuple-element.35.forward_ref, f32[80,128]{1,0:T(8,128)S(1)} %get-tuple-element.36.lines_ref, f32[128,128]{1,0:T(8,128)S(1)} %get-tuple-element.37.green_ref), custom_call_target="tpu_custom_call" | custom-call | tf_op jit(solution)/shard_map/pallas_call | solution.py:745
  40.3 0.0 copy-start.1
  40.3 7.3 %all_to_all.16 = f32[8,3,256]{2,1,0:T(4,128)S(1)} all-to-all(f32[8,3,256]{2,1,0:T(4,128)S(1)} %shard_map.110), channel_id=1, replica_groups=mesh['dx'=4,'dy'=4,'dz'=2] {'dy','dz'}, dimensions={0} | all-to-all | bytes 49152 | tf_op jit(solution)/shard_map/all_to_all | solution.py:750
  47.6 0.0 collective-permute-done.4
  47.6 0.0 copy-done.1
  47.7 16.6 %shard_map.109 = (bf16[256,128]{1,0:T(8,128)(2,1)}, f32[3,256]{1,0:T(4,128)S(1)}) custom-call(bf16[16,2,48,128]{3,2,1,0:T(8,128)(2,1)S(1)} %bitcast.12, bf16[16,2,48,128]{3,2,1,0:T(8,128)(2,1)S(1)} %bitcast.13, bf16[16,2,48,128]{3,2,1,0:T(8,128)(2,1)S(1)} %bitcast.14, f32[8,7,32,128]{3,2,1,0:T(8,128)S(1)} %get-tuple-element.29.count_ref, ...), custom_call_target="tpu_custom_call" | custom-call | flops 8000000000 | bytes 2000000 | tf_op jit(solution)/shard_map/pallas_call | solution.py:421
  64.2 0.7 %reshape.35 = f32[3,2,2,2,32]{4,3,2,1,0:T(2,128)} reshape(f32[3,256]{1,0:T(4,128)S(1)} %add.3) | data formatting | bytes 6144 | tf_op jit(solution)/shard_map/reshape | solution.py:777
  (5 shorter events, 0.1 us)
Async XLA Ops:
  1.8 7.3 %collective-permute-start = (bf16[1,2,2,48,128]{4,3,2,1,0:T(8,128)(2,1)S(1)}, bf16[1,2,2,48,128]{4,3,2,1,0:T(8,128)(2,1)S(1)}, u32[]{:S(2)}, u32[]{:S(2)}) collective-permute-start(bf16[1,2,2,48,128]{4,3,2,1,0:T(8,128)(2,1)S(1)} %bitcast.18), channel_id=1, source_target_pairs={{0,8},{8,16},{16,24},{24,0},{1,9},{9,17},{17,25},{25,1},{2,10},{10... | collective-permute-start | bytes 147464 | tf_op jit(solution)/shard_map/ppermute | solution.py:31
  4.9 4.6 %collective-permute-start.1 = (bf16[1,2,2,48,128]{4,3,2,1,0:T(8,128)(2,1)S(1)}, bf16[1,2,2,48,128]{4,3,2,1,0:T(8,128)(2,1)S(1)}, u32[]{:S(2)}, u32[]{:S(2)}) collective-permute-start(bf16[1,2,2,48,128]{4,3,2,1,0:T(8,128)(2,1)S(1)} %bitcast.17), channel_id=1, source_target_pairs={{8,0},{16,8},{24,16},{0,24},{9,1},{17,9},{25,17},{1,25},{10,2},{18... | collective-permute-start | bytes 147464 | tf_op jit(solution)/shard_map/ppermute | solution.py:32
  9.5 5.6 %collective-permute-start.2 = (bf16[4,1,2,48,128]{4,3,2,1,0:T(8,128)(2,1)S(1)}, bf16[4,1,2,48,128]{4,3,2,1,0:T(8,128)(2,1)S(1)}, u32[]{:S(2)}, u32[]{:S(2)}) collective-permute-start(bf16[4,1,2,48,128]{4,3,2,1,0:T(8,128)(2,1)S(1)} %get-tuple-element.38), channel_id=1, source_target_pairs={{0,2},{2,4},{4,6},{6,0},{1,3},{3,5},{5,7},{7,1},{8,10},{10,12},{12... | collective-permute-start | bytes 294920 | tf_op jit(solution)/shard_map/ppermute | solution.py:31
  11.1 5.1 %collective-permute-start.3 = (bf16[4,1,2,48,128]{4,3,2,1,0:T(8,128)(2,1)S(1)}, bf16[4,1,2,48,128]{4,3,2,1,0:T(8,128)(2,1)S(1)}, u32[]{:S(2)}, u32[]{:S(2)}) collective-permute-start(bf16[4,1,2,48,128]{4,3,2,1,0:T(8,128)(2,1)S(1)} %get-tuple-element.39), channel_id=1, source_target_pairs={{2,0},{4,2},{6,4},{0,6},{3,1},{5,3},{7,5},{1,7},{10,8},{12,10},{14... | collective-permute-start | bytes 294920 | tf_op jit(solution)/shard_map/ppermute | solution.py:32
  16.3 31.4 %collective-permute-start.4 = (bf16[4,4,2,48,128]{4,3,2,1,0:T(8,128)(2,1)S(1)}, bf16[4,4,2,48,128]{4,3,2,1,0:T(8,128)(2,1)S(1)}, u32[]{:S(2)}, u32[]{:S(2)}) collective-permute-start(bf16[4,4,2,48,128]{4,3,2,1,0:T(8,128)(2,1)S(1)} %pad_maximum_fusion), channel_id=1, source_target_pairs={{0,1},{1,0},{2,3},{3,2},{4,5},{5,4},{6,7},{7,6},{8,9},{9,8},{10,11... | collective-permute-start | bytes 1179656 | tf_op jit(solution)/shard_map/ppermute | solution.py:27
  26.3 5.2 %copy-start = (s32[2,2,2,32,128]{4,3,2,1,0:T(8,128)S(1)}, s32[2,2,2,32,128]{4,3,2,1,0:T(8,128)}, u32[]{:S(2)}) copy-start(s32[2,2,2,32,128]{4,3,2,1,0:T(8,128)} %param.13) | copy-start | bytes 393220
  26.3 11.3 %all-to-all-start.1 = ((f32[4,40,256]{2,1,0:T(8,128)}), f32[4,40,256]{2,1,0:T(8,128)S(1)}, u32[]{:S(2)}, u32[]{:S(2)}) async-start(f32[4,40,256]{2,1,0:T(8,128)} %shard_map.105), calls=%async_computation.1 | async-start | bytes 327680 | tf_op jit(solution)/shard_map/all_to_all | solution.py:733
  40.3 7.4 %copy-start.1 = (bf16[3,128,128]{2,1,0:T(8,128)(2,1)S(1)}, bf16[3,128,128]{2,1,0:T(8,128)(2,1)}, u32[]{:S(2)}) copy-start(bf16[3,128,128]{2,1,0:T(8,128)(2,1)} %mix_ref.1) | copy-start | bytes 294916
